TPU v7x, 32 devices: a whole 2x2x4 slice. The times are simulated.
32 devices in a mesh: groups: 2 (over x), tok: 8 (over z, y), dom: 2 (over core).
Axes of the slice: x: 2, y: 2, z: 4, core: 2. Of those that a mesh axis runs over, the one named last changes fastest.
Arguments:
- states: bfloat16 [32, 128, 768], P(('groups', 'dom'), 'tok'), parts along dimension 0, may hold values from -12 to 12
- ancestors: int32 [32], P(('groups', 'dom')), parts along dimension 0, may hold values from 0 to 15, as said below
- noise: bfloat16 [32, 128, 768], P(('groups', 'dom'), 'tok'), parts along dimension 0, may hold values from -6 to 6
- pair: bfloat16 [256, 128, 128], P(('groups', 'tok')), parts along dimension 0, may hold values from -200 to 200
- token_mask: int32 [256], P('groups'), parts along dimension 0, may hold values 0 or 1
- w_qkv: bfloat16 [2, 768, 2304], replicated, may hold values from -0.21875 to 0.21875
- w_out: bfloat16 [2, 768, 768], replicated, may hold values from -0.21875 to 0.21875
- w_pair: bfloat16 [2, 128, 16], replicated, may hold values from -1.5 to 1.5
Outputs:
- new_states: bfloat16 [32, 128, 768], P(('groups', 'dom'), 'tok'), parts along dimension 0
There are 2 independent parts, one for each index of `groups`. A program takes and returns all parts, laid end to end along the dimension named above; an argument that names none is the same for every part. Nothing has to cross between parts.
Inputs may be any that keep to these rules, and one draw needn't show every extreme that they name: `ancestors`: nondecreasing over particles; the first entry is 0 and the last is 15.
All inputs are finite; a program needn't handle non-finite values.
Results may differ from a plain program's by a relative error of at most 0.015.
Values may be sent and summed in bfloat16 or wider, within the bound.
No kernel may reach another device: no remote copies, remote signals or barrier semaphores. Data moves between devices by JAX's collectives and lax.ppermute only.
A program may use at most 128 MiB of HBM per device.

v0:
```python
import jax
import jax.numpy as jnp
from jax import lax
from jax.sharding import PartitionSpec as P


def layer_norm(stream):
    values = stream.astype(jnp.float32)
    average = jnp.mean(values, axis=-1, keepdims=True)
    centred = values - average
    spread = jnp.mean(centred * centred, axis=-1, keepdims=True)
    return centred * lax.rsqrt(spread + 1e-05)


def body(states, ancestors, noise, pair, token_mask, w_qkv, w_out, w_pair):
    part_count = states.shape[0]
    tok_rows = states.shape[1]
    model_width = states.shape[2]
    head_count = w_pair.shape[2]
    head_width = model_width // head_count
    layer_count = w_qkv.shape[0]
    total_keys = pair.shape[1]
    everyone = lax.all_gather(states, "dom", axis=0, tiled=True)
    chosen = jnp.take(everyone, ancestors, axis=0)
    stream = (chosen.astype(jnp.float32) + 0.5 * noise.astype(jnp.float32)).astype(jnp.bfloat16)
    penalty = jnp.where(token_mask > 0, 0.0, -1000000000.0).astype(jnp.float32)
    pair_terms = jnp.einsum("ijc,lch->lhij", pair, w_pair, preferred_element_type=jnp.float32)
    full_bias = pair_terms + penalty[None, None, None, :]
    query_scale = head_width ** (-0.5)
    for layer_index in range(layer_count):
        normed = layer_norm(stream).astype(jnp.bfloat16)
        projected = jnp.dot(
            normed.reshape(part_count * tok_rows, model_width),
            w_qkv[layer_index],
            preferred_element_type=jnp.float32,
        )
        projected = projected.reshape(part_count, tok_rows, 3 * model_width)
        query = (projected[..., :model_width] * query_scale).astype(jnp.bfloat16)
        key_tiles = projected[..., model_width : 2 * model_width].astype(jnp.bfloat16)
        value_tiles = projected[..., 2 * model_width :].astype(jnp.bfloat16)
        layer_bias = full_bias[layer_index]
        query_heads = query.reshape(part_count, tok_rows, head_count, head_width)
        all_keys, all_values = (
            lax.all_gather(key_tiles, "tok", axis=1, tiled=True),
            lax.all_gather(value_tiles, "tok", axis=1, tiled=True),
        )
        key_heads = all_keys.reshape(part_count, total_keys, head_count, head_width)
        scores = (
            jnp.einsum(
                "pihe,pjhe->phij", query_heads, key_heads, preferred_element_type=jnp.float32
            )
            + layer_bias[None]
        )
        weights = jax.nn.softmax(scores, axis=-1).astype(jnp.bfloat16)
        value_heads = all_values.reshape(part_count, total_keys, head_count, head_width)
        attended = jnp.einsum(
            "phij,pjhe->pihe", weights, value_heads, preferred_element_type=jnp.float32
        ).astype(jnp.bfloat16)
        attended = attended.reshape(part_count * tok_rows, model_width)
        update = jnp.dot(attended, w_out[layer_index], preferred_element_type=jnp.float32)
        update = update.reshape(part_count, tok_rows, model_width)
        stream = (stream.astype(jnp.float32) + update).astype(jnp.bfloat16)
    return stream


def solution(mesh):
    placed = (
        P(("groups", "dom"), "tok", None),
        P(("groups", "dom")),
        P(("groups", "dom"), "tok", None),
        P(("groups", "tok"), None, None),
        P("groups"),
        P(),
        P(),
        P(),
    )
    return jax.shard_map(
        body,
        mesh=mesh,
        in_specs=placed,
        out_specs=P(("groups", "dom"), "tok", None),
        check_vma=False,
    )
```

profile of v0, /device:TPU:0, one launch (start us, length us, event | category | flops | bytes accessed | tf_op | source)
XLA Modules:
  0.0 227.2 jit_solution(12180136776357450781)
XLA Ops:
  6.5 0.0 copy-start
  6.5 0.7 compare_select_fusion
  7.3 0.7 compare_and_fusion
  7.9 2.4 %all_gather.15 = bf16[16,16,768]{2,1,0:T(8,128)(2,1)S(1)} all-gather(bf16[8,16,768]{2,1,0:T(8,128)(2,1)} %param.8), channel_id=1, replica_groups=mesh['groups'=2,'tok'=8,'dom'=2] {'dom'}, dimensions={0}, use_global_device_ids=true | all-gather | bytes 589824 | tf_op jit(solution)/shard_map/all_gather | solution.py:23
  10.3 0.6 gather_fusion
  10.9 1.1 convert_reduce_fusion
  12.0 0.2 fusion.34
  12.2 2.7 %fusion.48 = (bf16[8,16,2304]{2,1,0:T(8,128)(2,1)S(1)}, f32[8,16,2304]{2,1,0:T(8,128)S(1)}) fusion(bf16[2,768,2304]{2,1,0:T(8,128)(2,1)} %param.13, bf16[8,16,768]{2,1,0:T(8,128)(2,1)S(1)} %get-tuple-element.6, f32[8,16]{1,0:T(8,128)S(1)} %add_rsqrt_fusion.1, f32[8,16]{1,0:T(8,128)S(1)} %broadcast_multiply_fusion.1), kind=kOutput, calls=%fused_computation.68 | convolution fusion | flops 453672960 | bytes 5506048 | tf_op jit(solution)/shard_map/dot_general | solution.py:32
  14.9 0.0 copy-start.3
  14.9 0.0 copy-start.2
  14.9 0.8 fusion.47
  15.7 0.0 all-gather.7.cloned.1.call-update
  15.7 0.0 all-gather.5.cloned.1.call-start
  15.8 0.7 all-gather.5.cloned.1.call-update
  16.5 0.0 all-gather.11.cloned.1.call-start
  16.6 1.4 reshape.69
  18.0 0.0 copy-done.3
  18.0 0.0 copy-done.2
  18.0 0.3 convolution_add_fusion.4
  18.3 0.7 slice_bitcast_fusion
  19.0 43.7 %all-gather.7.cloned.1.call-done = bf16[8,128,768]{2,1,0:T(8,128)(2,1)} async-done(((bf16[8,16,768]{2,1,0:T(8,128)(2,1)}), bf16[8,128,768]{2,1,0:T(8,128)(2,1)}) %all-gather.7.cloned.1.call-update) | async-done | bytes 1572880 | tf_op jit(solution)/shard_map/all_gather | solution.py:44
  62.7 1.9 copy.28
  64.6 1.7 convolution_add_fusion.1
  66.3 0.6 fusion.49
  66.9 41.0 %all-gather.5.cloned.1.call-done = bf16[8,128,768]{2,1,0:T(8,128)(2,1)} async-done(((bf16[8,16,768]{2,1,0:T(8,128)(2,1)}), bf16[8,128,768]{2,1,0:T(8,128)(2,1)}) %all-gather.5.cloned.1.call-update) | async-done | bytes 1572880 | tf_op jit(solution)/shard_map/all_gather | solution.py:45
  107.9 1.9 copy.27
  109.8 4.4 %fusion.12 = bf16[8,16,16,48]{3,1,2,0:T(8,128)(2,1)} fusion(bf16[8,128,16,48]{1,3,2,0:T(8,128)(2,1)S(1)} %bitcast.64, f32[8,16,16]{2,1,0:T(8,128)S(1)} %fusion.49, f32[8,16,16,128]{3,2,1,0:T(8,128)S(1)} %convolution_add_fusion.1), kind=kOutput, calls=%fused_computation.17 | convolution fusion | flops 26052736 | bytes 2826240 | tf_op jit(solution)/shard_map/phij,pjhe->pihe/dot_general | solution.py:56
  114.3 1.2 copy.31
  115.5 0.5 dot_general.35
  115.9 1.7 fusion.50
  117.6 0.2 multiply_reduce_fusion
  117.8 2.7 %fusion.51 = (bf16[8,16,2304]{2,1,0:T(8,128)(2,1)S(1)}, f32[8,16,2304]{2,1,0:T(8,128)S(1)}) fusion(bf16[2,768,2304]{2,1,0:T(8,128)(2,1)} %param.13, f32[8,16,768]{2,1,0:T(8,128)S(1)} %get-tuple-element.16, f32[8,16]{1,0:T(8,128)S(1)} %add_rsqrt_fusion, f32[8,16]{1,0:T(8,128)S(1)} %broadcast_multiply_fusion), kind=kOutput, calls=%fused_computation.71 | convolution fusion | flops 453574656 | bytes 5702656 | tf_op jit(solution)/shard_map/dot_general | solution.py:32
  120.5 0.8 fusion.46
  121.3 0.0 all-gather.11.cloned.1.call-update
  121.3 0.2 all-gather.9.cloned.1.call-start
  121.6 0.3 all-gather.9.cloned.1.call-update
  121.9 0.7 copy.35
  122.7 1.4 reshape.72
  124.1 40.4 %all-gather.11.cloned.1.call-done = bf16[8,128,768]{2,1,0:T(8,128)(2,1)} async-done(((bf16[8,16,768]{2,1,0:T(8,128)(2,1)}), bf16[8,128,768]{2,1,0:T(8,128)(2,1)}) %all-gather.11.cloned.1.call-update) | async-done | bytes 1572880 | tf_op jit(solution)/shard_map/all_gather | solution.py:44
  164.5 1.9 copy.33
  166.4 1.6 convolution_add_fusion
  168.0 1.3 fusion.52
  169.3 40.3 %all-gather.9.cloned.1.call-done = bf16[8,128,768]{2,1,0:T(8,128)(2,1)} async-done(((bf16[8,16,768]{2,1,0:T(8,128)(2,1)}), bf16[8,128,768]{2,1,0:T(8,128)(2,1)}) %all-gather.9.cloned.1.call-update) | async-done | bytes 1572880 | tf_op jit(solution)/shard_map/all_gather | solution.py:45
  209.6 1.9 copy.32
  211.5 5.3 %fusion.13 = bf16[8,16,16,48]{3,1,2,0:T(8,128)(2,1)} fusion(bf16[8,128,16,48]{1,3,2,0:T(8,128)(2,1)S(1)} %bitcast.65, f32[8,16,16]{2,1,0:T(8,128)} %fusion.52, f32[8,16,16,128]{3,2,1,0:T(8,128)S(1)} %convolution_add_fusion), kind=kOutput, calls=%fused_computation.18 | convolution fusion | flops 26052736 | bytes 2826240 | tf_op jit(solution)/shard_map/phij,pjhe->pihe/dot_general | solution.py:56
  216.8 1.2 copy.36
  217.9 0.5 dot_general.40
  218.4 2.3 %fusion.24 = bf16[8,16,768]{2,1,0:T(8,128)(2,1)} fusion(f32[8,16,768]{2,1,0:T(8,128)S(1)} %get-tuple-element.16, bf16[8,16,768]{2,1,0:T(8,128)(2,1)S(1)} %dot_general.40, bf16[2,768,768]{2,1,0:T(8,128)(2,1)} %param.14), kind=kOutput, calls=%fused_computation.27 | convolution fusion | flops 151191552 | bytes 1966080 | tf_op jit(solution)/shard_map/dot_general | solution.py:60
  (13 shorter events, 0.1 us)
Async XLA Ops:
  6.5 11.5 %copy-start = (bf16[16,128,128]{2,1,0:T(8,128)(2,1)S(1)}, bf16[16,128,128]{2,1,0:T(8,128)(2,1)}, u32[]{:S(2)}) copy-start(bf16[16,128,128]{2,1,0:T(8,128)(2,1)} %param.11) | copy-start | bytes 1572868
  6.5 56.2 %all-gather.7.cloned.1.call-start = ((), (), s32[]{:S(2)}) async-start(), calls=%async_computation.1 | async-start | bytes 1769472 | tf_op jit(solution)/shard_map/all_gather | solution.py:44
  14.9 3.1 %copy-start.3 = (s32[128]{0:T(128)S(1)}, s32[128]{0:T(128)}, u32[]{:S(2)}) copy-start(s32[128]{0:T(128)} %param.12) | copy-start | bytes 1540
  14.9 3.1 %copy-start.2 = (bf16[2,128,16]{1,2,0:T(8,128)(2,1)S(1)}, bf16[2,128,16]{1,2,0:T(8,128)(2,1)}, u32[]{:S(2)}) copy-start(bf16[2,128,16]{1,2,0:T(8,128)(2,1)} %param.15) | copy-start | bytes 24580
  15.7 92.2 %all-gather.5.cloned.1.call-start = ((), (), s32[]{:S(2)}) async-start(), calls=%async_computation | async-start | bytes 1769472 | tf_op jit(solution)/shard_map/all_gather | solution.py:45
  16.5 148.0 %all-gather.11.cloned.1.call-start = ((), (), s32[]{:S(2)}) async-start(), calls=%async_computation.3 | async-start | bytes 1769472 | tf_op jit(solution)/shard_map/all_gather | solution.py:44
  117.8 4.1 %copy-start.1 = (f32[16,16,128]{2,0,1:T(8,128)S(1)}, f32[16,16,128]{2,0,1:T(8,128)}, u32[]{:S(2)}) copy-start(f32[16,16,128]{2,0,1:T(8,128)} %get-tuple-element.11) | copy-start | bytes 393220
  121.3 88.2 %all-gather.9.cloned.1.call-start = ((), (), s32[]{:S(2)}) async-start(), calls=%async_computation.2 | async-start | bytes 1769472 | tf_op jit(solution)/shard_map/all_gather | solution.py:45
Sparse Core Ops, SparseCore 0:
  15.9 46.7 all-gather.6
  64.9 42.9 all-gather.4
  121.5 42.9 all-gather.10
  166.5 42.9 all-gather.8
where the time goes:
time: 228 us; the launch traced here: 227 us
  waiting for transfers between devices  166 us (73%)
  matrix products  22.6 us (10%)
  local copies, waits for them, and re-layouts  17.3 us (8%)
  between operations  13.3 us (6%)
  other arithmetic  4.84 us (2%)
  blocking collectives  2.37 us (1%)
    all_gather x2, waiting for transfers between devices, body(): lax.all_gather(key_tiles, 'tok', axis=1, tiled=True)  84.1 us
    all_gather x2, waiting for transfers between devices, body(): lax.all_gather(value_tiles, 'tok', axis=1, tiled=True)  81.3 us
    dot_general x2, matrix products, body(): jnp.einsum('phij,pjhe->pihe', weights, value_heads, preferred_element_typ...  9.73 us
    dot_general x2, matrix products, body(): jnp.dot(normed.reshape(part_count * tok_rows, model_width), w_qkv[layer_i...  5.4 us
  transfers between devices with their start and end apart: 4, of which 4 were waited for; matrix products, arithmetic and copies ran while one was open for 6% of the time, Pallas kernels for 0%

commit v1 on v0

--- a/solution.py
+++ b/solution.py
@@ -1,7 +1,12 @@
 import jax
 import jax.numpy as jnp
 from jax import lax
+from jax.experimental import pallas as pl
+from jax.experimental.pallas import tpu as pltpu
 from jax.sharding import PartitionSpec as P
+
+MASKED = -1000000000.0
+LANES = 128
 
 
 def layer_norm(stream):
@@ -12,7 +17,7 @@
     return centred * lax.rsqrt(spread + 1e-05)
 
 
-def body(states, ancestors, noise, pair, token_mask, w_qkv, w_out, w_pair):
+def gathered_body(states, ancestors, noise, pair, token_mask, w_qkv, w_out, w_pair):
     part_count = states.shape[0]
     tok_rows = states.shape[1]
     model_width = states.shape[2]
@@ -23,7 +28,7 @@
     everyone = lax.all_gather(states, "dom", axis=0, tiled=True)
     chosen = jnp.take(everyone, ancestors, axis=0)
     stream = (chosen.astype(jnp.float32) + 0.5 * noise.astype(jnp.float32)).astype(jnp.bfloat16)
-    penalty = jnp.where(token_mask > 0, 0.0, -1000000000.0).astype(jnp.float32)
+    penalty = jnp.where(token_mask > 0, 0.0, MASKED).astype(jnp.float32)
     pair_terms = jnp.einsum("ijc,lch->lhij", pair, w_pair, preferred_element_type=jnp.float32)
     full_bias = pair_terms + penalty[None, None, None, :]
     query_scale = head_width ** (-0.5)
@@ -36,20 +41,16 @@
         )
         projected = projected.reshape(part_count, tok_rows, 3 * model_width)
         query = (projected[..., :model_width] * query_scale).astype(jnp.bfloat16)
-        key_tiles = projected[..., model_width : 2 * model_width].astype(jnp.bfloat16)
-        value_tiles = projected[..., 2 * model_width :].astype(jnp.bfloat16)
-        layer_bias = full_bias[layer_index]
+        both = projected[..., model_width:].astype(jnp.bfloat16)
         query_heads = query.reshape(part_count, tok_rows, head_count, head_width)
-        all_keys, all_values = (
-            lax.all_gather(key_tiles, "tok", axis=1, tiled=True),
-            lax.all_gather(value_tiles, "tok", axis=1, tiled=True),
-        )
+        gathered = lax.all_gather(both, "tok", axis=1, tiled=True)
+        all_keys, all_values = gathered[..., :model_width], gathered[..., model_width:]
         key_heads = all_keys.reshape(part_count, total_keys, head_count, head_width)
         scores = (
             jnp.einsum(
                 "pihe,pjhe->phij", query_heads, key_heads, preferred_element_type=jnp.float32
             )
-            + layer_bias[None]
+            + full_bias[layer_index][None]
         )
         weights = jax.nn.softmax(scores, axis=-1).astype(jnp.bfloat16)
         value_heads = all_values.reshape(part_count, total_keys, head_count, head_width)
@@ -63,6 +64,259 @@
     return stream
 
 
+def whole_vmem():
+    return pl.BlockSpec(memory_space=pltpu.VMEM)
+
+
+def in_hbm():
+    return pl.BlockSpec(memory_space=pl.ANY)
+
+
+def in_smem():
+    return pl.BlockSpec(memory_space=pltpu.SMEM)
+
+
+def make_bias(pair, mask_row, w_rows, particles, stream_rows):
+    rows, keys, _ = pair.shape
+    heads = w_rows.shape[0]
+
+    def kernel(pair_ref, mask_ref, w_ref, out_ref, rows_ref):
+        penalty = jnp.where(mask_ref[...] > 0, 0.0, MASKED).astype(jnp.float32)
+        for i in range(rows):
+            piece = lax.dot_general(
+                w_ref[...], pair_ref[i], (((1,), (1,)), ((), ())),
+                preferred_element_type=jnp.float32,
+            ) + penalty
+            rows_ref[:, i, :] = piece - jnp.max(piece, axis=-1, keepdims=True)
+        for h in range(heads):
+            block = rows_ref[h].astype(jnp.bfloat16)
+            for p in range(particles):
+                out_ref[p, stream_rows + h * rows : stream_rows + (h + 1) * rows, :] = block
+
+    return pl.pallas_call(
+        kernel,
+        out_shape=jax.ShapeDtypeStruct((particles, stream_rows + heads * rows, keys), jnp.bfloat16),
+        in_specs=[whole_vmem(), whole_vmem(), whole_vmem()],
+        out_specs=whole_vmem(),
+        scratch_shapes=[pltpu.VMEM((heads, rows, keys), jnp.float32)],
+        cost_estimate=pl.CostEstimate(
+            flops=2 * heads * rows * keys * LANES, transcendentals=0, bytes_accessed=2000000
+        ),
+        name="make_bias",
+    )(pair, mask_row, w_rows)
+
+
+def add_stream(dom, ancestors, own, other, noise, packed):
+    particles, rows, width = own.shape
+
+    def kernel(dom_ref, anc_ref, own_ref, other_ref, noise_ref, packed_ref, out_ref):
+        del packed_ref
+        for p in range(particles):
+            a = anc_ref[p]
+            local = lax.rem(a, particles)
+            mine = lax.div(a, particles) == dom_ref[0]
+            value = jnp.where(mine, own_ref[local], other_ref[local])
+            value = value.astype(jnp.float32) + 0.5 * noise_ref[p].astype(jnp.float32)
+            value = value.astype(jnp.bfloat16)
+            for k in range(width // LANES):
+                out_ref[p, k * rows : (k + 1) * rows, :] = value[:, k * LANES : (k + 1) * LANES]
+
+    used = rows * (width // LANES)
+    free_rows = pl.BlockSpec((particles, used, LANES), lambda i: (0, 0, 0))
+    return pl.pallas_call(
+        kernel,
+        out_shape=jax.ShapeDtypeStruct(packed.shape, packed.dtype),
+        in_specs=[in_smem(), in_smem(), whole_vmem(), whole_vmem(), whole_vmem(), in_hbm()],
+        out_specs=free_rows,
+        grid=(1,),
+        input_output_aliases={5: 0},
+        name="add_stream",
+    )(dom, ancestors, own, other, noise, packed)
+
+
+def project(normed, w_buf, q_ref, k_ref, v_ref, width, scale):
+    q_ref[...] = (
+        jnp.dot(normed, w_buf[:, :width], preferred_element_type=jnp.float32) * scale
+    ).astype(jnp.bfloat16)
+    k_ref[...] = jnp.dot(
+        normed, w_buf[:, width : 2 * width], preferred_element_type=jnp.float32
+    ).astype(jnp.bfloat16)
+    v_ref[...] = jnp.dot(
+        normed, w_buf[:, 2 * width :], preferred_element_type=jnp.float32
+    ).astype(jnp.bfloat16)
+
+
+def first_project(received, w_qkv, rows, width, scale):
+    sources = received.shape[0]
+    tokens = sources * rows
+
+    def kernel(recv_ref, w_hbm, x_ref, q_ref, k_ref, v_ref, w_buf, sem):
+        copies = []
+        for n in range(3):
+            cols = pl.ds(n * width, width)
+            copies.append(
+                pltpu.make_async_copy(w_hbm.at[0, :, cols], w_buf.at[:, cols], sem.at[n])
+            )
+            copies[n].start()
+        for s in range(sources):
+            for k in range(width // LANES):
+                x_ref[s * rows : (s + 1) * rows, k * LANES : (k + 1) * LANES] = recv_ref[
+                    s, k * rows : (k + 1) * rows, :
+                ]
+        normed = layer_norm(x_ref[...]).astype(jnp.bfloat16)
+        for n, ref in enumerate((q_ref, k_ref, v_ref)):
+            copies[n].wait()
+            value = jnp.dot(
+                normed, w_buf[:, n * width : (n + 1) * width], preferred_element_type=jnp.float32
+            )
+            if n == 0:
+                value = value * scale
+            ref[...] = value.astype(jnp.bfloat16)
+
+    shape = jax.ShapeDtypeStruct((tokens, width), jnp.bfloat16)
+    return pl.pallas_call(
+        kernel,
+        out_shape=(shape,) * 4,
+        in_specs=[whole_vmem(), in_hbm()],
+        out_specs=(whole_vmem(),) * 4,
+        scratch_shapes=[
+            pltpu.VMEM((width, 3 * width), jnp.bfloat16),
+            pltpu.SemaphoreType.DMA((3,)),
+        ],
+        compiler_params=pltpu.CompilerParams(vmem_limit_bytes=24 * 2**20),
+        cost_estimate=pl.CostEstimate(
+            flops=6 * tokens * width * width, transcendentals=0, bytes_accessed=8 * width * width
+        ),
+        name="first_project",
+    )(received, w_qkv)
+
+
+def layers(dom, mask, stream, query, keys, values, received, other, w_qkv, w_out, rows, heads, scale):
+    tokens, width = stream.shape
+    layer_count = w_qkv.shape[0]
+    sources = received.shape[0]
+    head_width = width // heads
+    half = heads // 2
+    stream_rows = rows * (width // LANES)
+
+    def kernel(
+        dom_ref, mask_ref, x_ref, q_in, k_in, v_in, recv_ref, other_ref, wq_hbm, wo_hbm,
+        out_ref, x_buf, q_buf, k_buf, v_buf, att_buf, wq_buf, wo_buf, wq_sem, wo_sem,
+    ):
+        wo_copies = [
+            pltpu.make_async_copy(wo_hbm.at[l], wo_buf.at[l], wo_sem.at[l])
+            for l in range(layer_count)
+        ]
+        wq_copies = [
+            pltpu.make_async_copy(wq_hbm.at[l], wq_buf.at[l - 1], wq_sem.at[l - 1])
+            for l in range(1, layer_count)
+        ]
+        wo_copies[0].start()
+        for l in range(1, layer_count):
+            wq_copies[l - 1].start()
+            wo_copies[l].start()
+        is_first = dom_ref[0] == 0
+        anyone = jnp.max(mask_ref[...], axis=-1, keepdims=True)
+        floor = jnp.where(anyone > 0, 0.0, MASKED).astype(jnp.float32)
+
+        for l in range(layer_count):
+            q_ref, k_ref, v_ref = (q_in, k_in, v_in) if l == 0 else (q_buf, k_buf, v_buf)
+            stream_ref = x_ref if l == 0 else x_buf
+            for h in range(heads):
+                low = h * head_width
+                high = low + head_width
+                start = low // LANES * LANES
+                stop = -(-high // LANES) * LANES
+                lane = lax.broadcasted_iota(jnp.int32, (tokens, stop - start), 1) + start
+                inside = (lane >= low) & (lane < high)
+                q_head = jnp.where(inside, q_ref[:, start:stop].astype(jnp.float32), 0.0)
+                scores = lax.dot_general(
+                    q_head.astype(jnp.bfloat16), k_ref[:, start:stop], (((1,), (1,)), ((), ())),
+                    preferred_element_type=jnp.float32,
+                )
+                base = stream_rows + (l * half + h % half) * rows
+                near = recv_ref[:, base : base + rows, :].reshape(tokens, tokens)
+                far = other_ref[:, base : base + rows, :].reshape(tokens, tokens)
+                bias = jnp.where(is_first, near, far) if h < half else jnp.where(is_first, far, near)
+                scores = scores + (bias.astype(jnp.float32) + floor)
+                top = jnp.max(scores, axis=-1, keepdims=True)
+                raised = jnp.exp(scores - top)
+                total = jnp.sum(raised, axis=-1, keepdims=True)
+                weights = (raised / total).astype(jnp.bfloat16)
+                out = jnp.dot(weights, v_ref[:, start:stop], preferred_element_type=jnp.float32)
+                if low == start:
+                    att_buf[:, start:stop] = out
+                else:
+                    for t in range(start, stop, LANES):
+                        piece = out[:, t - start : t - start + LANES]
+                        if t >= low:
+                            att_buf[:, t : t + LANES] = piece
+                        else:
+                            att_buf[:, t : t + LANES] = jnp.where(
+                                inside[:, t - start : t - start + LANES], piece,
+                                att_buf[:, t : t + LANES],
+                            )
+            wo_copies[l].wait()
+            update = jnp.dot(
+                att_buf[...].astype(jnp.bfloat16), wo_buf[l], preferred_element_type=jnp.float32
+            )
+            moved = (stream_ref[...].astype(jnp.float32) + update).astype(jnp.bfloat16)
+            if l + 1 < layer_count:
+                x_buf[...] = moved
+                normed = layer_norm(moved).astype(jnp.bfloat16)
+                wq_copies[l].wait()
+                project(normed, wq_buf.at[l], q_buf, k_buf, v_buf, width, scale)
+            else:
+                for s in range(sources):
+                    out_ref[s] = moved[s * rows : (s + 1) * rows, :]
+
+    wide = pltpu.VMEM((tokens, width), jnp.bfloat16)
+    return pl.pallas_call(
+        kernel,
+        out_shape=jax.ShapeDtypeStruct((sources, rows, width), jnp.bfloat16),
+        in_specs=[in_smem()] + [whole_vmem()] * 7 + [in_hbm()] * 2,
+        out_specs=whole_vmem(),
+        scratch_shapes=[
+            wide, wide, wide, wide, pltpu.VMEM((tokens, width), jnp.float32),
+            pltpu.VMEM((layer_count - 1, width, 3 * width), jnp.bfloat16),
+            pltpu.VMEM((layer_count, width, width), jnp.bfloat16),
+            pltpu.SemaphoreType.DMA((layer_count - 1,)),
+            pltpu.SemaphoreType.DMA((layer_count,)),
+        ],
+        compiler_params=pltpu.CompilerParams(vmem_limit_bytes=32 * 2**20),
+        cost_estimate=pl.CostEstimate(
+            flops=14 * tokens * width * width, transcendentals=2 * heads * tokens * tokens,
+            bytes_accessed=10 * width * width,
+        ),
+        name="layers",
+    )(dom, mask, stream, query, keys, values, received, other, w_qkv, w_out)
+
+
+def spread_body(states, ancestors, noise, pair, token_mask, w_qkv, w_out, w_pair):
+    particles, rows, width = states.shape
+    layer_count, channels, heads = w_pair.shape
+    half = heads // 2
+    scale = (width // heads) ** (-0.5)
+    stream_rows = rows * (width // LANES)
+    swap = [(0, 1), (1, 0)]
+    here = lax.axis_index("dom")
+    dom = here.astype(jnp.int32).reshape(1)
+    mask_row = token_mask.reshape(1, -1)
+    other_states = lax.ppermute(states, "dom", swap)
+    w_rows = lax.dynamic_slice_in_dim(w_pair.transpose(0, 2, 1), here * half, half, axis=1)
+    packed = make_bias(
+        pair, mask_row, w_rows.reshape(layer_count * half, channels), particles, stream_rows
+    )
+    packed = add_stream(dom, ancestors, states, other_states, noise, packed)
+    received = lax.all_to_all(packed, "tok", 0, 0, tiled=True)
+    other = lax.ppermute(received, "dom", swap)
+    stream, query, keys, values = first_project(received, w_qkv, rows, width, scale)
+    result = layers(
+        dom, mask_row, stream, query, keys, values, received, other, w_qkv, w_out, rows, heads, scale
+    )
+    return lax.all_to_all(result, "tok", 0, 0, tiled=True)
+
+
 def solution(mesh):
     placed = (
         P(("groups", "dom"), "tok", None),
@@ -74,6 +328,21 @@
         P(),
         P(),
     )
+
+    def body(states, ancestors, noise, pair, token_mask, w_qkv, w_out, w_pair):
+        particles, rows, width = states.shape
+        fits = (
+            particles == mesh.shape["tok"]
+            and mesh.shape["dom"] == 2
+            and w_pair.shape[2] % 2 == 0
+            and pair.shape[1] == LANES
+            and pair.shape[2] == LANES
+            and width % LANES == 0
+            and rows % 16 == 0
+        )
+        chosen = spread_body if fits else gathered_body
+        return chosen(states, ancestors, noise, pair, token_mask, w_qkv, w_out, w_pair)
+
     return jax.shard_map(
         body,
         mesh=mesh,

time: 228 us -> 61.5 us (0.27)
  waiting for transfers between devices: 166 us -> 0.01 us
  blocking collectives: 2.37 us -> 38.1 us
  matrix products: 22.6 us -> 0 us
  Pallas kernels: 0 us -> 16 us
  between operations: 13.3 us -> 0.05 us
  local copies, waits for them, and re-layouts: 17.3 us -> 6.51 us
  other arithmetic: 4.84 us -> 0 us
    all_gather x4 -> x0, waiting for transfers between devices: 165 us -> none  [the longest x2 84.1 us: body(): lax.all_gather(key_tiles, 'tok', axis=1, tiled=True)]
    all_to_all x0 -> x2, blocking collectives: none -> 38.1 us  [the longest x1 26.1 us: spread_body(): received = lax.all_to_all(packed, 'tok', 0, 0, tiled=True)]
    dot_general x9 -> x0, matrix products: 22.6 us -> none  [the longest x2 9.73 us: body(): jnp.einsum('phij,pjhe->pihe', weights, value_heads, preferred_element_typ...]
    pallas_call x0 -> x4, Pallas kernels: none -> 16 us  [the longest x1 10.1 us: layers(): pl.pallas_call(kernel, out_shape=jax.ShapeDtypeStruct((sources, rows, wid...]
    all_gather x4 -> x0, local copies, waits for them, and re-layouts: 7.62 us -> none  [the longest x2 3.81 us: body(): lax.all_gather(key_tiles, 'tok', axis=1, tiled=True)]
    unnamed x8 -> x13, local copies, waits for them, and re-layouts: 0.02 us -> 5.92 us
    all_gather x1 -> x0, blocking collectives: 2.37 us -> none  [body(): everyone = lax.all_gather(states, 'dom', axis=0, tiled=True)]
    convert_element_type x2 -> x0, local copies, waits for them, and re-layouts: 2.35 us -> none  [body(): attended = jnp.einsum('phij,pjhe->pihe', weights, value_heads, preferred_...]
  transfers between devices with their start and end apart: 4 -> 2, of which waited for: 4 -> 0; matrix products, arithmetic and copies ran while one was open for 6% -> 1% of each run, Pallas kernels for 0% -> 7%
where the time goes in v1:
time: 61.5 us; the launch traced here: 61.2 us
  blocking collectives  38.1 us (62%)
  Pallas kernels  16 us (26%)
  local copies, waits for them, and re-layouts  6.51 us (11%)
    all_to_all x1, blocking collectives, spread_body(): received = lax.all_to_all(packed, 'tok', 0, 0, tiled=True)  26.1 us
    all_to_all x1, blocking collectives, spread_body(): return lax.all_to_all(result, 'tok', 0, 0, tiled=True)  11.9 us
    pallas_call x1, Pallas kernels, layers(): pl.pallas_call(kernel, out_shape=jax.ShapeDtypeStruct((sources, rows, wid...  10.1 us
    unnamed x13, local copies, waits for them, and re-layouts  5.92 us
    pallas_call x1, Pallas kernels, make_bias(): pl.pallas_call(kernel, out_shape=jax.ShapeDtypeStruct((particles, stream_...  2.43 us
    pallas_call x1, Pallas kernels, add_stream(): pl.pallas_call(kernel, out_shape=jax.ShapeDtypeStruct(packed.shape, packe...  1.88 us
    pallas_call x1, Pallas kernels, first_project(): pl.pallas_call(kernel, out_shape=(shape,) * 4, in_specs=[whole_vmem(), in...  1.59 us
  transfers between devices with their start and end apart: 2, of which 0 were waited for; matrix products, arithmetic and copies ran while one was open for 1% of the time, Pallas kernels for 7%

profile of v1, /device:TPU:0, one launch (start us, length us, event | category | flops | bytes accessed | tf_op | source)
XLA Modules:
  0.0 61.2 jit_solution(14478043007551251364)
XLA Ops:
  0.0 0.0 copy-start
  0.0 0.0 copy-start.4
  0.0 0.0 copy-start.3
  0.0 0.5 collective-permute-start
  0.5 0.2 copy-done
  0.7 0.6 dynamic-slice_bitcast_fusion.w_ref
  1.3 2.4 %make_bias.1.packed_ref = bf16[8,352,128]{2,1,0:T(8,128)(2,1)} custom-call(bf16[16,128,128]{2,1,0:T(8,128)(2,1)} %pair_ref.1, s32[1,128]{1,0:T(1,128)} %bitcast.6, bf16[16,128]{1,0:T(8,128)(2,1)} %dynamic-slice_bitcast_fusion.w_ref), custom_call_target="tpu_custom_call" | custom-call | flops 8388608 | bytes 2000000 | tf_op jit(solution)/shard_map/make_bias/pallas_call | solution.py:96
  3.7 0.0 collective-permute-done.other_ref
  3.7 0.0 copy-start.5
  3.7 0.7 %copy-done.5 = bf16[8,16,768]{2,1,0:T(8,128)(2,1)} copy-done((bf16[8,16,768]{2,1,0:T(8,128)(2,1)}, bf16[8,16,768]{2,1,0:T(8,128)(2,1)S(1)}, u32[]{:S(2)}) %copy-start.5) | copy-done | bytes 196632
  4.4 1.9 %add_stream.1 = bf16[8,352,128]{2,1,0:T(8,128)(2,1)} custom-call(s32[1]{0:T(128)} %bitcast.dom_ref, s32[8]{0:T(128)} %anc_ref.1, bf16[8,16,768]{2,1,0:T(8,128)(2,1)} %own_ref.1, bf16[8,16,768]{2,1,0:T(8,128)(2,1)} %copy-done.5, bf16[8,16,768]{2,1,0:T(8,128)(2,1)} %noise_ref.1, bf16[8,352,128]{2,1,0:T(8,128)(2,1)} %make_bias.1.packed_ref), custom_call_target="tpu_custom_call", output_to_operand_aliasing={{}: (5, {})} | custom-call | tf_op jit(solution)/shard_map/add_stream/pallas_call | solution.py:126
  6.3 26.1 %all_to_all.10.recv_ref = bf16[8,352,128]{2,1,0:T(8,128)(2,1)S(1)} all-to-all(bf16[8,352,128]{2,1,0:T(8,128)(2,1)} %add_stream.1), channel_id=1, replica_groups=mesh['groups'=2,'tok'=8,'dom'=2] {'tok'}, dimensions={0} | all-to-all | bytes 1441792 | tf_op jit(solution)/shard_map/all_to_all | solution.py:311
  32.4 0.0 collective-permute-start.1
  32.4 0.0 copy-start.1
  32.4 3.0 %copy-done.1 = bf16[2,768,2304]{2,1,0:T(8,128)(2,1)S(1)} copy-done((bf16[2,768,2304]{2,1,0:T(8,128)(2,1)S(1)}, bf16[2,768,2304]{2,1,0:T(8,128)(2,1)}, u32[]{:S(2)}) %copy-start.1) | copy-done | bytes 7077912
  35.4 0.0 copy-start.2
  35.5 1.6 %first_project.1 = (bf16[128,768]{1,0:T(8,128)(2,1)S(1)}, bf16[128,768]{1,0:T(8,128)(2,1)S(1)}, bf16[128,768]{1,0:T(8,128)(2,1)S(1)}, bf16[128,768]{1,0:T(8,128)(2,1)S(1)}) custom-call(bf16[8,352,128]{2,1,0:T(8,128)(2,1)S(1)} %all_to_all.10.recv_ref, bf16[2,768,2304]{2,1,0:T(8,128)(2,1)S(1)} %copy-done.1), custom_call_target="tpu_custom_call" | custom-call | flops 452984832 | bytes 4718592 | tf_op jit(solution)/shard_map/first_project/pallas_call | solution.py:177
  37.0 0.0 collective-permute-done.1.other_ref
  37.1 0.0 copy-done.4
  37.1 0.0 copy-done.3
  37.1 1.4 %copy-done.2 = bf16[2,768,2304]{2,1,0:T(8,128)(2,1)S(1)} copy-done((bf16[2,768,2304]{2,1,0:T(8,128)(2,1)S(1)}, bf16[2,768,2304]{2,1,0:T(8,128)(2,1)}, u32[]{:S(2)}) %copy-start.2) | copy-done | bytes 7077912
  38.5 10.1 %layers.1 = bf16[8,16,768]{2,1,0:T(8,128)(2,1)S(1)} custom-call(s32[1]{0:T(128)} %bitcast.dom_ref, s32[1,128]{1,0:T(1,128)S(1)} %bitcast.7, bf16[128,768]{1,0:T(8,128)(2,1)S(1)} %get-tuple-element.9.x_ref, bf16[128,768]{1,0:T(8,128)(2,1)S(1)} %get-tuple-element.10.q_in, bf16[128,768]{1,0:T(8,128)(2,1)S(1)} %get-tuple-element.11.k_in, ...), custom_call_target="tpu_custom_call" | custom-call | flops 1056964608 | bytes 5898240 | tf_op jit(solution)/shard_map/layers/pallas_call | solution.py:274
  48.5 11.9 %all_to_all.11 = bf16[8,16,768]{2,1,0:T(8,128)(2,1)S(1)} all-to-all(bf16[8,16,768]{2,1,0:T(8,128)(2,1)S(1)} %layers.1), channel_id=1, replica_groups=mesh['groups'=2,'tok'=8,'dom'=2] {'tok'}, dimensions={0} | all-to-all | bytes 393216 | tf_op jit(solution)/shard_map/all_to_all | solution.py:317
  60.5 0.7 %copy.12 = bf16[8,16,768]{2,1,0:T(8,128)(2,1)} copy(bf16[8,16,768]{2,1,0:T(8,128)(2,1)S(1)} %all_to_all.11) | data formatting | bytes 393216
Async XLA Ops:
  0.0 0.7 %copy-start = (bf16[2,128,16]{1,2,0:T(8,128)(2,1)S(1)}, bf16[2,128,16]{1,2,0:T(8,128)(2,1)}, u32[]{:S(2)}) copy-start(bf16[2,128,16]{1,2,0:T(8,128)(2,1)} %param.15) | copy-start | bytes 24580
  0.0 37.1 %copy-start.4 = (s32[128]{0:T(128)S(1)}, s32[128]{0:T(128)}, u32[]{:S(2)}) copy-start(s32[128]{0:T(128)} %param.12) | copy-start | bytes 1540
  0.0 37.1 %copy-start.3 = (bf16[2,768,768]{2,1,0:T(8,128)(2,1)S(1)}, bf16[2,768,768]{2,1,0:T(8,128)(2,1)}, u32[]{:S(2)}) copy-start(bf16[2,768,768]{2,1,0:T(8,128)(2,1)} %wo_hbm.1) | copy-start | bytes 7077892
  0.0 3.7 %collective-permute-start = (bf16[8,16,768]{2,1,0:T(8,128)(2,1)}, bf16[8,16,768]{2,1,0:T(8,128)(2,1)S(1)}, u32[]{:S(2)}, u32[]{:S(2)}) collective-permute-start(bf16[8,16,768]{2,1,0:T(8,128)(2,1)} %own_ref.1), channel_id=1, source_target_pairs={{0,1},{1,0},{2,3},{3,2},{4,5},{5,4},{6,7},{7,6},{8,9},{9,8},{10,11... | collective-permute-start | bytes 589832 | tf_op jit(solution)/shard_map/ppermute | solution.py:305
  3.7 0.7 %copy-start.5 = (bf16[8,16,768]{2,1,0:T(8,128)(2,1)}, bf16[8,16,768]{2,1,0:T(8,128)(2,1)S(1)}, u32[]{:S(2)}) copy-start(bf16[8,16,768]{2,1,0:T(8,128)(2,1)S(1)} %collective-permute-done.other_ref) | copy-start | bytes 589828
  32.4 4.6 %collective-permute-start.1 = (bf16[8,352,128]{2,1,0:T(8,128)(2,1)S(1)}, bf16[8,352,128]{2,1,0:T(8,128)(2,1)S(1)}, u32[]{:S(2)}, u32[]{:S(2)}) collective-permute-start(bf16[8,352,128]{2,1,0:T(8,128)(2,1)S(1)} %all_to_all.10.recv_ref), channel_id=1, source_target_pairs={{0,1},{1,0},{2,3},{3,2},{4,5},{5,4},{6,7},{7,6},{8,9},{9,8},{10,11... | collective-permute-start | bytes 2162696 | tf_op jit(solution)/shard_map/ppermute | solution.py:312
  32.4 3.0 %copy-start.1 = (bf16[2,768,2304]{2,1,0:T(8,128)(2,1)S(1)}, bf16[2,768,2304]{2,1,0:T(8,128)(2,1)}, u32[]{:S(2)}) copy-start(bf16[2,768,2304]{2,1,0:T(8,128)(2,1)} %wq_hbm.1) | copy-start | bytes 21233668
  35.4 3.0 %copy-start.2 = (bf16[2,768,2304]{2,1,0:T(8,128)(2,1)S(1)}, bf16[2,768,2304]{2,1,0:T(8,128)(2,1)}, u32[]{:S(2)}) copy-start(bf16[2,768,2304]{2,1,0:T(8,128)(2,1)} %wq_hbm.1) | copy-start | bytes 21233668

commit v2 on v1

v2 whole, which is shorter than its diff:
```python
import jax
import jax.numpy as jnp
from jax import lax
from jax.experimental import pallas as pl
from jax.experimental.pallas import tpu as pltpu
from jax.sharding import PartitionSpec as P

MASKED = -1000000000.0
LANES = 128


def layer_norm(stream):
    values = stream.astype(jnp.float32)
    average = jnp.mean(values, axis=-1, keepdims=True)
    centred = values - average
    spread = jnp.mean(centred * centred, axis=-1, keepdims=True)
    return centred * lax.rsqrt(spread + 1e-05)


def gathered_body(states, ancestors, noise, pair, token_mask, w_qkv, w_out, w_pair):
    part_count = states.shape[0]
    tok_rows = states.shape[1]
    model_width = states.shape[2]
    head_count = w_pair.shape[2]
    head_width = model_width // head_count
    layer_count = w_qkv.shape[0]
    total_keys = pair.shape[1]
    everyone = lax.all_gather(states, "dom", axis=0, tiled=True)
    chosen = jnp.take(everyone, ancestors, axis=0)
    stream = (chosen.astype(jnp.float32) + 0.5 * noise.astype(jnp.float32)).astype(jnp.bfloat16)
    penalty = jnp.where(token_mask > 0, 0.0, MASKED).astype(jnp.float32)
    pair_terms = jnp.einsum("ijc,lch->lhij", pair, w_pair, preferred_element_type=jnp.float32)
    full_bias = pair_terms + penalty[None, None, None, :]
    query_scale = head_width ** (-0.5)
    for layer_index in range(layer_count):
        normed = layer_norm(stream).astype(jnp.bfloat16)
        projected = jnp.dot(
            normed.reshape(part_count * tok_rows, model_width),
            w_qkv[layer_index],
            preferred_element_type=jnp.float32,
        )
        projected = projected.reshape(part_count, tok_rows, 3 * model_width)
        query = (projected[..., :model_width] * query_scale).astype(jnp.bfloat16)
        both = projected[..., model_width:].astype(jnp.bfloat16)
        query_heads = query.reshape(part_count, tok_rows, head_count, head_width)
        gathered = lax.all_gather(both, "tok", axis=1, tiled=True)
        all_keys, all_values = gathered[..., :model_width], gathered[..., model_width:]
        key_heads = all_keys.reshape(part_count, total_keys, head_count, head_width)
        scores = (
            jnp.einsum(
                "pihe,pjhe->phij", query_heads, key_heads, preferred_element_type=jnp.float32
            )
            + full_bias[layer_index][None]
        )
        weights = jax.nn.softmax(scores, axis=-1).astype(jnp.bfloat16)
        value_heads = all_values.reshape(part_count, total_keys, head_count, head_width)
        attended = jnp.einsum(
            "phij,pjhe->pihe", weights, value_heads, preferred_element_type=jnp.float32
        ).astype(jnp.bfloat16)
        attended = attended.reshape(part_count * tok_rows, model_width)
        update = jnp.dot(attended, w_out[layer_index], preferred_element_type=jnp.float32)
        update = update.reshape(part_count, tok_rows, model_width)
        stream = (stream.astype(jnp.float32) + update).astype(jnp.bfloat16)
    return stream


def whole_vmem():
    return pl.BlockSpec(memory_space=pltpu.VMEM)


def in_hbm():
    return pl.BlockSpec(memory_space=pltpu.HBM)


def stay(array):
    return pltpu.with_memory_space_constraint(array, pltpu.HBM)


def in_smem():
    return pl.BlockSpec(memory_space=pltpu.SMEM)


def prepare(pair, mask_row, w_rows, own, noise, w_qkv):
    rows, keys, channels = pair.shape
    layer_count, heads, _ = w_rows.shape
    half = heads // 2
    blocks = layer_count * half

    def kernel(
        pair_hbm, mask_hbm, w_hbm, own_hbm, noise_hbm, wq_hbm,
        bias_ref, own_ref, noise_ref, first_ref, pair_ref, mask_ref, w_ref, rows_ref, sem,
    ):
        copies = [
            pltpu.make_async_copy(mask_hbm, mask_ref, sem.at[0]),
            pltpu.make_async_copy(w_hbm, w_ref, sem.at[1]),
            pltpu.make_async_copy(pair_hbm, pair_ref, sem.at[2]),
            pltpu.make_async_copy(own_hbm, own_ref, sem.at[3]),
            pltpu.make_async_copy(noise_hbm, noise_ref, sem.at[4]),
            pltpu.make_async_copy(wq_hbm.at[0], first_ref, sem.at[5]),
        ]
        for copy in copies:
            copy.start()
        copies[0].wait()
        copies[1].wait()
        penalty = jnp.where(mask_ref[...] > 0, 0.0, MASKED).astype(jnp.float32)
        is_first = lax.axis_index("dom") == 0
        sent = jnp.concatenate(
            [
                jnp.where(is_first, w[:half], w[half:])
                for w in (w_ref[l].astype(jnp.float32) for l in range(layer_count))
            ],
            axis=0,
        ).astype(jnp.bfloat16)
        copies[2].wait()
        for i in range(rows):
            piece = across(sent, pair_ref[i]) + penalty
            rows_ref[:, i, :] = piece - jnp.max(piece, axis=-1, keepdims=True)
        for h in range(blocks):
            bias_ref[h * rows : (h + 1) * rows, :] = rows_ref[h].astype(jnp.bfloat16)
        for copy in copies[3:]:
            copy.wait()

    return pl.pallas_call(
        kernel,
        out_shape=(
            jax.ShapeDtypeStruct((blocks * rows, keys), jnp.bfloat16),
            jax.ShapeDtypeStruct(own.shape, own.dtype),
            jax.ShapeDtypeStruct(noise.shape, noise.dtype),
            jax.ShapeDtypeStruct(w_qkv.shape[1:], w_qkv.dtype),
        ),
        in_specs=[in_hbm()] * 6,
        out_specs=(whole_vmem(),) * 4,
        scratch_shapes=[
            pltpu.VMEM(pair.shape, pair.dtype),
            pltpu.VMEM(mask_row.shape, mask_row.dtype),
            pltpu.VMEM(w_rows.shape, w_rows.dtype),
            pltpu.VMEM((blocks, rows, keys), jnp.float32),
            pltpu.SemaphoreType.DMA((6,)),
        ],
        cost_estimate=pl.CostEstimate(
            flops=2 * blocks * rows * keys * channels, transcendentals=0, bytes_accessed=8000000
        ),
        compiler_params=pltpu.CompilerParams(vmem_limit_bytes=6 * 2**20),
        name="prepare",
    )(*(stay(a) for a in (pair, mask_row, w_rows, own, noise, w_qkv)))


def pack(ancestors, own, other, noise, bias):
    particles, rows, width = own.shape
    used = rows * (width // LANES)

    def kernel(anc_ref, own_ref, other_ref, noise_ref, bias_ref, out_ref):
        dom = lax.axis_index("dom")
        for p in range(particles):
            a = anc_ref[p]
            local = lax.rem(a, particles)
            mine = lax.div(a, particles) == dom
            value = jnp.where(mine, own_ref[local], other_ref[local])
            value = value.astype(jnp.float32) + 0.5 * noise_ref[p].astype(jnp.float32)
            value = value.astype(jnp.bfloat16)
            for k in range(width // LANES):
                out_ref[p, k * rows : (k + 1) * rows, :] = value[:, k * LANES : (k + 1) * LANES]
            out_ref[p, used:, :] = bias_ref[...]

    return pl.pallas_call(
        kernel,
        out_shape=jax.ShapeDtypeStruct((particles, used + bias.shape[0], LANES), jnp.bfloat16),
        in_specs=[in_smem()] + [whole_vmem()] * 4,
        out_specs=whole_vmem(),
        compiler_params=pltpu.CompilerParams(vmem_limit_bytes=6 * 2**20),
        name="pack",
    )(ancestors, own, other, noise, bias)


def across(left, right):
    return lax.dot_general(
        left, right, (((1,), (1,)), ((), ())), preferred_element_type=jnp.float32
    )


def project(normed, w_buf, q_ref, k_ref, v_ref, width, scale):
    q_ref[...] = (
        jnp.dot(normed, w_buf[:, :width], preferred_element_type=jnp.float32) * scale
    ).astype(jnp.bfloat16)
    k_ref[...] = jnp.dot(
        normed, w_buf[:, width : 2 * width], preferred_element_type=jnp.float32
    ).astype(jnp.bfloat16)
    v_ref[...] = jnp.dot(
        normed, w_buf[:, 2 * width :], preferred_element_type=jnp.float32
    ).astype(jnp.bfloat16)


def first_project(received, w_first, rows, width, scale):
    sources = received.shape[0]
    tokens = sources * rows

    def kernel(recv_ref, w_ref, x_ref, q_ref, k_ref, v_ref):
        for s in range(sources):
            for k in range(width // LANES):
                x_ref[s * rows : (s + 1) * rows, k * LANES : (k + 1) * LANES] = recv_ref[
                    s, k * rows : (k + 1) * rows, :
                ]
        normed = layer_norm(x_ref[...]).astype(jnp.bfloat16)
        project(normed, w_ref, q_ref, k_ref, v_ref, width, scale)

    shape = jax.ShapeDtypeStruct((tokens, width), jnp.bfloat16)
    return pl.pallas_call(
        kernel,
        out_shape=(shape,) * 4,
        in_specs=[whole_vmem(), whole_vmem()],
        out_specs=(whole_vmem(),) * 4,
        compiler_params=pltpu.CompilerParams(vmem_limit_bytes=12 * 2**20),
        cost_estimate=pl.CostEstimate(
            flops=6 * tokens * width * width, transcendentals=0, bytes_accessed=8 * width * width
        ),
        name="first_project",
    )(received, w_first)


def layers(mask, stream, query, keys, values, received, other, w_qkv, w_out, rows, heads, scale):
    tokens, width = stream.shape
    layer_count = w_qkv.shape[0]
    sources = received.shape[0]
    head_width = width // heads
    half = heads // 2
    stream_rows = rows * (width // LANES)

    def kernel(
        mask_ref, x_ref, q_in, k_in, v_in, recv_ref, other_ref, wq_hbm, wo_hbm,
        out_ref, x_buf, q_buf, k_buf, v_buf, vt_buf, at_buf, wq_buf, wo_buf, wq_sem, wo_sem,
    ):
        wo_copies = [
            pltpu.make_async_copy(wo_hbm.at[l], wo_buf.at[l], wo_sem.at[l])
            for l in range(layer_count)
        ]
        wq_copies = [
            pltpu.make_async_copy(wq_hbm.at[l], wq_buf.at[l - 1], wq_sem.at[l - 1])
            for l in range(1, layer_count)
        ]
        wo_copies[0].start()
        for l in range(1, layer_count):
            wq_copies[l - 1].start()
            wo_copies[l].start()
        is_first = lax.axis_index("dom") == 0
        anyone = jnp.max(mask_ref[...], axis=-1, keepdims=True)
        floor = jnp.where(anyone > 0, 0.0, MASKED).astype(jnp.float32)
        eye = jnp.where(
            lax.broadcasted_iota(jnp.int32, (tokens, tokens), 0)
            == lax.broadcasted_iota(jnp.int32, (tokens, tokens), 1),
            1.0, 0.0,
        ).astype(jnp.bfloat16)

        for l in range(layer_count):
            q_ref, k_ref, v_ref = (q_in, k_in, v_in) if l == 0 else (q_buf, k_buf, v_buf)
            stream_ref = x_ref if l == 0 else x_buf
            for t in range(0, width, LANES):
                vt_buf[t : t + LANES, :] = across(eye, v_ref[:, t : t + LANES]).astype(jnp.bfloat16)
            for h in range(heads):
                low = h * head_width
                high = low + head_width
                start = low // LANES * LANES
                stop = -(-high // LANES) * LANES
                lane = lax.broadcasted_iota(jnp.int32, (1, stop - start), 1) + start
                inside = jnp.where((lane >= low) & (lane < high), 1.0, 0.0).astype(jnp.bfloat16)
                base = stream_rows + (l * half + h % half) * rows
                near = recv_ref[:, base : base + rows, :].reshape(tokens, tokens)
                far = other_ref[:, base : base + rows, :].reshape(tokens, tokens)
                bias = jnp.where(is_first, near, far) if h < half else jnp.where(is_first, far, near)
                scores = across(
                    jnp.concatenate([k_ref[:, start:stop], eye], axis=1),
                    jnp.concatenate([q_ref[:, start:stop] * inside, bias], axis=1),
                ) + floor
                raised = jnp.exp(scores - jnp.max(scores, axis=0, keepdims=True))
                total = jnp.sum(raised, axis=0, keepdims=True)
                out = jnp.dot(
                    vt_buf[low:high, :], raised.astype(jnp.bfloat16),
                    preferred_element_type=jnp.float32,
                )
                at_buf[low:high, :] = (out * (1.0 / total)).astype(jnp.bfloat16)
            attended = across(eye, at_buf[...]).astype(jnp.bfloat16)
            wo_copies[l].wait()
            update = jnp.dot(attended, wo_buf[l], preferred_element_type=jnp.float32)
            moved = (stream_ref[...].astype(jnp.float32) + update).astype(jnp.bfloat16)
            if l + 1 < layer_count:
                x_buf[...] = moved
                normed = layer_norm(moved).astype(jnp.bfloat16)
                wq_copies[l].wait()
                project(normed, wq_buf.at[l], q_buf, k_buf, v_buf, width, scale)
            else:
                for s in range(sources):
                    out_ref[s] = moved[s * rows : (s + 1) * rows, :]

    wide = pltpu.VMEM((tokens, width), jnp.bfloat16)
    tall = pltpu.VMEM((width, tokens), jnp.bfloat16)
    return pl.pallas_call(
        kernel,
        out_shape=jax.ShapeDtypeStruct((sources, rows, width), jnp.bfloat16),
        in_specs=[whole_vmem()] * 7 + [in_hbm()] * 2,
        out_specs=whole_vmem(),
        scratch_shapes=[
            wide, wide, wide, wide, tall, tall,
            pltpu.VMEM((layer_count - 1, width, 3 * width), jnp.bfloat16),
            pltpu.VMEM((layer_count, width, width), jnp.bfloat16),
            pltpu.SemaphoreType.DMA((layer_count - 1,)),
            pltpu.SemaphoreType.DMA((layer_count,)),
        ],
        compiler_params=pltpu.CompilerParams(vmem_limit_bytes=20 * 2**20),
        cost_estimate=pl.CostEstimate(
            flops=14 * tokens * width * width, transcendentals=2 * heads * tokens * tokens,
            bytes_accessed=10 * width * width,
        ),
        name="layers",
    )(mask, stream, query, keys, values, received, other, stay(w_qkv), stay(w_out))


def spread_body(states, ancestors, noise, pair, token_mask, w_qkv, w_out, w_pair):
    particles, rows, width = states.shape
    heads = w_pair.shape[2]
    scale = (width // heads) ** (-0.5)
    swap = [(0, 1), (1, 0)]
    mask_row = token_mask.reshape(1, -1)
    other_states = lax.ppermute(states, "dom", swap)
    bias, own, local_noise, w_first = prepare(
        pair, mask_row, w_pair.transpose(0, 2, 1), states, noise, w_qkv
    )
    packed = pack(ancestors, own, other_states, local_noise, bias)
    received = lax.all_to_all(packed, "tok", 0, 0, tiled=True)
    other = lax.ppermute(received, "dom", swap)
    stream, query, keys, values = first_project(received, w_first, rows, width, scale)
    result = layers(
        mask_row, stream, query, keys, values, received, other, w_qkv, w_out, rows, heads, scale
    )
    return lax.all_to_all(result, "tok", 0, 0, tiled=True)


def solution(mesh):
    placed = (
        P(("groups", "dom"), "tok", None),
        P(("groups", "dom")),
        P(("groups", "dom"), "tok", None),
        P(("groups", "tok"), None, None),
        P("groups"),
        P(),
        P(),
        P(),
    )

    def body(states, ancestors, noise, pair, token_mask, w_qkv, w_out, w_pair):
        particles, rows, width = states.shape
        fits = (
            particles == mesh.shape["tok"]
            and mesh.shape["dom"] == 2
            and w_pair.shape[2] % 2 == 0
            and pair.shape[1] == LANES
            and pair.shape[2] == LANES
            and width % LANES == 0
            and rows % 16 == 0
            and (width // w_pair.shape[2]) % 16 == 0
        )
        chosen = spread_body if fits else gathered_body
        return chosen(states, ancestors, noise, pair, token_mask, w_qkv, w_out, w_pair)

    return jax.shard_map(
        body,
        mesh=mesh,
        in_specs=placed,
        out_specs=P(("groups", "dom"), "tok", None),
        check_vma=False,
    )
```

time: 61.5 us -> 52 us (0.85)
  local copies, waits for them, and re-layouts: 6.51 us -> 0.69 us
  Pallas kernels: 16 us -> 11.5 us
  waiting for transfers between devices: 0.01 us -> 1.37 us
    unnamed x13 -> x5, local copies, waits for them, and re-layouts: 5.92 us -> 0.69 us
    pallas_call x1, Pallas kernels: 10.1 us -> 7.65 us  [layers(): pl.pallas_call(kernel, out_shape=jax.ShapeDtypeStruct((sources, rows, wid...]
    pallas_call x3, Pallas kernels: 5.91 us -> 3.85 us  [the longest x1 2.38 us: prepare(): pl.pallas_call(kernel, out_shape=(jax.ShapeDtypeStruct((blocks * rows, ke...]
    ppermute x1, waiting for transfers between devices: 0.01 us -> 1.37 us  [spread_body(): other = lax.ppermute(received, 'dom', swap)]
  transfers between devices with their start and end apart: 2 -> 2, of which waited for: 0 -> 1; matrix products, arithmetic and copies ran while one was open for 1% -> 0% of each run, Pallas kernels for 7% -> 6%
where the time goes in v2:
time: 52 us; the launch traced here: 51.8 us
  blocking collectives  37.7 us (73%)
  Pallas kernels  11.5 us (22%)
  waiting for transfers between devices  1.37 us (3%)
  local copies, waits for them, and re-layouts  0.69 us (1%)
    all_to_all x1, blocking collectives, spread_body(): received = lax.all_to_all(packed, 'tok', 0, 0, tiled=True)  26 us
    all_to_all x1, blocking collectives, spread_body(): return lax.all_to_all(result, 'tok', 0, 0, tiled=True)  11.7 us
    pallas_call x1, Pallas kernels, layers(): pl.pallas_call(kernel, out_shape=jax.ShapeDtypeStruct((sources, rows, wid...  7.65 us
    pallas_call x1, Pallas kernels, prepare(): pl.pallas_call(kernel, out_shape=(jax.ShapeDtypeStruct((blocks * rows, ke...  2.38 us
    ppermute x1, waiting for transfers between devices, spread_body(): other = lax.ppermute(received, 'dom', swap)  1.37 us
  transfers between devices with their start and end apart: 2, of which 1 were waited for; matrix products, arithmetic and copies ran while one was open for 0% of the time, Pallas kernels for 6%

profile of v2, /device:TPU:0, one launch (start us, length us, event | category | flops | bytes accessed | tf_op | source)
XLA Modules:
  0.0 51.8 jit_solution(10020643274114682538)
XLA Ops:
  0.0 0.5 collective-permute-start
  0.5 0.0 copy-start.1
  0.5 2.4 %prepare.1 = (bf16[256,128]{1,0:T(8,128)(2,1)S(1)}, bf16[8,16,768]{2,1,0:T(8,128)(2,1)S(1)}, bf16[8,16,768]{2,1,0:T(8,128)(2,1)S(1)}, bf16[768,2304]{1,0:T(8,128)(2,1)S(1)}) custom-call(bf16[16,128,128]{2,1,0:T(8,128)(2,1)} %pair_hbm.1, s32[1,128]{1,0:T(1,128)} %bitcast.2, bf16[2,16,128]{2,1,0:T(8,128)(2,1)} %bitcast.4, bf16[8,16,768]{2,1,0:T(8,128)(2,1)} %own_hbm.1, ...), custom_call_target="tpu_custom_call" | custom-call | flops 8388608 | bytes 8000000 | tf_op jit(solution)/shard_map/prepare/pallas_call | solution.py:123
  2.8 0.0 collective-permute-done.other_ref
  2.9 0.0 copy-done.1
  2.9 0.0 copy-start
  2.9 0.7 %pack.1 = bf16[8,352,128]{2,1,0:T(8,128)(2,1)S(1)} custom-call(s32[8]{0:T(128)S(1)} %copy-done.1, bf16[8,16,768]{2,1,0:T(8,128)(2,1)S(1)} %get-tuple-element.13.own_ref, bf16[8,16,768]{2,1,0:T(8,128)(2,1)S(1)} %collective-permute-done.other_ref, bf16[8,16,768]{2,1,0:T(8,128)(2,1)S(1)} %get-tuple-element.14.noise_ref, ...), custom_call_target="tpu_custom_call" | custom-call | tf_op jit(solution)/shard_map/pack/pallas_call | solution.py:165
  3.5 26.0 %all_to_all.10.recv_ref = bf16[8,352,128]{2,1,0:T(8,128)(2,1)S(1)} all-to-all(bf16[8,352,128]{2,1,0:T(8,128)(2,1)S(1)} %pack.1), channel_id=1, replica_groups=mesh['groups'=2,'tok'=8,'dom'=2] {'tok'}, dimensions={0} | all-to-all | bytes 1441792 | tf_op jit(solution)/shard_map/all_to_all | solution.py:327
  29.6 0.0 collective-permute-start.1
  29.6 0.8 %first_project.1 = (bf16[128,768]{1,0:T(8,128)(2,1)S(1)}, bf16[128,768]{1,0:T(8,128)(2,1)S(1)}, bf16[128,768]{1,0:T(8,128)(2,1)S(1)}, bf16[128,768]{1,0:T(8,128)(2,1)S(1)}) custom-call(bf16[8,352,128]{2,1,0:T(8,128)(2,1)S(1)} %all_to_all.10.recv_ref, bf16[768,2304]{1,0:T(8,128)(2,1)S(1)} %get-tuple-element.16.w_ref), custom_call_target="tpu_custom_call" | custom-call | flops 452984832 | bytes 4718592 | tf_op jit(solution)/shard_map/first_project/pallas_call | solution.py:207
  30.4 1.4 %collective-permute-done.1.other_ref = bf16[8,352,128]{2,1,0:T(8,128)(2,1)S(1)} collective-permute-done((bf16[8,352,128]{2,1,0:T(8,128)(2,1)S(1)}, bf16[8,352,128]{2,1,0:T(8,128)(2,1)S(1)}, u32[]{:S(2)}, u32[]{:S(2)}) %collective-permute-start.1) | collective-permute-done | bytes 720928 | tf_op jit(solution)/shard_map/ppermute | solution.py:328
  31.7 0.0 copy-done
  31.8 7.6 %layers.1 = bf16[8,16,768]{2,1,0:T(8,128)(2,1)S(1)} custom-call(s32[1,128]{1,0:T(1,128)S(1)} %bitcast.3, bf16[128,768]{1,0:T(8,128)(2,1)S(1)} %get-tuple-element.17.x_ref, bf16[128,768]{1,0:T(8,128)(2,1)S(1)} %get-tuple-element.18.q_in, bf16[128,768]{1,0:T(8,128)(2,1)S(1)} %get-tuple-element.19.k_in, bf16[128,768]{1,0:T(8,128)(2,1)S(1)} %get-tuple-element.20.v_in, ...), custom_call_target="tpu_custom_call" | custom-call | flops 1056964608 | bytes 5898240 | tf_op jit(solution)/shard_map/layers/pallas_call | solution.py:295
  39.4 11.7 %all_to_all.11 = bf16[8,16,768]{2,1,0:T(8,128)(2,1)S(1)} all-to-all(bf16[8,16,768]{2,1,0:T(8,128)(2,1)S(1)} %layers.1), channel_id=1, replica_groups=mesh['groups'=2,'tok'=8,'dom'=2] {'tok'}, dimensions={0} | all-to-all | bytes 393216 | tf_op jit(solution)/shard_map/all_to_all | solution.py:333
  51.1 0.7 %copy.10 = bf16[8,16,768]{2,1,0:T(8,128)(2,1)} copy(bf16[8,16,768]{2,1,0:T(8,128)(2,1)S(1)} %all_to_all.11) | data formatting | bytes 393216
Async XLA Ops:
  0.0 2.8 %collective-permute-start = (bf16[8,16,768]{2,1,0:T(8,128)(2,1)}, bf16[8,16,768]{2,1,0:T(8,128)(2,1)S(1)}, u32[]{:S(2)}, u32[]{:S(2)}) collective-permute-start(bf16[8,16,768]{2,1,0:T(8,128)(2,1)} %own_hbm.1), channel_id=1, source_target_pairs={{0,1},{1,0},{2,3},{3,2},{4,5},{5,4},{6,7},{7,6},{8,9},{9,8},{10,11... | collective-permute-start | bytes 589832 | tf_op jit(solution)/shard_map/ppermute | solution.py:322
  0.5 2.4 %copy-start.1 = (s32[8]{0:T(128)S(1)}, s32[8]{0:T(128)}, u32[]{:S(2)}) copy-start(s32[8]{0:T(128)} %anc_ref.1) | copy-start | bytes 100
  2.9 28.9 %copy-start = (s32[128]{0:T(128)S(1)}, s32[128]{0:T(128)}, u32[]{:S(2)}) copy-start(s32[128]{0:T(128)} %param.12) | copy-start | bytes 1540
  29.6 2.2 %collective-permute-start.1 = (bf16[8,352,128]{2,1,0:T(8,128)(2,1)S(1)}, bf16[8,352,128]{2,1,0:T(8,128)(2,1)S(1)}, u32[]{:S(2)}, u32[]{:S(2)}) collective-permute-start(bf16[8,352,128]{2,1,0:T(8,128)(2,1)S(1)} %all_to_all.10.recv_ref), channel_id=1, source_target_pairs={{0,1},{1,0},{2,3},{3,2},{4,5},{5,4},{6,7},{7,6},{8,9},{9,8},{10,11... | collective-permute-start | bytes 2162696 | tf_op jit(solution)/shard_map/ppermute | solution.py:328

commit v3 on v2

--- a/solution.py
+++ b/solution.py
@@ -88,7 +88,7 @@
 
     def kernel(
         pair_hbm, mask_hbm, w_hbm, own_hbm, noise_hbm, wq_hbm,
-        bias_ref, own_ref, noise_ref, first_ref, pair_ref, mask_ref, w_ref, rows_ref, sem,
+        bias_ref, own_ref, noise_ref, pair_ref, mask_ref, w_ref, rows_ref, sem,
     ):
         copies = [
             pltpu.make_async_copy(mask_hbm, mask_ref, sem.at[0]),
@@ -96,7 +96,6 @@
             pltpu.make_async_copy(pair_hbm, pair_ref, sem.at[2]),
             pltpu.make_async_copy(own_hbm, own_ref, sem.at[3]),
             pltpu.make_async_copy(noise_hbm, noise_ref, sem.at[4]),
-            pltpu.make_async_copy(wq_hbm.at[0], first_ref, sem.at[5]),
         ]
         for copy in copies:
             copy.start()
@@ -126,16 +125,15 @@
             jax.ShapeDtypeStruct((blocks * rows, keys), jnp.bfloat16),
             jax.ShapeDtypeStruct(own.shape, own.dtype),
             jax.ShapeDtypeStruct(noise.shape, noise.dtype),
-            jax.ShapeDtypeStruct(w_qkv.shape[1:], w_qkv.dtype),
         ),
         in_specs=[in_hbm()] * 6,
-        out_specs=(whole_vmem(),) * 4,
+        out_specs=(whole_vmem(),) * 3,
         scratch_shapes=[
             pltpu.VMEM(pair.shape, pair.dtype),
             pltpu.VMEM(mask_row.shape, mask_row.dtype),
             pltpu.VMEM(w_rows.shape, w_rows.dtype),
             pltpu.VMEM((blocks, rows, keys), jnp.float32),
-            pltpu.SemaphoreType.DMA((6,)),
+            pltpu.SemaphoreType.DMA((5,)),
         ],
         cost_estimate=pl.CostEstimate(
             flops=2 * blocks * rows * keys * channels, transcendentals=0, bytes_accessed=8000000
@@ -178,114 +176,141 @@
     )
 
 
-def project(normed, w_buf, q_ref, k_ref, v_ref, width, scale):
+def identity(size):
+    down = lax.broadcasted_iota(jnp.int32, (size, size), 0)
+    along = lax.broadcasted_iota(jnp.int32, (size, size), 1)
+    return jnp.where(down == along, 1.0, 0.0).astype(jnp.bfloat16)
+
+
+def project(stream, w_ref, q_ref, k_ref, vt_ref, eye, scale):
+    width = stream.shape[1]
+    normed = layer_norm(stream).astype(jnp.bfloat16)
     q_ref[...] = (
-        jnp.dot(normed, w_buf[:, :width], preferred_element_type=jnp.float32) * scale
+        jnp.dot(normed, w_ref[:, :width], preferred_element_type=jnp.float32) * scale
     ).astype(jnp.bfloat16)
     k_ref[...] = jnp.dot(
-        normed, w_buf[:, width : 2 * width], preferred_element_type=jnp.float32
+        normed, w_ref[:, width : 2 * width], preferred_element_type=jnp.float32
     ).astype(jnp.bfloat16)
-    v_ref[...] = jnp.dot(
-        normed, w_buf[:, 2 * width :], preferred_element_type=jnp.float32
+    values = jnp.dot(
+        normed, w_ref[:, 2 * width :], preferred_element_type=jnp.float32
     ).astype(jnp.bfloat16)
-
-
-def first_project(received, w_first, rows, width, scale):
+    for t in range(0, width, LANES):
+        vt_ref[t : t + LANES, :] = across(eye, values[:, t : t + LANES]).astype(jnp.bfloat16)
+
+
+def attend(groups, first_row, rows, head_width, q_ref, k_ref, vt_ref, at_ref, work, eye, floor):
+    s_buf, e_buf, n_buf = work
+    tokens = eye.shape[0]
+    half = q_ref.shape[1] // head_width // 2
+    every = [(g * half + h, h, base, bias) for g, (base, bias) in enumerate(groups) for h in range(half)]
+    for slot, h, base, bias_ref in every:
+        low = h * head_width
+        high = low + head_width
+        start = low // LANES * LANES
+        stop = -(-high // LANES) * LANES
+        lane = lax.broadcasted_iota(jnp.int32, (1, stop - start), 1) + start
+        inside = jnp.where((lane >= low) & (lane < high), 1.0, 0.0).astype(jnp.bfloat16)
+        cols = pl.ds(pl.multiple_of(base + start, LANES), stop - start)
+        at = first_row + h * rows
+        bias = bias_ref[:, at : at + rows, :].reshape(tokens, tokens)
+        s_buf[slot] = across(
+            jnp.concatenate([k_ref[:, cols], eye], axis=1),
+            jnp.concatenate([q_ref[:, cols] * inside, bias], axis=1),
+        )
+    for slot, h, base, bias_ref in every:
+        scores = s_buf[slot] + floor
+        raised = jnp.exp(scores - jnp.max(scores, axis=0, keepdims=True))
+        n_buf[slot : slot + 1, :] = 1.0 / jnp.sum(raised, axis=0, keepdims=True)
+        e_buf[slot] = raised.astype(jnp.bfloat16)
+    for slot, h, base, bias_ref in every:
+        own = pl.ds(pl.multiple_of(base + h * head_width, 16), head_width)
+        out = jnp.dot(vt_ref[own, :], e_buf[slot], preferred_element_type=jnp.float32)
+        at_ref[own, :] = (out * n_buf[slot : slot + 1, :]).astype(jnp.bfloat16)
+
+
+def row_floor(mask_ref):
+    anyone = jnp.max(mask_ref[...], axis=-1, keepdims=True)
+    return jnp.where(anyone > 0, 0.0, MASKED).astype(jnp.float32)
+
+
+def work_space(slots, tokens):
+    return [
+        pltpu.VMEM((slots, tokens, tokens), jnp.float32),
+        pltpu.VMEM((slots, tokens, tokens), jnp.bfloat16),
+        pltpu.VMEM((slots, tokens), jnp.float32),
+    ]
+
+
+def first_half(mask, received, w_qkv, rows, heads, scale):
     sources = received.shape[0]
     tokens = sources * rows
-
-    def kernel(recv_ref, w_ref, x_ref, q_ref, k_ref, v_ref):
+    width = w_qkv.shape[1]
+    stream_rows = rows * (width // LANES)
+
+    def kernel(mask_ref, recv_ref, w_ref, x_ref, q_ref, k_ref, vt_ref, at_ref, *work):
         for s in range(sources):
             for k in range(width // LANES):
                 x_ref[s * rows : (s + 1) * rows, k * LANES : (k + 1) * LANES] = recv_ref[
                     s, k * rows : (k + 1) * rows, :
                 ]
-        normed = layer_norm(x_ref[...]).astype(jnp.bfloat16)
-        project(normed, w_ref, q_ref, k_ref, v_ref, width, scale)
-
-    shape = jax.ShapeDtypeStruct((tokens, width), jnp.bfloat16)
+        eye = identity(tokens)
+        project(x_ref[...], w_ref.at[0], q_ref, k_ref, vt_ref, eye, scale)
+        near = lax.axis_index("dom") * (width // 2)
+        attend(
+            [(near, recv_ref)], stream_rows, rows, width // heads,
+            q_ref, k_ref, vt_ref, at_ref, work, eye, row_floor(mask_ref),
+        )
+
+    wide = jax.ShapeDtypeStruct((tokens, width), jnp.bfloat16)
+    tall = jax.ShapeDtypeStruct((width, tokens), jnp.bfloat16)
     return pl.pallas_call(
         kernel,
-        out_shape=(shape,) * 4,
-        in_specs=[whole_vmem(), whole_vmem()],
-        out_specs=(whole_vmem(),) * 4,
-        compiler_params=pltpu.CompilerParams(vmem_limit_bytes=12 * 2**20),
+        out_shape=(wide, wide, wide, tall, tall),
+        in_specs=[whole_vmem()] * 3,
+        out_specs=(whole_vmem(),) * 5,
+        scratch_shapes=work_space(heads // 2, tokens),
+        compiler_params=pltpu.CompilerParams(vmem_limit_bytes=8 * 2**20),
         cost_estimate=pl.CostEstimate(
-            flops=6 * tokens * width * width, transcendentals=0, bytes_accessed=8 * width * width
+            flops=6 * tokens * width * width, transcendentals=heads * tokens * tokens // 2,
+            bytes_accessed=8 * width * width,
         ),
-        name="first_project",
-    )(received, w_first)
-
-
-def layers(mask, stream, query, keys, values, received, other, w_qkv, w_out, rows, heads, scale):
+        name="first_half",
+    )(mask, received, w_qkv)
+
+
+def layers(mask, stream, query, keys, values, attended, received, other, w_qkv, w_out, rows, heads, scale):
     tokens, width = stream.shape
     layer_count = w_qkv.shape[0]
     sources = received.shape[0]
-    head_width = width // heads
     half = heads // 2
     stream_rows = rows * (width // LANES)
 
     def kernel(
-        mask_ref, x_ref, q_in, k_in, v_in, recv_ref, other_ref, wq_hbm, wo_hbm,
-        out_ref, x_buf, q_buf, k_buf, v_buf, vt_buf, at_buf, wq_buf, wo_buf, wq_sem, wo_sem,
+        mask_ref, x_ref, q_in, k_in, vt_in, at_in, recv_ref, other_ref, wq_ref, wo_ref,
+        out_ref, x_buf, q_buf, k_buf, vt_buf, at_buf, *work,
     ):
-        wo_copies = [
-            pltpu.make_async_copy(wo_hbm.at[l], wo_buf.at[l], wo_sem.at[l])
-            for l in range(layer_count)
-        ]
-        wq_copies = [
-            pltpu.make_async_copy(wq_hbm.at[l], wq_buf.at[l - 1], wq_sem.at[l - 1])
-            for l in range(1, layer_count)
-        ]
-        wo_copies[0].start()
-        for l in range(1, layer_count):
-            wq_copies[l - 1].start()
-            wo_copies[l].start()
-        is_first = lax.axis_index("dom") == 0
-        anyone = jnp.max(mask_ref[...], axis=-1, keepdims=True)
-        floor = jnp.where(anyone > 0, 0.0, MASKED).astype(jnp.float32)
-        eye = jnp.where(
-            lax.broadcasted_iota(jnp.int32, (tokens, tokens), 0)
-            == lax.broadcasted_iota(jnp.int32, (tokens, tokens), 1),
-            1.0, 0.0,
-        ).astype(jnp.bfloat16)
+        here = lax.axis_index("dom")
+        near = here * (width // 2)
+        far = (1 - here) * (width // 2)
+        floor = row_floor(mask_ref)
+        eye = identity(tokens)
+        ready = pl.ds(pl.multiple_of(near, LANES), width // 2)
+        at_buf[ready, :] = at_in[ready, :]
 
         for l in range(layer_count):
-            q_ref, k_ref, v_ref = (q_in, k_in, v_in) if l == 0 else (q_buf, k_buf, v_buf)
+            q_ref, k_ref, vt_ref = (q_in, k_in, vt_in) if l == 0 else (q_buf, k_buf, vt_buf)
             stream_ref = x_ref if l == 0 else x_buf
-            for t in range(0, width, LANES):
-                vt_buf[t : t + LANES, :] = across(eye, v_ref[:, t : t + LANES]).astype(jnp.bfloat16)
-            for h in range(heads):
-                low = h * head_width
-                high = low + head_width
-                start = low // LANES * LANES
-                stop = -(-high // LANES) * LANES
-                lane = lax.broadcasted_iota(jnp.int32, (1, stop - start), 1) + start
-                inside = jnp.where((lane >= low) & (lane < high), 1.0, 0.0).astype(jnp.bfloat16)
-                base = stream_rows + (l * half + h % half) * rows
-                near = recv_ref[:, base : base + rows, :].reshape(tokens, tokens)
-                far = other_ref[:, base : base + rows, :].reshape(tokens, tokens)
-                bias = jnp.where(is_first, near, far) if h < half else jnp.where(is_first, far, near)
-                scores = across(
-                    jnp.concatenate([k_ref[:, start:stop], eye], axis=1),
-                    jnp.concatenate([q_ref[:, start:stop] * inside, bias], axis=1),
-                ) + floor
-                raised = jnp.exp(scores - jnp.max(scores, axis=0, keepdims=True))
-                total = jnp.sum(raised, axis=0, keepdims=True)
-                out = jnp.dot(
-                    vt_buf[low:high, :], raised.astype(jnp.bfloat16),
-                    preferred_element_type=jnp.float32,
-                )
-                at_buf[low:high, :] = (out * (1.0 / total)).astype(jnp.bfloat16)
-            attended = across(eye, at_buf[...]).astype(jnp.bfloat16)
-            wo_copies[l].wait()
-            update = jnp.dot(attended, wo_buf[l], preferred_element_type=jnp.float32)
+            groups = [(far, other_ref)] if l == 0 else [(near, recv_ref), (far, other_ref)]
+            attend(
+                groups, stream_rows + l * half * rows, rows, width // heads,
+                q_ref, k_ref, vt_ref, at_buf, work, eye, floor,
+            )
+            together = across(eye, at_buf[...]).astype(jnp.bfloat16)
+            update = jnp.dot(together, wo_ref[l], preferred_element_type=jnp.float32)
             moved = (stream_ref[...].astype(jnp.float32) + update).astype(jnp.bfloat16)
             if l + 1 < layer_count:
                 x_buf[...] = moved
-                normed = layer_norm(moved).astype(jnp.bfloat16)
-                wq_copies[l].wait()
-                project(normed, wq_buf.at[l], q_buf, k_buf, v_buf, width, scale)
+                project(moved, wq_ref.at[l + 1], q_buf, k_buf, vt_buf, eye, scale)
             else:
                 for s in range(sources):
                     out_ref[s] = moved[s * rows : (s + 1) * rows, :]
@@ -295,22 +320,18 @@
     return pl.pallas_call(
         kernel,
         out_shape=jax.ShapeDtypeStruct((sources, rows, width), jnp.bfloat16),
-        in_specs=[whole_vmem()] * 7 + [in_hbm()] * 2,
+        in_specs=[whole_vmem()] * 10,
         out_specs=whole_vmem(),
         scratch_shapes=[
-            wide, wide, wide, wide, tall, tall,
-            pltpu.VMEM((layer_count - 1, width, 3 * width), jnp.bfloat16),
-            pltpu.VMEM((layer_count, width, width), jnp.bfloat16),
-            pltpu.SemaphoreType.DMA((layer_count - 1,)),
-            pltpu.SemaphoreType.DMA((layer_count,)),
-        ],
-        compiler_params=pltpu.CompilerParams(vmem_limit_bytes=20 * 2**20),
+            wide, wide, wide, tall, tall,
+        ] + work_space(heads, tokens),
+        compiler_params=pltpu.CompilerParams(vmem_limit_bytes=8 * 2**20),
         cost_estimate=pl.CostEstimate(
             flops=14 * tokens * width * width, transcendentals=2 * heads * tokens * tokens,
             bytes_accessed=10 * width * width,
         ),
         name="layers",
-    )(mask, stream, query, keys, values, received, other, stay(w_qkv), stay(w_out))
+    )(mask, stream, query, keys, values, attended, received, other, w_qkv, w_out)
 
 
 def spread_body(states, ancestors, noise, pair, token_mask, w_qkv, w_out, w_pair):
@@ -320,16 +341,14 @@
     swap = [(0, 1), (1, 0)]
     mask_row = token_mask.reshape(1, -1)
     other_states = lax.ppermute(states, "dom", swap)
-    bias, own, local_noise, w_first = prepare(
+    bias, own, local_noise = prepare(
         pair, mask_row, w_pair.transpose(0, 2, 1), states, noise, w_qkv
     )
     packed = pack(ancestors, own, other_states, local_noise, bias)
     received = lax.all_to_all(packed, "tok", 0, 0, tiled=True)
     other = lax.ppermute(received, "dom", swap)
-    stream, query, keys, values = first_project(received, w_first, rows, width, scale)
-    result = layers(
-        mask_row, stream, query, keys, values, received, other, w_qkv, w_out, rows, heads, scale
-    )
+    state = first_half(mask_row, received, w_qkv, rows, heads, scale)
+    result = layers(mask_row, *state, received, other, w_qkv, w_out, rows, heads, scale)
     return lax.all_to_all(result, "tok", 0, 0, tiled=True)
 
 
@@ -350,10 +369,9 @@
         fits = (
             particles == mesh.shape["tok"]
             and mesh.shape["dom"] == 2
-            and w_pair.shape[2] % 2 == 0
+            and width % (2 * LANES) == 0
             and pair.shape[1] == LANES
             and pair.shape[2] == LANES
-            and width % LANES == 0
             and rows % 16 == 0
             and (width // w_pair.shape[2]) % 16 == 0
         )

time: 52 us -> 47 us (0.904)
  Pallas kernels: 11.5 us -> 6.99 us
  waiting for transfers between devices: 1.37 us -> 0.71 us
    pallas_call x1, Pallas kernels: 7.65 us -> 3.02 us  [layers(): pl.pallas_call(kernel, out_shape=jax.ShapeDtypeStruct((sources, rows, wid...]
    ppermute x1, waiting for transfers between devices: 1.37 us -> 0.7 us  [spread_body(): other = lax.ppermute(received, 'dom', swap)]
    pallas_call x1, Pallas kernels: 0.81 us -> 1.48 us  [first_half(): pl.pallas_call(kernel, out_shape=(wide, wide, wide, tall, tall), in_specs...]
    pallas_call x1, Pallas kernels: 2.38 us -> 1.83 us  [prepare(): pl.pallas_call(kernel, out_shape=(jax.ShapeDtypeStruct((blocks * rows, ke...]
  transfers between devices with their start and end apart: 2 -> 2, of which waited for: 1 -> 1; matrix products, arithmetic and copies ran while one was open for 0% -> 0% of each run, Pallas kernels for 6% -> 7%
where the time goes in v3:
time: 47 us; the launch traced here: 46.8 us
  blocking collectives  37.8 us (80%)
  Pallas kernels  6.99 us (15%)
  waiting for transfers between devices  0.71 us (2%)
  local copies, waits for them, and re-layouts  0.69 us (1%)
  starting transfers between devices  0.52 us (1%)
    all_to_all x1, blocking collectives, spread_body(): received = lax.all_to_all(packed, 'tok', 0, 0, tiled=True)  26.1 us
    all_to_all x1, blocking collectives, spread_body(): return lax.all_to_all(result, 'tok', 0, 0, tiled=True)  11.7 us
    pallas_call x1, Pallas kernels, layers(): pl.pallas_call(kernel, out_shape=jax.ShapeDtypeStruct((sources, rows, wid...  3.02 us
    pallas_call x1, Pallas kernels, prepare(): pl.pallas_call(kernel, out_shape=(jax.ShapeDtypeStruct((blocks * rows, ke...  1.83 us
    pallas_call x1, Pallas kernels, first_half(): pl.pallas_call(kernel, out_shape=(wide, wide, wide, tall, tall), in_specs...  1.48 us
  transfers between devices with their start and end apart: 2, of which 1 were waited for; matrix products, arithmetic and copies ran while one was open for 0% of the time, Pallas kernels for 7%

profile of v3, /device:TPU:0, one launch (start us, length us, event | category | flops | bytes accessed | tf_op | source)
XLA Modules:
  0.0 46.8 jit_solution(15311094860191400049)
XLA Ops:
  0.0 0.0 copy-start
  0.0 0.0 copy-start.2
  0.0 0.0 copy-start.3
  0.0 0.5 %collective-permute-start = (bf16[8,16,768]{2,1,0:T(8,128)(2,1)}, bf16[8,16,768]{2,1,0:T(8,128)(2,1)S(1)}, u32[]{:S(2)}, u32[]{:S(2)}) collective-permute-start(bf16[8,16,768]{2,1,0:T(8,128)(2,1)} %own_hbm.1), channel_id=1, source_target_pairs={{0,1},{1,0},{2,3},{3,2},{4,5},{5,4},{6,7},{7,6},{8,9},{9,8},{10,11... | collective-permute-start | bytes 589832 | tf_op jit(solution)/shard_map/ppermute | solution.py:343
  0.5 1.8 %prepare.1 = (bf16[256,128]{1,0:T(8,128)(2,1)S(1)}, bf16[8,16,768]{2,1,0:T(8,128)(2,1)S(1)}, bf16[8,16,768]{2,1,0:T(8,128)(2,1)S(1)}) custom-call(bf16[16,128,128]{2,1,0:T(8,128)(2,1)} %pair_hbm.1, s32[1,128]{1,0:T(1,128)} %bitcast.2, bf16[2,16,128]{2,1,0:T(8,128)(2,1)} %bitcast.5, bf16[8,16,768]{2,1,0:T(8,128)(2,1)} %own_hbm.1, ...), custom_call_target="tpu_custom_call" | custom-call | flops 8388608 | bytes 8000000 | tf_op jit(solution)/shard_map/prepare/pallas_call | solution.py:122
  2.4 0.0 copy-start.1
  2.4 0.0 collective-permute-done.other_ref
  2.4 0.0 copy-done.3
  2.4 0.7 %pack.1 = bf16[8,352,128]{2,1,0:T(8,128)(2,1)S(1)} custom-call(s32[8]{0:T(128)S(1)} %copy-done.3, bf16[8,16,768]{2,1,0:T(8,128)(2,1)S(1)} %get-tuple-element.13.own_ref, bf16[8,16,768]{2,1,0:T(8,128)(2,1)S(1)} %collective-permute-done.other_ref, bf16[8,16,768]{2,1,0:T(8,128)(2,1)S(1)} %get-tuple-element.14.noise_ref, ...), custom_call_target="tpu_custom_call" | custom-call | tf_op jit(solution)/shard_map/pack/pallas_call | solution.py:163
  3.1 26.1 %all_to_all.10.recv_ref = bf16[8,352,128]{2,1,0:T(8,128)(2,1)S(1)} all-to-all(bf16[8,352,128]{2,1,0:T(8,128)(2,1)S(1)} %pack.1), channel_id=1, replica_groups=mesh['groups'=2,'tok'=8,'dom'=2] {'tok'}, dimensions={0} | all-to-all | bytes 1441792 | tf_op jit(solution)/shard_map/all_to_all | solution.py:348
  29.2 0.0 collective-permute-start.1
  29.2 0.0 copy-done
  29.2 0.0 copy-done.2
  29.2 1.5 %first_half.1 = (bf16[128,768]{1,0:T(8,128)(2,1)S(1)}, bf16[128,768]{1,0:T(8,128)(2,1)S(1)}, bf16[128,768]{1,0:T(8,128)(2,1)S(1)}, bf16[768,128]{1,0:T(8,128)(2,1)S(1)}, bf16[768,128]{1,0:T(8,128)(2,1)S(1)}) custom-call(s32[1,128]{1,0:T(1,128)S(1)} %bitcast.3, bf16[8,352,128]{2,1,0:T(8,128)(2,1)S(1)} %all_to_all.10.recv_ref, bf16[2,768,2304]{2,1,0:T(8,128)(2,1)S(1)} %copy-done), custom_call_target="tpu_custom_call" | custom-call | flops 452984832 | bytes 4718592 | tf_op jit(solution)/shard_map/first_half/pallas_call | solution.py:266
  30.6 0.7 %collective-permute-done.1.other_ref = bf16[8,352,128]{2,1,0:T(8,128)(2,1)S(1)} collective-permute-done((bf16[8,352,128]{2,1,0:T(8,128)(2,1)S(1)}, bf16[8,352,128]{2,1,0:T(8,128)(2,1)S(1)}, u32[]{:S(2)}, u32[]{:S(2)}) %collective-permute-start.1) | collective-permute-done | bytes 720928 | tf_op jit(solution)/shard_map/ppermute | solution.py:349
  31.3 0.0 copy-done.1
  31.3 3.0 %layers.1 = bf16[8,16,768]{2,1,0:T(8,128)(2,1)S(1)} custom-call(s32[1,128]{1,0:T(1,128)S(1)} %bitcast.4, bf16[128,768]{1,0:T(8,128)(2,1)S(1)} %get-tuple-element.16.x_ref, bf16[128,768]{1,0:T(8,128)(2,1)S(1)} %get-tuple-element.17.q_in, bf16[128,768]{1,0:T(8,128)(2,1)S(1)} %get-tuple-element.18.k_in, bf16[768,128]{1,0:T(8,128)(2,1)S(1)} %get-tuple-element.19.vt_in, ...), custom_call_target="tpu_custom_call" | custom-call | flops 1056964608 | bytes 5898240 | tf_op jit(solution)/shard_map/layers/pallas_call | solution.py:320
  34.4 11.7 %all_to_all.11 = bf16[8,16,768]{2,1,0:T(8,128)(2,1)S(1)} all-to-all(bf16[8,16,768]{2,1,0:T(8,128)(2,1)S(1)} %layers.1), channel_id=1, replica_groups=mesh['groups'=2,'tok'=8,'dom'=2] {'tok'}, dimensions={0} | all-to-all | bytes 393216 | tf_op jit(solution)/shard_map/all_to_all | solution.py:352
  46.1 0.7 %copy.10 = bf16[8,16,768]{2,1,0:T(8,128)(2,1)} copy(bf16[8,16,768]{2,1,0:T(8,128)(2,1)S(1)} %all_to_all.11) | data formatting | bytes 393216
Async XLA Ops:
  0.0 29.2 %copy-start = (bf16[2,768,2304]{2,1,0:T(8,128)(2,1)S(1)}, bf16[2,768,2304]{2,1,0:T(8,128)(2,1)}, u32[]{:S(2)}) copy-start(bf16[2,768,2304]{2,1,0:T(8,128)(2,1)} %wq_ref.1) | copy-start | bytes 21233668
  0.0 29.2 %copy-start.2 = (s32[128]{0:T(128)S(1)}, s32[128]{0:T(128)}, u32[]{:S(2)}) copy-start(s32[128]{0:T(128)} %param.12) | copy-start | bytes 1540
  0.0 2.4 %copy-start.3 = (s32[8]{0:T(128)S(1)}, s32[8]{0:T(128)}, u32[]{:S(2)}) copy-start(s32[8]{0:T(128)} %anc_ref.1) | copy-start | bytes 100
  0.0 2.4 %collective-permute-start = (bf16[8,16,768]{2,1,0:T(8,128)(2,1)}, bf16[8,16,768]{2,1,0:T(8,128)(2,1)S(1)}, u32[]{:S(2)}, u32[]{:S(2)}) collective-permute-start(bf16[8,16,768]{2,1,0:T(8,128)(2,1)} %own_hbm.1), channel_id=1, source_target_pairs={{0,1},{1,0},{2,3},{3,2},{4,5},{5,4},{6,7},{7,6},{8,9},{9,8},{10,11... | collective-permute-start | bytes 589832 | tf_op jit(solution)/shard_map/ppermute | solution.py:343
  2.4 29.0 %copy-start.1 = (bf16[2,768,768]{2,1,0:T(8,128)(2,1)S(1)}, bf16[2,768,768]{2,1,0:T(8,128)(2,1)}, u32[]{:S(2)}) copy-start(bf16[2,768,768]{2,1,0:T(8,128)(2,1)} %wo_ref.1) | copy-start | bytes 7077892
  29.2 2.2 %collective-permute-start.1 = (bf16[8,352,128]{2,1,0:T(8,128)(2,1)S(1)}, bf16[8,352,128]{2,1,0:T(8,128)(2,1)S(1)}, u32[]{:S(2)}, u32[]{:S(2)}) collective-permute-start(bf16[8,352,128]{2,1,0:T(8,128)(2,1)S(1)} %all_to_all.10.recv_ref), channel_id=1, source_target_pairs={{0,1},{1,0},{2,3},{3,2},{4,5},{5,4},{6,7},{7,6},{8,9},{9,8},{10,11... | collective-permute-start | bytes 2162696 | tf_op jit(solution)/shard_map/ppermute | solution.py:349

commit v4 on v3

--- a/solution.py
+++ b/solution.py
@@ -82,9 +82,7 @@
 
 def prepare(pair, mask_row, w_rows, own, noise, w_qkv):
     rows, keys, channels = pair.shape
-    layer_count, heads, _ = w_rows.shape
-    half = heads // 2
-    blocks = layer_count * half
+    blocks = w_rows.shape[0]
 
     def kernel(
         pair_hbm, mask_hbm, w_hbm, own_hbm, noise_hbm, wq_hbm,
@@ -102,17 +100,9 @@
         copies[0].wait()
         copies[1].wait()
         penalty = jnp.where(mask_ref[...] > 0, 0.0, MASKED).astype(jnp.float32)
-        is_first = lax.axis_index("dom") == 0
-        sent = jnp.concatenate(
-            [
-                jnp.where(is_first, w[:half], w[half:])
-                for w in (w_ref[l].astype(jnp.float32) for l in range(layer_count))
-            ],
-            axis=0,
-        ).astype(jnp.bfloat16)
         copies[2].wait()
         for i in range(rows):
-            piece = across(sent, pair_ref[i]) + penalty
+            piece = across(w_ref[...], pair_ref[i]) + penalty
             rows_ref[:, i, :] = piece - jnp.max(piece, axis=-1, keepdims=True)
         for h in range(blocks):
             bias_ref[h * rows : (h + 1) * rows, :] = rows_ref[h].astype(jnp.bfloat16)
@@ -143,31 +133,51 @@
     )(*(stay(a) for a in (pair, mask_row, w_rows, own, noise, w_qkv)))
 
 
-def pack(ancestors, own, other, noise, bias):
+def block_source(position):
+    here, dom = lax.axis_index("tok"), lax.axis_index("dom")
+    if position < 2:
+        return jnp.bitwise_xor(here, position)
+    return jnp.bitwise_xor(here, position + dom if position % 2 == 0 else position - dom)
+
+
+def pack(ancestors, other_ancestors, own, other, noise, other_noise, bias):
     particles, rows, width = own.shape
     used = rows * (width // LANES)
-
-    def kernel(anc_ref, own_ref, other_ref, noise_ref, bias_ref, out_ref):
+    total = bias.shape[0]
+    served = [0, 1] + list(range(2, particles, 2))
+
+    def kernel(anc_ref, far_anc_ref, own_ref, other_ref, noise_ref, far_noise_ref, bias_ref, *outs):
         dom = lax.axis_index("dom")
-        for p in range(particles):
-            a = anc_ref[p]
-            local = lax.rem(a, particles)
-            mine = lax.div(a, particles) == dom
+
+        def put(out_ref, first, ancestor, noise_block):
+            local = lax.rem(ancestor, particles)
+            mine = lax.div(ancestor, particles) == dom
             value = jnp.where(mine, own_ref[local], other_ref[local])
-            value = value.astype(jnp.float32) + 0.5 * noise_ref[p].astype(jnp.float32)
+            value = value.astype(jnp.float32) + 0.5 * noise_block.astype(jnp.float32)
             value = value.astype(jnp.bfloat16)
             for k in range(width // LANES):
-                out_ref[p, k * rows : (k + 1) * rows, :] = value[:, k * LANES : (k + 1) * LANES]
-            out_ref[p, used:, :] = bias_ref[...]
+                out_ref[first + k * rows : first + (k + 1) * rows, :] = value[
+                    :, k * LANES : (k + 1) * LANES
+                ]
+
+        for position, out_ref in zip(served, outs):
+            target = block_source(position)
+            put(out_ref, 0, anc_ref[target], noise_ref[target])
+            out_ref[used : used + total, :] = bias_ref[...]
+            if position > 1:
+                put(out_ref, used + total, far_anc_ref[target], far_noise_ref[target])
 
     return pl.pallas_call(
         kernel,
-        out_shape=jax.ShapeDtypeStruct((particles, used + bias.shape[0], LANES), jnp.bfloat16),
-        in_specs=[in_smem()] + [whole_vmem()] * 4,
-        out_specs=whole_vmem(),
+        out_shape=tuple(
+            jax.ShapeDtypeStruct((total + used * (1 if p < 2 else 2), LANES), own.dtype)
+            for p in served
+        ),
+        in_specs=[in_smem()] * 2 + [whole_vmem()] * 5,
+        out_specs=(whole_vmem(),) * len(served),
         compiler_params=pltpu.CompilerParams(vmem_limit_bytes=6 * 2**20),
         name="pack",
-    )(ancestors, own, other, noise, bias)
+    )(ancestors, other_ancestors, own, other, noise, other_noise, bias)
 
 
 def across(left, right):
@@ -182,10 +192,14 @@
     return jnp.where(down == along, 1.0, 0.0).astype(jnp.bfloat16)
 
 
-def project(stream, w_ref, q_ref, k_ref, vt_ref, eye, scale):
-    width = stream.shape[1]
+def block_rows(position, rows):
+    return pl.ds(pl.multiple_of(block_source(position) * rows, rows), rows)
+
+
+def project(stream, w_ref, q_ref, k_ref, vt_ref, n_ref, eye, scale, rows):
+    tokens, width = stream.shape
     normed = layer_norm(stream).astype(jnp.bfloat16)
-    q_ref[...] = (
+    n_ref[...] = (
         jnp.dot(normed, w_ref[:, :width], preferred_element_type=jnp.float32) * scale
     ).astype(jnp.bfloat16)
     k_ref[...] = jnp.dot(
@@ -196,36 +210,35 @@
     ).astype(jnp.bfloat16)
     for t in range(0, width, LANES):
         vt_ref[t : t + LANES, :] = across(eye, values[:, t : t + LANES]).astype(jnp.bfloat16)
-
-
-def attend(groups, first_row, rows, head_width, q_ref, k_ref, vt_ref, at_ref, work, eye, floor):
+    for p in range(tokens // rows):
+        q_ref[p * rows : (p + 1) * rows, :] = n_ref[block_rows(p, rows), :]
+
+
+def attend(blocks, first_row, rows, head_width, q_ref, k_ref, vt_ref, at_ref, work, eye, floor):
     s_buf, e_buf, n_buf = work
-    tokens = eye.shape[0]
-    half = q_ref.shape[1] // head_width // 2
-    every = [(g * half + h, h, base, bias) for g, (base, bias) in enumerate(groups) for h in range(half)]
-    for slot, h, base, bias_ref in every:
+    heads = q_ref.shape[1] // head_width
+    for h in range(heads):
         low = h * head_width
         high = low + head_width
         start = low // LANES * LANES
         stop = -(-high // LANES) * LANES
         lane = lax.broadcasted_iota(jnp.int32, (1, stop - start), 1) + start
         inside = jnp.where((lane >= low) & (lane < high), 1.0, 0.0).astype(jnp.bfloat16)
-        cols = pl.ds(pl.multiple_of(base + start, LANES), stop - start)
         at = first_row + h * rows
-        bias = bias_ref[:, at : at + rows, :].reshape(tokens, tokens)
-        s_buf[slot] = across(
-            jnp.concatenate([k_ref[:, cols], eye], axis=1),
-            jnp.concatenate([q_ref[:, cols] * inside, bias], axis=1),
-        )
-    for slot, h, base, bias_ref in every:
-        scores = s_buf[slot] + floor
+        bias = jnp.concatenate([block[at : at + rows, :] for block in blocks], axis=0)
+        s_buf[h] = across(
+            jnp.concatenate([k_ref[:, start:stop], eye], axis=1),
+            jnp.concatenate([q_ref[:, start:stop] * inside, bias], axis=1),
+        )
+    for h in range(heads):
+        scores = s_buf[h] + floor
         raised = jnp.exp(scores - jnp.max(scores, axis=0, keepdims=True))
-        n_buf[slot : slot + 1, :] = 1.0 / jnp.sum(raised, axis=0, keepdims=True)
-        e_buf[slot] = raised.astype(jnp.bfloat16)
-    for slot, h, base, bias_ref in every:
-        own = pl.ds(pl.multiple_of(base + h * head_width, 16), head_width)
-        out = jnp.dot(vt_ref[own, :], e_buf[slot], preferred_element_type=jnp.float32)
-        at_ref[own, :] = (out * n_buf[slot : slot + 1, :]).astype(jnp.bfloat16)
+        n_buf[h : h + 1, :] = 1.0 / jnp.sum(raised, axis=0, keepdims=True)
+        e_buf[h] = raised.astype(jnp.bfloat16)
+    for h in range(heads):
+        own = slice(h * head_width, (h + 1) * head_width)
+        out = jnp.dot(vt_ref[own, :], e_buf[h], preferred_element_type=jnp.float32)
+        at_ref[own, :] = (out * n_buf[h : h + 1, :]).astype(jnp.bfloat16)
 
 
 def row_floor(mask_ref):
@@ -241,76 +254,66 @@
     ]
 
 
-def first_half(mask, received, w_qkv, rows, heads, scale):
-    sources = received.shape[0]
+def first_project(blocks, w_qkv, rows, bias_rows, scale):
+    sources = len(blocks)
+    width = w_qkv.shape[1]
     tokens = sources * rows
-    width = w_qkv.shape[1]
-    stream_rows = rows * (width // LANES)
-
-    def kernel(mask_ref, recv_ref, w_ref, x_ref, q_ref, k_ref, vt_ref, at_ref, *work):
-        for s in range(sources):
+
+    def kernel(w_ref, *refs):
+        blocks, (x_ref, q_ref, k_ref, vt_ref, n_ref) = refs[:sources], refs[sources:]
+        for p in range(sources):
+            first = 0 if p < 2 or p % 2 == 0 else rows * (width // LANES) + bias_rows
             for k in range(width // LANES):
-                x_ref[s * rows : (s + 1) * rows, k * LANES : (k + 1) * LANES] = recv_ref[
-                    s, k * rows : (k + 1) * rows, :
+                x_ref[block_rows(p, rows), k * LANES : (k + 1) * LANES] = blocks[p][
+                    first + k * rows : first + (k + 1) * rows, :
                 ]
-        eye = identity(tokens)
-        project(x_ref[...], w_ref.at[0], q_ref, k_ref, vt_ref, eye, scale)
-        near = lax.axis_index("dom") * (width // 2)
-        attend(
-            [(near, recv_ref)], stream_rows, rows, width // heads,
-            q_ref, k_ref, vt_ref, at_ref, work, eye, row_floor(mask_ref),
+        project(
+            x_ref[...], w_ref.at[0], q_ref, k_ref, vt_ref, n_ref, identity(tokens), scale, rows
         )
 
     wide = jax.ShapeDtypeStruct((tokens, width), jnp.bfloat16)
-    tall = jax.ShapeDtypeStruct((width, tokens), jnp.bfloat16)
     return pl.pallas_call(
         kernel,
-        out_shape=(wide, wide, wide, tall, tall),
-        in_specs=[whole_vmem()] * 3,
-        out_specs=(whole_vmem(),) * 5,
-        scratch_shapes=work_space(heads // 2, tokens),
+        out_shape=(wide, wide, wide, jax.ShapeDtypeStruct((width, tokens), jnp.bfloat16)),
+        in_specs=[whole_vmem()] * (1 + sources),
+        out_specs=(whole_vmem(),) * 4,
+        scratch_shapes=[pltpu.VMEM((tokens, width), jnp.bfloat16)],
         compiler_params=pltpu.CompilerParams(vmem_limit_bytes=8 * 2**20),
         cost_estimate=pl.CostEstimate(
-            flops=6 * tokens * width * width, transcendentals=heads * tokens * tokens // 2,
-            bytes_accessed=8 * width * width,
+            flops=6 * tokens * width * width, transcendentals=0, bytes_accessed=8 * width * width
         ),
-        name="first_half",
-    )(mask, received, w_qkv)
-
-
-def layers(mask, stream, query, keys, values, attended, received, other, w_qkv, w_out, rows, heads, scale):
+        name="first_project",
+    )(w_qkv, *blocks)
+
+
+def layers(mask, stream, query, keys, values, blocks, w_qkv, w_out, heads, scale):
     tokens, width = stream.shape
+    sources = len(blocks)
+    rows = tokens // sources
     layer_count = w_qkv.shape[0]
-    sources = received.shape[0]
-    half = heads // 2
-    stream_rows = rows * (width // LANES)
-
-    def kernel(
-        mask_ref, x_ref, q_in, k_in, vt_in, at_in, recv_ref, other_ref, wq_ref, wo_ref,
-        out_ref, x_buf, q_buf, k_buf, vt_buf, at_buf, *work,
-    ):
-        here = lax.axis_index("dom")
-        near = here * (width // 2)
-        far = (1 - here) * (width // 2)
+
+    def kernel(mask_ref, x_ref, q_in, k_in, vt_in, wq_ref, wo_ref, *refs):
+        bias_refs, refs = refs[:sources], refs[sources:]
+        out_ref, x_buf, q_buf, k_buf, vt_buf, at_buf, n_buf, *work = refs
         floor = row_floor(mask_ref)
         eye = identity(tokens)
-        ready = pl.ds(pl.multiple_of(near, LANES), width // 2)
-        at_buf[ready, :] = at_in[ready, :]
-
         for l in range(layer_count):
             q_ref, k_ref, vt_ref = (q_in, k_in, vt_in) if l == 0 else (q_buf, k_buf, vt_buf)
-            stream_ref = x_ref if l == 0 else x_buf
-            groups = [(far, other_ref)] if l == 0 else [(near, recv_ref), (far, other_ref)]
             attend(
-                groups, stream_rows + l * half * rows, rows, width // heads,
+                bias_refs, (width // LANES + l * heads) * rows, rows, width // heads,
                 q_ref, k_ref, vt_ref, at_buf, work, eye, floor,
             )
             together = across(eye, at_buf[...]).astype(jnp.bfloat16)
-            update = jnp.dot(together, wo_ref[l], preferred_element_type=jnp.float32)
-            moved = (stream_ref[...].astype(jnp.float32) + update).astype(jnp.bfloat16)
+            for p in range(sources):
+                n_buf[block_rows(p, rows), :] = together[p * rows : (p + 1) * rows, :]
+            update = jnp.dot(n_buf[...], wo_ref[l], preferred_element_type=jnp.float32)
+            before = x_ref[...] if l == 0 else x_buf[...]
+            moved = (before.astype(jnp.float32) + update).astype(jnp.bfloat16)
             if l + 1 < layer_count:
                 x_buf[...] = moved
-                project(moved, wq_ref.at[l + 1], q_buf, k_buf, vt_buf, eye, scale)
+                project(
+                    moved, wq_ref.at[l + 1], q_buf, k_buf, vt_buf, n_buf, eye, scale, rows
+                )
             else:
                 for s in range(sources):
                     out_ref[s] = moved[s * rows : (s + 1) * rows, :]
@@ -320,35 +323,47 @@
     return pl.pallas_call(
         kernel,
         out_shape=jax.ShapeDtypeStruct((sources, rows, width), jnp.bfloat16),
-        in_specs=[whole_vmem()] * 10,
+        in_specs=[whole_vmem()] * (7 + sources),
         out_specs=whole_vmem(),
-        scratch_shapes=[
-            wide, wide, wide, tall, tall,
-        ] + work_space(heads, tokens),
+        scratch_shapes=[wide, wide, wide, tall, tall, wide] + work_space(heads, tokens),
         compiler_params=pltpu.CompilerParams(vmem_limit_bytes=8 * 2**20),
         cost_estimate=pl.CostEstimate(
             flops=14 * tokens * width * width, transcendentals=2 * heads * tokens * tokens,
             bytes_accessed=10 * width * width,
         ),
         name="layers",
-    )(mask, stream, query, keys, values, attended, received, other, w_qkv, w_out)
+    )(mask, stream, query, keys, values, w_qkv, w_out, *blocks)
 
 
 def spread_body(states, ancestors, noise, pair, token_mask, w_qkv, w_out, w_pair):
     particles, rows, width = states.shape
-    heads = w_pair.shape[2]
+    layer_count, channels, heads = w_pair.shape
     scale = (width // heads) ** (-0.5)
     swap = [(0, 1), (1, 0)]
     mask_row = token_mask.reshape(1, -1)
     other_states = lax.ppermute(states, "dom", swap)
+    other_noise = lax.ppermute(noise, "dom", swap)
+    other_ancestors = lax.ppermute(ancestors, "dom", swap)
     bias, own, local_noise = prepare(
-        pair, mask_row, w_pair.transpose(0, 2, 1), states, noise, w_qkv
+        pair, mask_row, w_pair.transpose(0, 2, 1).reshape(layer_count * heads, channels),
+        states, noise, w_qkv,
     )
-    packed = pack(ancestors, own, other_states, local_noise, bias)
-    received = lax.all_to_all(packed, "tok", 0, 0, tiled=True)
-    other = lax.ppermute(received, "dom", swap)
-    state = first_half(mask_row, received, w_qkv, rows, heads, scale)
-    result = layers(mask_row, *state, received, other, w_qkv, w_out, rows, heads, scale)
+    kept, beside, *sent = pack(
+        ancestors, other_ancestors, own, other_states, local_noise, other_noise, bias
+    )
+    beside = lax.ppermute(beside, "tok", [(t, t ^ 1) for t in range(particles)])
+    blocks = []
+    for k, block in reversed(list(zip(range(2, particles, 2), sent))):
+        brought = lax.ppermute(
+            block, ("tok", "dom"),
+            [(2 * t + d, 2 * (t ^ (k + d)) + d) for t in range(particles) for d in range(2)],
+        )
+        if not blocks:
+            brought, beside = lax.optimization_barrier((brought, beside))
+        blocks = [brought, lax.ppermute(brought, "dom", swap)] + blocks
+    blocks = [kept, beside] + blocks
+    state = first_project(blocks, w_qkv, rows, bias.shape[0], scale)
+    result = layers(mask_row, *state, blocks, w_qkv, w_out, heads, scale)
     return lax.all_to_all(result, "tok", 0, 0, tiled=True)
 
 
@@ -368,8 +383,10 @@
         particles, rows, width = states.shape
         fits = (
             particles == mesh.shape["tok"]
+            and particles & (particles - 1) == 0
+            and particles > 2
             and mesh.shape["dom"] == 2
-            and width % (2 * LANES) == 0
+            and width % LANES == 0
             and pair.shape[1] == LANES
             and pair.shape[2] == LANES
             and rows % 16 == 0

time: 47 us -> 44 us (0.936)
  blocking collectives: 37.8 us -> 12.7 us
  waiting for transfers between devices: 0.71 us -> 13.1 us
  starting transfers between devices: 0.52 us -> 10.1 us
    all_to_all x1 -> x0, blocking collectives: 26.1 us -> none  [spread_body(): received = lax.all_to_all(packed, 'tok', 0, 0, tiled=True)]
    ppermute x1 -> x9, waiting for transfers between devices: 0.7 us -> 13.1 us  [the longest x1 7.66 us: spread_body(): beside = lax.ppermute(beside, 'tok', [(t, t ^ 1) for t in range(particles)])]
    ppermute x1 -> x9, starting transfers between devices: 0.01 us -> 9.68 us  [the longest x3 5.22 us: spread_body(): lax.ppermute(block, ('tok', 'dom'), [(2 * t + d, 2 * (t ^ k + d) + d) for...]
    all_to_all x1, blocking collectives: 11.7 us -> 12.7 us  [spread_body(): return lax.all_to_all(result, 'tok', 0, 0, tiled=True)]
  transfers between devices with their start and end apart: 2 -> 10, of which waited for: 1 -> 3; matrix products, arithmetic and copies ran while one was open for 0% -> 0% of each run, Pallas kernels for 7% -> 5%
where the time goes in v4:
time: 44 us; the launch traced here: 43.8 us
  waiting for transfers between devices  13.1 us (30%)
  blocking collectives  12.7 us (29%)
  starting transfers between devices  10.1 us (23%)
  Pallas kernels  7.2 us (16%)
  local copies, waits for them, and re-layouts  0.69 us (2%)
    all_to_all x1, blocking collectives, spread_body(): return lax.all_to_all(result, 'tok', 0, 0, tiled=True)  12.7 us
    ppermute x1, waiting for transfers between devices, spread_body(): beside = lax.ppermute(beside, 'tok', [(t, t ^ 1) for t in range(particles)])  7.66 us
    ppermute x3, starting transfers between devices, spread_body(): lax.ppermute(block, ('tok', 'dom'), [(2 * t + d, 2 * (t ^ k + d) + d) for...  5.22 us
    ppermute x3, waiting for transfers between devices, spread_body(): lax.ppermute(block, ('tok', 'dom'), [(2 * t + d, 2 * (t ^ k + d) + d) for...  4.34 us
    pallas_call x1, Pallas kernels, layers(): pl.pallas_call(kernel, out_shape=jax.ShapeDtypeStruct((sources, rows, wid...  3.41 us
    ppermute x3, starting transfers between devices, spread_body(): blocks = [brought, lax.ppermute(brought, 'dom', swap)] + blocks  2.28 us
    pallas_call x1, Pallas kernels, prepare(): pl.pallas_call(kernel, out_shape=(jax.ShapeDtypeStruct((blocks * rows, ke...  2.03 us
    ppermute x1, starting transfers between devices, spread_body(): beside = lax.ppermute(beside, 'tok', [(t, t ^ 1) for t in range(particles)])  1.66 us
  transfers between devices with their start and end apart: 10, of which 3 were waited for; matrix products, arithmetic and copies ran while one was open for 0% of the time, Pallas kernels for 5%

profile of v4, /device:TPU:0, one launch (start us, length us, event | category | flops | bytes accessed | tf_op | source)
XLA Modules:
  0.0 43.8 jit_solution(11098824916857874458)
XLA Ops:
  0.0 0.0 copy-start.3
  0.0 0.0 copy-start
  0.0 0.5 %collective-permute-start.1 = (bf16[8,16,768]{2,1,0:T(8,128)(2,1)}, bf16[8,16,768]{2,1,0:T(8,128)(2,1)S(1)}, u32[]{:S(2)}, u32[]{:S(2)}) collective-permute-start(bf16[8,16,768]{2,1,0:T(8,128)(2,1)} %own_hbm.1), channel_id=1, source_target_pairs={{0,1},{1,0},{2,3},{3,2},{4,5},{5,4},{6,7},{7,6},{8,9},{9,8},{10,11... | collective-permute-start | bytes 589832 | tf_op jit(solution)/shard_map/ppermute | solution.py:344
  0.5 0.1 collective-permute-start.2
  0.5 0.4 collective-permute-start
  1.0 0.0 copy-start.1
  1.0 0.0 copy-start.2
  1.0 2.0 %prepare.1 = (bf16[512,128]{1,0:T(8,128)(2,1)S(1)}, bf16[8,16,768]{2,1,0:T(8,128)(2,1)S(1)}, bf16[8,16,768]{2,1,0:T(8,128)(2,1)S(1)}) custom-call(bf16[16,128,128]{2,1,0:T(8,128)(2,1)} %pair_hbm.1, s32[1,128]{1,0:T(1,128)} %bitcast.4, bf16[32,128]{1,0:T(8,128)(2,1)} %bitcast.6, bf16[8,16,768]{2,1,0:T(8,128)(2,1)} %own_hbm.1, bf16[8,16,768]{2,1,0:T(8,128)(2,1)} %noise_hbm.1, ...), custom_call_target="tpu_custom_call" | custom-call | flops 16777216 | bytes 8000000 | tf_op jit(solution)/shard_map/prepare/pallas_call | solution.py:112
  3.0 0.0 collective-permute-done.far_anc_ref
  3.0 0.0 collective-permute-done.1.other_ref
  3.0 0.0 collective-permute-done.2.far_noise_ref
  3.0 0.0 copy-done.3
  3.1 0.7 %pack.1 = (bf16[608,128]{1,0:T(8,128)(2,1)S(1)}, bf16[608,128]{1,0:T(8,128)(2,1)S(1)}, bf16[704,128]{1,0:T(8,128)(2,1)S(1)}, bf16[704,128]{1,0:T(8,128)(2,1)S(1)}, bf16[704,128]{1,0:T(8,128)(2,1)S(1)}) custom-call(s32[8]{0:T(128)S(1)} %copy-done.3, s32[8]{0:T(128)S(1)} %collective-permute-done.far_anc_ref, ...), custom_call_target="tpu_custom_call" | custom-call | tf_op jit(solution)/shard_map/pack/pallas_call | solution.py:170
  3.7 4.6 %collective-permute-start.3 = (bf16[704,128]{1,0:T(8,128)(2,1)S(1)}, bf16[704,128]{1,0:T(8,128)(2,1)S(1)}, u32[]{:S(2)}, u32[]{:S(2)}) collective-permute-start(bf16[704,128]{1,0:T(8,128)(2,1)S(1)} %get-tuple-element.23), channel_id=1, source_target_pairs={{0,12},{1,15},{2,14},{3,13},{4,8},{5,11},{6,10},{7,9},{8,4},{9,7},... | collective-permute-start | bytes 540680 | tf_op jit(solution)/shard_map/ppermute | solution.py:357
  8.3 0.0 collective-permute-start.5
  8.3 0.6 %collective-permute-start.7 = (bf16[704,128]{1,0:T(8,128)(2,1)S(1)}, bf16[704,128]{1,0:T(8,128)(2,1)S(1)}, u32[]{:S(2)}, u32[]{:S(2)}) collective-permute-start(bf16[704,128]{1,0:T(8,128)(2,1)S(1)} %get-tuple-element.27), channel_id=1, source_target_pairs={{0,8},{1,11},{2,10},{3,9},{4,12},{5,15},{6,14},{7,13},{8,0},{9,3},... | collective-permute-start | bytes 540680 | tf_op jit(solution)/shard_map/ppermute | solution.py:357
  9.0 1.7 %collective-permute-start.4 = (bf16[608,128]{1,0:T(8,128)(2,1)S(1)}, bf16[608,128]{1,0:T(8,128)(2,1)S(1)}, u32[]{:S(2)}, u32[]{:S(2)}) collective-permute-start(bf16[608,128]{1,0:T(8,128)(2,1)S(1)} %get-tuple-element.24), channel_id=1, source_target_pairs={{0,2},{2,0},{4,6},{6,4},{8,10},{10,8},{12,14},{14,12},{1,3},{3,1},... | collective-permute-start | bytes 466952 | tf_op jit(solution)/shard_map/ppermute | solution.py:354
  10.6 7.7 %collective-permute-done.4.refs_1_ = bf16[608,128]{1,0:T(8,128)(2,1)S(1)} collective-permute-done((bf16[608,128]{1,0:T(8,128)(2,1)S(1)}, bf16[608,128]{1,0:T(8,128)(2,1)S(1)}, u32[]{:S(2)}, u32[]{:S(2)}) %collective-permute-start.4) | collective-permute-done | bytes 155680 | tf_op jit(solution)/shard_map/ppermute | solution.py:354
  18.3 0.0 collective-permute-done.3.refs_6_
  18.3 1.0 %collective-permute-start.9 = (bf16[704,128]{1,0:T(8,128)(2,1)S(1)}, bf16[704,128]{1,0:T(8,128)(2,1)S(1)}, u32[]{:S(2)}, u32[]{:S(2)}) collective-permute-start(bf16[704,128]{1,0:T(8,128)(2,1)S(1)} %collective-permute-done.3.refs_6_), channel_id=1, source_target_pairs={{0,1},{1,0},{2,3},{3,2},{4,5},{5,4},{6,7},{7,6},{8,9},{9,8},{10,11... | collective-permute-start | bytes 540680 | tf_op jit(solution)/shard_map/ppermute | solution.py:363
  19.3 0.0 collective-permute-done.5.refs_2_
  19.3 0.5 %collective-permute-start.6 = (bf16[704,128]{1,0:T(8,128)(2,1)S(1)}, bf16[704,128]{1,0:T(8,128)(2,1)S(1)}, u32[]{:S(2)}, u32[]{:S(2)}) collective-permute-start(bf16[704,128]{1,0:T(8,128)(2,1)S(1)} %collective-permute-done.5.refs_2_), channel_id=1, source_target_pairs={{0,1},{1,0},{2,3},{3,2},{4,5},{5,4},{6,7},{7,6},{8,9},{9,8},{10,11... | collective-permute-start | bytes 540680 | tf_op jit(solution)/shard_map/ppermute | solution.py:363
  19.8 4.3 %collective-permute-done.7.refs_4_ = bf16[704,128]{1,0:T(8,128)(2,1)S(1)} collective-permute-done((bf16[704,128]{1,0:T(8,128)(2,1)S(1)}, bf16[704,128]{1,0:T(8,128)(2,1)S(1)}, u32[]{:S(2)}, u32[]{:S(2)}) %collective-permute-start.7) | collective-permute-done | bytes 180256 | tf_op jit(solution)/shard_map/ppermute | solution.py:357
  24.1 0.8 %collective-permute-start.8 = (bf16[704,128]{1,0:T(8,128)(2,1)S(1)}, bf16[704,128]{1,0:T(8,128)(2,1)S(1)}, u32[]{:S(2)}, u32[]{:S(2)}) collective-permute-start(bf16[704,128]{1,0:T(8,128)(2,1)S(1)} %collective-permute-done.7.refs_4_), channel_id=1, source_target_pairs={{0,1},{1,0},{2,3},{3,2},{4,5},{5,4},{6,7},{7,6},{8,9},{9,8},{10,11... | collective-permute-start | bytes 540680 | tf_op jit(solution)/shard_map/ppermute | solution.py:363
  24.9 0.0 collective-permute-done.9.refs_7_
  24.9 0.0 collective-permute-done.6.refs_3_
  24.9 1.0 %collective-permute-done.8.refs_5_ = bf16[704,128]{1,0:T(8,128)(2,1)S(1)} collective-permute-done((bf16[704,128]{1,0:T(8,128)(2,1)S(1)}, bf16[704,128]{1,0:T(8,128)(2,1)S(1)}, u32[]{:S(2)}, u32[]{:S(2)}) %collective-permute-start.8) | collective-permute-done | bytes 180256 | tf_op jit(solution)/shard_map/ppermute | solution.py:363
  26.0 0.0 copy-done
  26.0 1.1 %first_project.1 = (bf16[128,768]{1,0:T(8,128)(2,1)S(1)}, bf16[128,768]{1,0:T(8,128)(2,1)S(1)}, bf16[128,768]{1,0:T(8,128)(2,1)S(1)}, bf16[768,128]{1,0:T(8,128)(2,1)S(1)}) custom-call(bf16[2,768,2304]{2,1,0:T(8,128)(2,1)S(1)} %copy-done, bf16[608,128]{1,0:T(8,128)(2,1)S(1)} %get-tuple-element.22.refs_0_, ...), custom_call_target="tpu_custom_call" | custom-call | flops 452984832 | bytes 4718592 | tf_op jit(solution)/shard_map/first_project/pallas_call | solution.py:275
  27.0 0.0 copy-done.1
  27.1 0.0 copy-done.2
  27.1 3.4 %layers.1 = bf16[8,16,768]{2,1,0:T(8,128)(2,1)S(1)} custom-call(s32[1,128]{1,0:T(1,128)S(1)} %bitcast.5, bf16[128,768]{1,0:T(8,128)(2,1)S(1)} %get-tuple-element.29.x_ref, bf16[128,768]{1,0:T(8,128)(2,1)S(1)} %get-tuple-element.30.q_in, bf16[128,768]{1,0:T(8,128)(2,1)S(1)} %get-tuple-element.31.k_in, bf16[768,128]{1,0:T(8,128)(2,1)S(1)} %get-tuple-element.32.vt_in, ...), custom_call_target="tpu_custom_call" | custom-call | flops 1056964608 | bytes 5898240 | tf_op jit(solution)/shard_map/layers/pallas_call | solution.py:323
  30.5 12.7 %all_to_all.5 = bf16[8,16,768]{2,1,0:T(8,128)(2,1)S(1)} all-to-all(bf16[8,16,768]{2,1,0:T(8,128)(2,1)S(1)} %layers.1), channel_id=1, replica_groups=mesh['groups'=2,'tok'=8,'dom'=2] {'tok'}, dimensions={0} | all-to-all | bytes 393216 | tf_op jit(solution)/shard_map/all_to_all | solution.py:367
  43.2 0.7 %copy.10 = bf16[8,16,768]{2,1,0:T(8,128)(2,1)} copy(bf16[8,16,768]{2,1,0:T(8,128)(2,1)S(1)} %all_to_all.5) | data formatting | bytes 393216
Async XLA Ops:
  0.0 3.0 %copy-start.3 = (s32[8]{0:T(128)S(1)}, s32[8]{0:T(128)}, u32[]{:S(2)}) copy-start(s32[8]{0:T(128)} %anc_ref.1) | copy-start | bytes 100
  0.0 26.0 %copy-start = (bf16[2,768,2304]{2,1,0:T(8,128)(2,1)S(1)}, bf16[2,768,2304]{2,1,0:T(8,128)(2,1)}, u32[]{:S(2)}) copy-start(bf16[2,768,2304]{2,1,0:T(8,128)(2,1)} %wq_ref.1) | copy-start | bytes 21233668
  0.0 3.0 %collective-permute-start.1 = (bf16[8,16,768]{2,1,0:T(8,128)(2,1)}, bf16[8,16,768]{2,1,0:T(8,128)(2,1)S(1)}, u32[]{:S(2)}, u32[]{:S(2)}) collective-permute-start(bf16[8,16,768]{2,1,0:T(8,128)(2,1)} %own_hbm.1), channel_id=1, source_target_pairs={{0,1},{1,0},{2,3},{3,2},{4,5},{5,4},{6,7},{7,6},{8,9},{9,8},{10,11... | collective-permute-start | bytes 589832 | tf_op jit(solution)/shard_map/ppermute | solution.py:344
  0.5 2.6 %collective-permute-start.2 = (bf16[8,16,768]{2,1,0:T(8,128)(2,1)}, bf16[8,16,768]{2,1,0:T(8,128)(2,1)S(1)}, u32[]{:S(2)}, u32[]{:S(2)}) collective-permute-start(bf16[8,16,768]{2,1,0:T(8,128)(2,1)} %noise_hbm.1), channel_id=1, source_target_pairs={{0,1},{1,0},{2,3},{3,2},{4,5},{5,4},{6,7},{7,6},{8,9},{9,8},{10,11... | collective-permute-start | bytes 589832 | tf_op jit(solution)/shard_map/ppermute | solution.py:345
  0.5 2.5 %collective-permute-start = (s32[8]{0:T(128)}, s32[8]{0:T(128)S(1)}, u32[]{:S(2)}, u32[]{:S(2)}) collective-permute-start(s32[8]{0:T(128)} %anc_ref.1), channel_id=1, source_target_pairs={{0,1},{1,0},{2,3},{3,2},{4,5},{5,4},{6,7},{7,6},{8,9},{9,8},{10,11... | collective-permute-start | bytes 104 | tf_op jit(solution)/shard_map/ppermute | solution.py:346
  1.0 26.1 %copy-start.1 = (bf16[2,768,768]{2,1,0:T(8,128)(2,1)S(1)}, bf16[2,768,768]{2,1,0:T(8,128)(2,1)}, u32[]{:S(2)}) copy-start(bf16[2,768,768]{2,1,0:T(8,128)(2,1)} %wo_ref.1) | copy-start | bytes 7077892
  1.0 26.1 %copy-start.2 = (s32[128]{0:T(128)S(1)}, s32[128]{0:T(128)}, u32[]{:S(2)}) copy-start(s32[128]{0:T(128)} %param.12) | copy-start | bytes 1540
  3.7 14.6 %collective-permute-start.3 = (bf16[704,128]{1,0:T(8,128)(2,1)S(1)}, bf16[704,128]{1,0:T(8,128)(2,1)S(1)}, u32[]{:S(2)}, u32[]{:S(2)}) collective-permute-start(bf16[704,128]{1,0:T(8,128)(2,1)S(1)} %get-tuple-element.23), channel_id=1, source_target_pairs={{0,12},{1,15},{2,14},{3,13},{4,8},{5,11},{6,10},{7,9},{8,4},{9,7},... | collective-permute-start | bytes 540680 | tf_op jit(solution)/shard_map/ppermute | solution.py:357
  8.3 11.0 %collective-permute-start.5 = (bf16[704,128]{1,0:T(8,128)(2,1)S(1)}, bf16[704,128]{1,0:T(8,128)(2,1)S(1)}, u32[]{:S(2)}, u32[]{:S(2)}) collective-permute-start(bf16[704,128]{1,0:T(8,128)(2,1)S(1)} %get-tuple-element.26), channel_id=1, source_target_pairs={{0,4},{1,7},{2,6},{3,5},{4,0},{5,3},{6,2},{7,1},{8,12},{9,15},{10,... | collective-permute-start | bytes 540680 | tf_op jit(solution)/shard_map/ppermute | solution.py:357
  8.3 15.8 %collective-permute-start.7 = (bf16[704,128]{1,0:T(8,128)(2,1)S(1)}, bf16[704,128]{1,0:T(8,128)(2,1)S(1)}, u32[]{:S(2)}, u32[]{:S(2)}) collective-permute-start(bf16[704,128]{1,0:T(8,128)(2,1)S(1)} %get-tuple-element.27), channel_id=1, source_target_pairs={{0,8},{1,11},{2,10},{3,9},{4,12},{5,15},{6,14},{7,13},{8,0},{9,3},... | collective-permute-start | bytes 540680 | tf_op jit(solution)/shard_map/ppermute | solution.py:357
  9.0 9.3 %collective-permute-start.4 = (bf16[608,128]{1,0:T(8,128)(2,1)S(1)}, bf16[608,128]{1,0:T(8,128)(2,1)S(1)}, u32[]{:S(2)}, u32[]{:S(2)}) collective-permute-start(bf16[608,128]{1,0:T(8,128)(2,1)S(1)} %get-tuple-element.24), channel_id=1, source_target_pairs={{0,2},{2,0},{4,6},{6,4},{8,10},{10,8},{12,14},{14,12},{1,3},{3,1},... | collective-permute-start | bytes 466952 | tf_op jit(solution)/shard_map/ppermute | solution.py:354
  18.3 6.6 %collective-permute-start.9 = (bf16[704,128]{1,0:T(8,128)(2,1)S(1)}, bf16[704,128]{1,0:T(8,128)(2,1)S(1)}, u32[]{:S(2)}, u32[]{:S(2)}) collective-permute-start(bf16[704,128]{1,0:T(8,128)(2,1)S(1)} %collective-permute-done.3.refs_6_), channel_id=1, source_target_pairs={{0,1},{1,0},{2,3},{3,2},{4,5},{5,4},{6,7},{7,6},{8,9},{9,8},{10,11... | collective-permute-start | bytes 540680 | tf_op jit(solution)/shard_map/ppermute | solution.py:363
  19.3 5.6 %collective-permute-start.6 = (bf16[704,128]{1,0:T(8,128)(2,1)S(1)}, bf16[704,128]{1,0:T(8,128)(2,1)S(1)}, u32[]{:S(2)}, u32[]{:S(2)}) collective-permute-start(bf16[704,128]{1,0:T(8,128)(2,1)S(1)} %collective-permute-done.5.refs_2_), channel_id=1, source_target_pairs={{0,1},{1,0},{2,3},{3,2},{4,5},{5,4},{6,7},{7,6},{8,9},{9,8},{10,11... | collective-permute-start | bytes 540680 | tf_op jit(solution)/shard_map/ppermute | solution.py:363
  24.1 1.8 %collective-permute-start.8 = (bf16[704,128]{1,0:T(8,128)(2,1)S(1)}, bf16[704,128]{1,0:T(8,128)(2,1)S(1)}, u32[]{:S(2)}, u32[]{:S(2)}) collective-permute-start(bf16[704,128]{1,0:T(8,128)(2,1)S(1)} %collective-permute-done.7.refs_4_), channel_id=1, source_target_pairs={{0,1},{1,0},{2,3},{3,2},{4,5},{5,4},{6,7},{7,6},{8,9},{9,8},{10,11... | collective-permute-start | bytes 540680 | tf_op jit(solution)/shard_map/ppermute | solution.py:363

commit v5 on v3

--- a/solution.py
+++ b/solution.py
@@ -84,11 +84,11 @@
     rows, keys, channels = pair.shape
     layer_count, heads, _ = w_rows.shape
     half = heads // 2
-    blocks = layer_count * half
+    blocks = layer_count * heads
 
     def kernel(
         pair_hbm, mask_hbm, w_hbm, own_hbm, noise_hbm, wq_hbm,
-        bias_ref, own_ref, noise_ref, pair_ref, mask_ref, w_ref, rows_ref, sem,
+        near_ref, far_ref, own_ref, noise_ref, pair_ref, mask_ref, w_ref, rows_ref, sem,
     ):
         copies = [
             pltpu.make_async_copy(mask_hbm, mask_ref, sem.at[0]),
@@ -102,32 +102,32 @@
         copies[0].wait()
         copies[1].wait()
         penalty = jnp.where(mask_ref[...] > 0, 0.0, MASKED).astype(jnp.float32)
-        is_first = lax.axis_index("dom") == 0
-        sent = jnp.concatenate(
-            [
-                jnp.where(is_first, w[:half], w[half:])
-                for w in (w_ref[l].astype(jnp.float32) for l in range(layer_count))
-            ],
-            axis=0,
-        ).astype(jnp.bfloat16)
+        w_all = w_ref[...].reshape(blocks, channels)
         copies[2].wait()
         for i in range(rows):
-            piece = across(sent, pair_ref[i]) + penalty
+            piece = across(w_all, pair_ref[i]) + penalty
             rows_ref[:, i, :] = piece - jnp.max(piece, axis=-1, keepdims=True)
-        for h in range(blocks):
-            bias_ref[h * rows : (h + 1) * rows, :] = rows_ref[h].astype(jnp.bfloat16)
+        dom = lax.axis_index("dom")
+        for l in range(layer_count):
+            for h in range(half):
+                at = (l * half + h) * rows
+                near = l * heads + dom * half + h
+                far = l * heads + (1 - dom) * half + h
+                near_ref[at : at + rows, :] = rows_ref[near].astype(jnp.bfloat16)
+                far_ref[at : at + rows, :] = rows_ref[far].astype(jnp.bfloat16)
         for copy in copies[3:]:
             copy.wait()
 
+    part = jax.ShapeDtypeStruct((blocks // 2 * rows, keys), jnp.bfloat16)
     return pl.pallas_call(
         kernel,
         out_shape=(
-            jax.ShapeDtypeStruct((blocks * rows, keys), jnp.bfloat16),
+            part, part,
             jax.ShapeDtypeStruct(own.shape, own.dtype),
             jax.ShapeDtypeStruct(noise.shape, noise.dtype),
         ),
         in_specs=[in_hbm()] * 6,
-        out_specs=(whole_vmem(),) * 3,
+        out_specs=(whole_vmem(),) * 4,
         scratch_shapes=[
             pltpu.VMEM(pair.shape, pair.dtype),
             pltpu.VMEM(mask_row.shape, mask_row.dtype),
@@ -143,28 +143,44 @@
     )(*(stay(a) for a in (pair, mask_row, w_rows, own, noise, w_qkv)))
 
 
+def block_source(position):
+    return jnp.bitwise_xor(lax.axis_index("tok"), position)
+
+
 def pack(ancestors, own, other, noise, bias):
     particles, rows, width = own.shape
     used = rows * (width // LANES)
-
-    def kernel(anc_ref, own_ref, other_ref, noise_ref, bias_ref, out_ref):
+    total = bias.shape[0]
+    served = [0, 1] + list(range(2, particles, 2))
+
+    def kernel(anc_ref, own_ref, other_ref, noise_ref, bias_ref, *outs):
         dom = lax.axis_index("dom")
-        for p in range(particles):
-            a = anc_ref[p]
-            local = lax.rem(a, particles)
-            mine = lax.div(a, particles) == dom
+
+        def put(out_ref, first, particle):
+            ancestor = anc_ref[particle]
+            local = lax.rem(ancestor, particles)
+            mine = lax.div(ancestor, particles) == dom
             value = jnp.where(mine, own_ref[local], other_ref[local])
-            value = value.astype(jnp.float32) + 0.5 * noise_ref[p].astype(jnp.float32)
+            value = value.astype(jnp.float32) + 0.5 * noise_ref[particle].astype(jnp.float32)
             value = value.astype(jnp.bfloat16)
             for k in range(width // LANES):
-                out_ref[p, k * rows : (k + 1) * rows, :] = value[:, k * LANES : (k + 1) * LANES]
-            out_ref[p, used:, :] = bias_ref[...]
-
+                out_ref[first + k * rows : first + (k + 1) * rows, :] = value[
+                    :, k * LANES : (k + 1) * LANES
+                ]
+
+        for position, out_ref in zip(served, outs):
+            put(out_ref, 0, block_source(position))
+            if position > 0:
+                out_ref[used : used + total, :] = bias_ref[...]
+            if position > 1:
+                put(out_ref, used + total, block_source(position + 1))
+
+    lengths = [used, used + total] + [total + 2 * used] * (len(served) - 2)
     return pl.pallas_call(
         kernel,
-        out_shape=jax.ShapeDtypeStruct((particles, used + bias.shape[0], LANES), jnp.bfloat16),
+        out_shape=tuple(jax.ShapeDtypeStruct((length, LANES), own.dtype) for length in lengths),
         in_specs=[in_smem()] + [whole_vmem()] * 4,
-        out_specs=whole_vmem(),
+        out_specs=(whole_vmem(),) * len(served),
         compiler_params=pltpu.CompilerParams(vmem_limit_bytes=6 * 2**20),
         name="pack",
     )(ancestors, own, other, noise, bias)
@@ -182,10 +198,14 @@
     return jnp.where(down == along, 1.0, 0.0).astype(jnp.bfloat16)
 
 
-def project(stream, w_ref, q_ref, k_ref, vt_ref, eye, scale):
-    width = stream.shape[1]
+def block_rows(position, rows):
+    return pl.ds(pl.multiple_of(block_source(position) * rows, rows), rows)
+
+
+def project(stream, w_ref, q_ref, k_ref, vt_ref, n_ref, eye, scale, rows):
+    tokens, width = stream.shape
     normed = layer_norm(stream).astype(jnp.bfloat16)
-    q_ref[...] = (
+    n_ref[...] = (
         jnp.dot(normed, w_ref[:, :width], preferred_element_type=jnp.float32) * scale
     ).astype(jnp.bfloat16)
     k_ref[...] = jnp.dot(
@@ -196,14 +216,15 @@
     ).astype(jnp.bfloat16)
     for t in range(0, width, LANES):
         vt_ref[t : t + LANES, :] = across(eye, values[:, t : t + LANES]).astype(jnp.bfloat16)
-
-
-def attend(groups, first_row, rows, head_width, q_ref, k_ref, vt_ref, at_ref, work, eye, floor):
+    for p in range(tokens // rows):
+        q_ref[p * rows : (p + 1) * rows, :] = n_ref[block_rows(p, rows), :]
+
+
+def attend(groups, layer, ahead, rows, head_width, q_ref, k_ref, vt_ref, at_ref, work, eye, floor):
     s_buf, e_buf, n_buf = work
-    tokens = eye.shape[0]
     half = q_ref.shape[1] // head_width // 2
-    every = [(g * half + h, h, base, bias) for g, (base, bias) in enumerate(groups) for h in range(half)]
-    for slot, h, base, bias_ref in every:
+    every = [(g * half + h, h, *group) for g, group in enumerate(groups) for h in range(half)]
+    for slot, h, base, blocks in every:
         low = h * head_width
         high = low + head_width
         start = low // LANES * LANES
@@ -211,18 +232,20 @@
         lane = lax.broadcasted_iota(jnp.int32, (1, stop - start), 1) + start
         inside = jnp.where((lane >= low) & (lane < high), 1.0, 0.0).astype(jnp.bfloat16)
         cols = pl.ds(pl.multiple_of(base + start, LANES), stop - start)
-        at = first_row + h * rows
-        bias = bias_ref[:, at : at + rows, :].reshape(tokens, tokens)
+        firsts = [(layer * half + h) * rows + (0 if p == 0 else ahead) for p in range(len(blocks))]
+        bias = jnp.concatenate(
+            [block[at : at + rows, :] for at, block in zip(firsts, blocks)], axis=0
+        )
         s_buf[slot] = across(
             jnp.concatenate([k_ref[:, cols], eye], axis=1),
             jnp.concatenate([q_ref[:, cols] * inside, bias], axis=1),
         )
-    for slot, h, base, bias_ref in every:
+    for slot, h, base, blocks in every:
         scores = s_buf[slot] + floor
         raised = jnp.exp(scores - jnp.max(scores, axis=0, keepdims=True))
         n_buf[slot : slot + 1, :] = 1.0 / jnp.sum(raised, axis=0, keepdims=True)
         e_buf[slot] = raised.astype(jnp.bfloat16)
-    for slot, h, base, bias_ref in every:
+    for slot, h, base, blocks in every:
         own = pl.ds(pl.multiple_of(base + h * head_width, 16), head_width)
         out = jnp.dot(vt_ref[own, :], e_buf[slot], preferred_element_type=jnp.float32)
         at_ref[own, :] = (out * n_buf[slot : slot + 1, :]).astype(jnp.bfloat16)
@@ -241,23 +264,27 @@
     ]
 
 
-def first_half(mask, received, w_qkv, rows, heads, scale):
-    sources = received.shape[0]
+def first_half(mask, kept, near, blocks, w_qkv, rows, heads, scale):
+    sources = 1 + len(blocks)
+    width = w_qkv.shape[1]
     tokens = sources * rows
-    width = w_qkv.shape[1]
-    stream_rows = rows * (width // LANES)
-
-    def kernel(mask_ref, recv_ref, w_ref, x_ref, q_ref, k_ref, vt_ref, at_ref, *work):
-        for s in range(sources):
+    used = rows * (width // LANES)
+    total = near.shape[0]
+
+    def kernel(mask_ref, w_ref, kept_ref, near_ref, *refs):
+        block_refs, refs = refs[: len(blocks)], refs[len(blocks) :]
+        x_ref, q_ref, k_ref, vt_ref, at_ref, n_ref, *work = refs
+        for p, block in enumerate((kept_ref, *block_refs)):
+            at = used + total if p % 2 == 1 and p > 1 else 0
             for k in range(width // LANES):
-                x_ref[s * rows : (s + 1) * rows, k * LANES : (k + 1) * LANES] = recv_ref[
-                    s, k * rows : (k + 1) * rows, :
+                x_ref[block_rows(p, rows), k * LANES : (k + 1) * LANES] = block[
+                    at + k * rows : at + (k + 1) * rows, :
                 ]
         eye = identity(tokens)
-        project(x_ref[...], w_ref.at[0], q_ref, k_ref, vt_ref, eye, scale)
-        near = lax.axis_index("dom") * (width // 2)
+        project(x_ref[...], w_ref.at[0], q_ref, k_ref, vt_ref, n_ref, eye, scale, rows)
+        here = lax.axis_index("dom") * (width // 2)
         attend(
-            [(near, recv_ref)], stream_rows, rows, width // heads,
+            [(here, (near_ref, *block_refs))], 0, used, rows, width // heads,
             q_ref, k_ref, vt_ref, at_ref, work, eye, row_floor(mask_ref),
         )
 
@@ -266,51 +293,51 @@
     return pl.pallas_call(
         kernel,
         out_shape=(wide, wide, wide, tall, tall),
-        in_specs=[whole_vmem()] * 3,
+        in_specs=[whole_vmem()] * (4 + len(blocks)),
         out_specs=(whole_vmem(),) * 5,
-        scratch_shapes=work_space(heads // 2, tokens),
+        scratch_shapes=[pltpu.VMEM((tokens, width), jnp.bfloat16)] + work_space(heads // 2, tokens),
         compiler_params=pltpu.CompilerParams(vmem_limit_bytes=8 * 2**20),
         cost_estimate=pl.CostEstimate(
             flops=6 * tokens * width * width, transcendentals=heads * tokens * tokens // 2,
             bytes_accessed=8 * width * width,
         ),
         name="first_half",
-    )(mask, received, w_qkv)
-
-
-def layers(mask, stream, query, keys, values, attended, received, other, w_qkv, w_out, rows, heads, scale):
-    tokens, width = stream.shape
-    layer_count = w_qkv.shape[0]
-    sources = received.shape[0]
-    half = heads // 2
-    stream_rows = rows * (width // LANES)
-
-    def kernel(
-        mask_ref, x_ref, q_in, k_in, vt_in, at_in, recv_ref, other_ref, wq_ref, wo_ref,
-        out_ref, x_buf, q_buf, k_buf, vt_buf, at_buf, *work,
-    ):
-        here = lax.axis_index("dom")
-        near = here * (width // 2)
-        far = (1 - here) * (width // 2)
+    )(mask, w_qkv, kept, near, *blocks)
+
+
+def layers(mask, state, near, far, w_qkv, w_out, rows, heads, scale):
+    sources = len(near)
+    layer_count, width, _ = w_qkv.shape
+    tokens = sources * rows
+    used = rows * (width // LANES)
+
+    def kernel(mask_ref, wq_ref, wo_ref, x_ref, q_in, k_in, vt_in, at_in, *refs):
+        near_refs, far_refs, refs = refs[:sources], refs[sources : 2 * sources], refs[2 * sources :]
+        out_ref, x_buf, q_buf, k_buf, vt_buf, at_buf, n_buf, *work = refs
+        dom = lax.axis_index("dom")
+        here = dom * (width // 2)
+        there = (1 - dom) * (width // 2)
         floor = row_floor(mask_ref)
         eye = identity(tokens)
-        ready = pl.ds(pl.multiple_of(near, LANES), width // 2)
+        ready = pl.ds(pl.multiple_of(here, LANES), width // 2)
         at_buf[ready, :] = at_in[ready, :]
-
         for l in range(layer_count):
             q_ref, k_ref, vt_ref = (q_in, k_in, vt_in) if l == 0 else (q_buf, k_buf, vt_buf)
-            stream_ref = x_ref if l == 0 else x_buf
-            groups = [(far, other_ref)] if l == 0 else [(near, recv_ref), (far, other_ref)]
+            groups = [(there, far_refs)] if l == 0 else [(here, near_refs), (there, far_refs)]
             attend(
-                groups, stream_rows + l * half * rows, rows, width // heads,
-                q_ref, k_ref, vt_ref, at_buf, work, eye, floor,
+                groups, l, used, rows, width // heads, q_ref, k_ref, vt_ref, at_buf, work, eye, floor
             )
             together = across(eye, at_buf[...]).astype(jnp.bfloat16)
-            update = jnp.dot(together, wo_ref[l], preferred_element_type=jnp.float32)
-            moved = (stream_ref[...].astype(jnp.float32) + update).astype(jnp.bfloat16)
+            for p in range(sources):
+                n_buf[block_rows(p, rows), :] = together[p * rows : (p + 1) * rows, :]
+            update = jnp.dot(n_buf[...], wo_ref[l], preferred_element_type=jnp.float32)
+            before = x_ref[...] if l == 0 else x_buf[...]
+            moved = (before.astype(jnp.float32) + update).astype(jnp.bfloat16)
             if l + 1 < layer_count:
                 x_buf[...] = moved
-                project(moved, wq_ref.at[l + 1], q_buf, k_buf, vt_buf, eye, scale)
+                project(
+                    moved, wq_ref.at[l + 1], q_buf, k_buf, vt_buf, n_buf, eye, scale, rows
+                )
             else:
                 for s in range(sources):
                     out_ref[s] = moved[s * rows : (s + 1) * rows, :]
@@ -320,18 +347,16 @@
     return pl.pallas_call(
         kernel,
         out_shape=jax.ShapeDtypeStruct((sources, rows, width), jnp.bfloat16),
-        in_specs=[whole_vmem()] * 10,
+        in_specs=[whole_vmem()] * (8 + 2 * sources),
         out_specs=whole_vmem(),
-        scratch_shapes=[
-            wide, wide, wide, tall, tall,
-        ] + work_space(heads, tokens),
+        scratch_shapes=[wide, wide, wide, tall, tall, wide] + work_space(heads, tokens),
         compiler_params=pltpu.CompilerParams(vmem_limit_bytes=8 * 2**20),
         cost_estimate=pl.CostEstimate(
             flops=14 * tokens * width * width, transcendentals=2 * heads * tokens * tokens,
             bytes_accessed=10 * width * width,
         ),
         name="layers",
-    )(mask, stream, query, keys, values, attended, received, other, w_qkv, w_out)
+    )(mask, w_qkv, w_out, *state, *near, *far)
 
 
 def spread_body(states, ancestors, noise, pair, token_mask, w_qkv, w_out, w_pair):
@@ -340,15 +365,26 @@
     scale = (width // heads) ** (-0.5)
     swap = [(0, 1), (1, 0)]
     mask_row = token_mask.reshape(1, -1)
+
+    def beside(block, k=1):
+        return lax.ppermute(block, "tok", [(t, t ^ k) for t in range(particles)])
+
     other_states = lax.ppermute(states, "dom", swap)
-    bias, own, local_noise = prepare(
+    near, far, own, local_noise = prepare(
         pair, mask_row, w_pair.transpose(0, 2, 1), states, noise, w_qkv
     )
-    packed = pack(ancestors, own, other_states, local_noise, bias)
-    received = lax.all_to_all(packed, "tok", 0, 0, tiled=True)
-    other = lax.ppermute(received, "dom", swap)
-    state = first_half(mask_row, received, w_qkv, rows, heads, scale)
-    result = layers(mask_row, *state, received, other, w_qkv, w_out, rows, heads, scale)
+    kept, neighbour, *sent = pack(ancestors, own, other_states, local_noise, near)
+    blocks = {}
+    for k in range(particles - 2, 0, -2):
+        blocks[k] = beside(sent[k // 2 - 1], k)
+        blocks[k + 1] = beside(blocks[k])
+    blocks[1] = beside(neighbour)
+    blocks = [blocks[p] for p in range(1, particles)]
+    swapped = [lax.ppermute(block, "dom", swap) for block in blocks]
+    state = first_half(mask_row, kept, near, blocks, w_qkv, rows, heads, scale)
+    result = layers(
+        mask_row, state, (near, *blocks), (far, *swapped), w_qkv, w_out, rows, heads, scale
+    )
     return lax.all_to_all(result, "tok", 0, 0, tiled=True)
 
 
@@ -368,8 +404,11 @@
         particles, rows, width = states.shape
         fits = (
             particles == mesh.shape["tok"]
+            and particles & (particles - 1) == 0
+            and particles > 2
             and mesh.shape["dom"] == 2
             and width % (2 * LANES) == 0
+            and w_pair.shape[2] % 2 == 0
             and pair.shape[1] == LANES
             and pair.shape[2] == LANES
             and rows % 16 == 0

time: 47 us -> 42.8 us (0.911)
  blocking collectives: 37.8 us -> 13.4 us
  starting transfers between devices: 0.52 us -> 13.4 us
  waiting for transfers between devices: 0.71 us -> 7.83 us
    all_to_all x1 -> x0, blocking collectives: 26.1 us -> none  [spread_body(): received = lax.all_to_all(packed, 'tok', 0, 0, tiled=True)]
    ppermute x1 -> x14, starting transfers between devices: 0.01 us -> 12.9 us  [the longest x7 12.2 us: beside(): return lax.ppermute(block, 'tok', [(t, t ^ k) for t in range(particles)])]
    ppermute x1 -> x14, waiting for transfers between devices: 0.7 us -> 7.82 us  [the longest x7 6.52 us: beside(): return lax.ppermute(block, 'tok', [(t, t ^ k) for t in range(particles)])]
    all_to_all x1, blocking collectives: 11.7 us -> 13.4 us  [spread_body(): return lax.all_to_all(result, 'tok', 0, 0, tiled=True)]
  transfers between devices with their start and end apart: 2 -> 15, of which waited for: 1 -> 4; matrix products, arithmetic and copies ran while one was open for 0% -> 0% of each run, Pallas kernels for 7% -> 8%
where the time goes in v5:
time: 42.8 us; the launch traced here: 42.6 us
  starting transfers between devices  13.4 us (31%)
  blocking collectives  13.4 us (31%)
  waiting for transfers between devices  7.83 us (18%)
  Pallas kernels  7.2 us (17%)
  local copies, waits for them, and re-layouts  0.69 us (2%)
    all_to_all x1, blocking collectives, spread_body(): return lax.all_to_all(result, 'tok', 0, 0, tiled=True)  13.4 us
    ppermute x7, starting transfers between devices, beside(): return lax.ppermute(block, 'tok', [(t, t ^ k) for t in range(particles)])  12.2 us
    ppermute x7, waiting for transfers between devices, beside(): return lax.ppermute(block, 'tok', [(t, t ^ k) for t in range(particles)])  6.52 us
    pallas_call x1, Pallas kernels, layers(): pl.pallas_call(kernel, out_shape=jax.ShapeDtypeStruct((sources, rows, wid...  3.2 us
    pallas_call x1, Pallas kernels, prepare(): pl.pallas_call(kernel, out_shape=(part, part, jax.ShapeDtypeStruct(own.sh...  1.87 us
    pallas_call x1, Pallas kernels, first_half(): pl.pallas_call(kernel, out_shape=(wide, wide, wide, tall, tall), in_specs...  1.49 us
    ppermute x7, waiting for transfers between devices, spread_body(): swapped = [lax.ppermute(block, 'dom', swap) for block in blocks]  1.3 us
  transfers between devices with their start and end apart: 15, of which 4 were waited for; matrix products, arithmetic and copies ran while one was open for 0% of the time, Pallas kernels for 8%

profile of v5, /device:TPU:0, one launch (start us, length us, event | category | flops | bytes accessed | tf_op | source)
XLA Modules:
  0.0 42.6 jit_solution(2856576119134484832)
XLA Ops:
  0.0 0.0 copy-start
  0.0 0.0 copy-start.2
  0.0 0.0 copy-start.3
  0.0 0.5 %collective-permute-start = (bf16[8,16,768]{2,1,0:T(8,128)(2,1)}, bf16[8,16,768]{2,1,0:T(8,128)(2,1)S(1)}, u32[]{:S(2)}, u32[]{:S(2)}) collective-permute-start(bf16[8,16,768]{2,1,0:T(8,128)(2,1)} %own_hbm.1), channel_id=1, source_target_pairs={{0,1},{1,0},{2,3},{3,2},{4,5},{5,4},{6,7},{7,6},{8,9},{9,8},{10,11... | collective-permute-start | bytes 589832 | tf_op jit(solution)/shard_map/ppermute | solution.py:372
  0.5 0.0 copy-start.1
  0.5 1.9 %prepare.1 = (bf16[256,128]{1,0:T(8,128)(2,1)S(1)}, bf16[256,128]{1,0:T(8,128)(2,1)S(1)}, bf16[8,16,768]{2,1,0:T(8,128)(2,1)S(1)}, bf16[8,16,768]{2,1,0:T(8,128)(2,1)S(1)}) custom-call(bf16[16,128,128]{2,1,0:T(8,128)(2,1)} %pair_hbm.1, s32[1,128]{1,0:T(1,128)} %bitcast.2, bf16[2,16,128]{2,1,0:T(8,128)(2,1)} %bitcast.5, bf16[8,16,768]{2,1,0:T(8,128)(2,1)} %own_hbm.1, ...), custom_call_target="tpu_custom_call" | custom-call | flops 16777216 | bytes 8000000 | tf_op jit(solution)/shard_map/prepare/pallas_call | solution.py:122
  2.4 0.0 collective-permute-done.other_ref
  2.4 0.0 copy-done.3
  2.4 0.6 %pack.1 = (bf16[96,128]{1,0:T(8,128)(2,1)S(1)}, bf16[352,128]{1,0:T(8,128)(2,1)S(1)}, bf16[448,128]{1,0:T(8,128)(2,1)S(1)}, bf16[448,128]{1,0:T(8,128)(2,1)S(1)}, bf16[448,128]{1,0:T(8,128)(2,1)S(1)}) custom-call(s32[8]{0:T(128)S(1)} %copy-done.3, bf16[8,16,768]{2,1,0:T(8,128)(2,1)S(1)} %get-tuple-element.19.own_ref, ...), custom_call_target="tpu_custom_call" | custom-call | tf_op jit(solution)/shard_map/pack/pallas_call | solution.py:179
  3.1 2.6 %collective-permute-start.2 = (bf16[448,128]{1,0:T(8,128)(2,1)S(1)}, bf16[448,128]{1,0:T(8,128)(2,1)S(1)}, u32[]{:S(2)}, u32[]{:S(2)}) collective-permute-start(bf16[448,128]{1,0:T(8,128)(2,1)S(1)} %get-tuple-element.24), channel_id=1, source_target_pairs={{0,4},{2,6},{4,0},{6,2},{8,12},{10,14},{12,8},{14,10},{1,5},{3,7},... | collective-permute-start | bytes 344072 | tf_op jit(solution)/shard_map/ppermute | solution.py:370
  5.6 2.6 %collective-permute-start.4 = (bf16[448,128]{1,0:T(8,128)(2,1)S(1)}, bf16[448,128]{1,0:T(8,128)(2,1)S(1)}, u32[]{:S(2)}, u32[]{:S(2)}) collective-permute-start(bf16[448,128]{1,0:T(8,128)(2,1)S(1)} %get-tuple-element.25), channel_id=1, source_target_pairs={{0,8},{2,10},{4,12},{6,14},{8,0},{10,2},{12,4},{14,6},{1,9},{3,11}... | collective-permute-start | bytes 344072 | tf_op jit(solution)/shard_map/ppermute | solution.py:370
  8.3 0.0 collective-permute-start.6
  8.3 1.7 %collective-permute-start.1 = (bf16[352,128]{1,0:T(8,128)(2,1)S(1)}, bf16[352,128]{1,0:T(8,128)(2,1)S(1)}, u32[]{:S(2)}, u32[]{:S(2)}) collective-permute-start(bf16[352,128]{1,0:T(8,128)(2,1)S(1)} %get-tuple-element.23), channel_id=1, source_target_pairs={{0,2},{2,0},{4,6},{6,4},{8,10},{10,8},{12,14},{14,12},{1,3},{3,1},... | collective-permute-start | bytes 270344 | tf_op jit(solution)/shard_map/ppermute | solution.py:370
  10.0 0.0 collective-permute-done.2.refs_1_.refs_2_
  10.0 0.0 collective-permute-start.9
  10.0 3.3 %collective-permute-start.3 = (bf16[448,128]{1,0:T(8,128)(2,1)S(1)}, bf16[448,128]{1,0:T(8,128)(2,1)S(1)}, u32[]{:S(2)}, u32[]{:S(2)}) collective-permute-start(bf16[448,128]{1,0:T(8,128)(2,1)S(1)} %collective-permute-done.2.refs_1_.refs_2_), channel_id=1, source_target_pairs={{0,2},{2,0},{4,6},{6,4},{8,10},{10,8},{12,14},{14,12},{1,3},{3,1},... | collective-permute-start | bytes 344072 | tf_op jit(solution)/shard_map/ppermute | solution.py:370
  13.3 4.2 %collective-permute-done.4.refs_3_.refs_4_ = bf16[448,128]{1,0:T(8,128)(2,1)S(1)} collective-permute-done((bf16[448,128]{1,0:T(8,128)(2,1)S(1)}, bf16[448,128]{1,0:T(8,128)(2,1)S(1)}, u32[]{:S(2)}, u32[]{:S(2)}) %collective-permute-start.4) | collective-permute-done | bytes 114720 | tf_op jit(solution)/shard_map/ppermute | solution.py:370
  17.5 1.5 %collective-permute-start.5 = (bf16[448,128]{1,0:T(8,128)(2,1)S(1)}, bf16[448,128]{1,0:T(8,128)(2,1)S(1)}, u32[]{:S(2)}, u32[]{:S(2)}) collective-permute-start(bf16[448,128]{1,0:T(8,128)(2,1)S(1)} %collective-permute-done.4.refs_3_.refs_4_), channel_id=1, source_target_pairs={{0,2},{2,0},{4,6},{6,4},{8,10},{10,8},{12,14},{14,12},{1,3},{3,1},... | collective-permute-start | bytes 344072 | tf_op jit(solution)/shard_map/ppermute | solution.py:370
  19.0 0.0 collective-permute-done.6.refs_5_.refs_6_
  19.0 0.5 %collective-permute-start.7 = (bf16[448,128]{1,0:T(8,128)(2,1)S(1)}, bf16[448,128]{1,0:T(8,128)(2,1)S(1)}, u32[]{:S(2)}, u32[]{:S(2)}) collective-permute-start(bf16[448,128]{1,0:T(8,128)(2,1)S(1)} %collective-permute-done.6.refs_5_.refs_6_), channel_id=1, source_target_pairs={{0,2},{2,0},{4,6},{6,4},{8,10},{10,8},{12,14},{14,12},{1,3},{3,1},... | collective-permute-start | bytes 344072 | tf_op jit(solution)/shard_map/ppermute | solution.py:370
  19.5 0.0 collective-permute-done.1.refs_0_.refs_1_
  19.5 0.0 collective-permute-start.8
  19.5 1.3 %collective-permute-done.8.refs_9_ = bf16[352,128]{1,0:T(8,128)(2,1)S(1)} collective-permute-done((bf16[352,128]{1,0:T(8,128)(2,1)S(1)}, bf16[352,128]{1,0:T(8,128)(2,1)S(1)}, u32[]{:S(2)}, u32[]{:S(2)}) %collective-permute-start.8) | collective-permute-done | bytes 90144 | tf_op jit(solution)/shard_map/ppermute | solution.py:383
  20.8 0.2 collective-permute-start.11
  21.0 0.0 collective-permute-done.9.refs_10_
  21.0 0.4 collective-permute-start.13
  21.3 0.0 collective-permute-done.3.refs_2_.refs_3_
  21.3 0.2 collective-permute-start.10
  21.5 0.8 %collective-permute-done.5.refs_4_.refs_5_ = bf16[448,128]{1,0:T(8,128)(2,1)S(1)} collective-permute-done((bf16[448,128]{1,0:T(8,128)(2,1)S(1)}, bf16[448,128]{1,0:T(8,128)(2,1)S(1)}, u32[]{:S(2)}, u32[]{:S(2)}) %collective-permute-start.5) | collective-permute-done | bytes 114720 | tf_op jit(solution)/shard_map/ppermute | solution.py:370
  22.3 0.0 collective-permute-start.12
  22.3 1.5 %collective-permute-done.7.refs_6_.refs_7_ = bf16[448,128]{1,0:T(8,128)(2,1)S(1)} collective-permute-done((bf16[448,128]{1,0:T(8,128)(2,1)S(1)}, bf16[448,128]{1,0:T(8,128)(2,1)S(1)}, u32[]{:S(2)}, u32[]{:S(2)}) %collective-permute-start.7) | collective-permute-done | bytes 114720 | tf_op jit(solution)/shard_map/ppermute | solution.py:370
  23.8 0.0 collective-permute-start.14
  23.8 0.0 copy-done
  23.8 0.0 copy-done.2
  23.8 1.5 %first_half.1 = (bf16[128,768]{1,0:T(8,128)(2,1)S(1)}, bf16[128,768]{1,0:T(8,128)(2,1)S(1)}, bf16[128,768]{1,0:T(8,128)(2,1)S(1)}, bf16[768,128]{1,0:T(8,128)(2,1)S(1)}, bf16[768,128]{1,0:T(8,128)(2,1)S(1)}) custom-call(s32[1,128]{1,0:T(1,128)S(1)} %bitcast.3, bf16[2,768,2304]{2,1,0:T(8,128)(2,1)S(1)} %copy-done, ...), custom_call_target="tpu_custom_call" | custom-call | flops 452984832 | bytes 4718592 | tf_op jit(solution)/shard_map/first_half/pallas_call | solution.py:293
  25.3 0.0 collective-permute-done.11.refs_12_
  25.3 0.0 collective-permute-done.13.refs_14_
  25.3 0.0 collective-permute-done.10.refs_11_
  25.3 0.0 collective-permute-done.12.refs_13_
  25.3 0.0 collective-permute-done.14.refs_15_
  25.4 0.0 copy-done.1
  25.4 3.2 %layers.1 = bf16[8,16,768]{2,1,0:T(8,128)(2,1)S(1)} custom-call(s32[1,128]{1,0:T(1,128)S(1)} %bitcast.4, bf16[2,768,2304]{2,1,0:T(8,128)(2,1)S(1)} %copy-done, bf16[2,768,768]{2,1,0:T(8,128)(2,1)S(1)} %copy-done.1, bf16[128,768]{1,0:T(8,128)(2,1)S(1)} %get-tuple-element.27.x_ref, bf16[128,768]{1,0:T(8,128)(2,1)S(1)} %get-tuple-element.28.q_in, ...), custom_call_target="tpu_custom_call" | custom-call | flops 1056964608 | bytes 5898240 | tf_op jit(solution)/shard_map/layers/pallas_call | solution.py:347
  28.6 13.4 %all_to_all.5 = bf16[8,16,768]{2,1,0:T(8,128)(2,1)S(1)} all-to-all(bf16[8,16,768]{2,1,0:T(8,128)(2,1)S(1)} %layers.1), channel_id=1, replica_groups=mesh['groups'=2,'tok'=8,'dom'=2] {'tok'}, dimensions={0} | all-to-all | bytes 393216 | tf_op jit(solution)/shard_map/all_to_all | solution.py:388
  41.9 0.7 %copy.10 = bf16[8,16,768]{2,1,0:T(8,128)(2,1)} copy(bf16[8,16,768]{2,1,0:T(8,128)(2,1)S(1)} %all_to_all.5) | data formatting | bytes 393216
Async XLA Ops:
  0.0 23.8 %copy-start = (bf16[2,768,2304]{2,1,0:T(8,128)(2,1)S(1)}, bf16[2,768,2304]{2,1,0:T(8,128)(2,1)}, u32[]{:S(2)}) copy-start(bf16[2,768,2304]{2,1,0:T(8,128)(2,1)} %wq_ref.1) | copy-start | bytes 21233668
  0.0 23.8 %copy-start.2 = (s32[128]{0:T(128)S(1)}, s32[128]{0:T(128)}, u32[]{:S(2)}) copy-start(s32[128]{0:T(128)} %param.12) | copy-start | bytes 1540
  0.0 2.4 %copy-start.3 = (s32[8]{0:T(128)S(1)}, s32[8]{0:T(128)}, u32[]{:S(2)}) copy-start(s32[8]{0:T(128)} %anc_ref.1) | copy-start | bytes 100
  0.0 2.4 %collective-permute-start = (bf16[8,16,768]{2,1,0:T(8,128)(2,1)}, bf16[8,16,768]{2,1,0:T(8,128)(2,1)S(1)}, u32[]{:S(2)}, u32[]{:S(2)}) collective-permute-start(bf16[8,16,768]{2,1,0:T(8,128)(2,1)} %own_hbm.1), channel_id=1, source_target_pairs={{0,1},{1,0},{2,3},{3,2},{4,5},{5,4},{6,7},{7,6},{8,9},{9,8},{10,11... | collective-permute-start | bytes 589832 | tf_op jit(solution)/shard_map/ppermute | solution.py:372
  0.5 24.8 %copy-start.1 = (bf16[2,768,768]{2,1,0:T(8,128)(2,1)S(1)}, bf16[2,768,768]{2,1,0:T(8,128)(2,1)}, u32[]{:S(2)}) copy-start(bf16[2,768,768]{2,1,0:T(8,128)(2,1)} %wo_ref.1) | copy-start | bytes 7077892
  3.1 6.9 %collective-permute-start.2 = (bf16[448,128]{1,0:T(8,128)(2,1)S(1)}, bf16[448,128]{1,0:T(8,128)(2,1)S(1)}, u32[]{:S(2)}, u32[]{:S(2)}) collective-permute-start(bf16[448,128]{1,0:T(8,128)(2,1)S(1)} %get-tuple-element.24), channel_id=1, source_target_pairs={{0,4},{2,6},{4,0},{6,2},{8,12},{10,14},{12,8},{14,10},{1,5},{3,7},... | collective-permute-start | bytes 344072 | tf_op jit(solution)/shard_map/ppermute | solution.py:370
  5.6 11.8 %collective-permute-start.4 = (bf16[448,128]{1,0:T(8,128)(2,1)S(1)}, bf16[448,128]{1,0:T(8,128)(2,1)S(1)}, u32[]{:S(2)}, u32[]{:S(2)}) collective-permute-start(bf16[448,128]{1,0:T(8,128)(2,1)S(1)} %get-tuple-element.25), channel_id=1, source_target_pairs={{0,8},{2,10},{4,12},{6,14},{8,0},{10,2},{12,4},{14,6},{1,9},{3,11}... | collective-permute-start | bytes 344072 | tf_op jit(solution)/shard_map/ppermute | solution.py:370
  8.3 10.8 %collective-permute-start.6 = (bf16[448,128]{1,0:T(8,128)(2,1)S(1)}, bf16[448,128]{1,0:T(8,128)(2,1)S(1)}, u32[]{:S(2)}, u32[]{:S(2)}) collective-permute-start(bf16[448,128]{1,0:T(8,128)(2,1)S(1)} %get-tuple-element.26), channel_id=1, source_target_pairs={{0,12},{2,14},{4,8},{6,10},{8,4},{10,6},{12,0},{14,2},{1,13},{3,15... | collective-permute-start | bytes 344072 | tf_op jit(solution)/shard_map/ppermute | solution.py:370
  8.3 11.3 %collective-permute-start.1 = (bf16[352,128]{1,0:T(8,128)(2,1)S(1)}, bf16[352,128]{1,0:T(8,128)(2,1)S(1)}, u32[]{:S(2)}, u32[]{:S(2)}) collective-permute-start(bf16[352,128]{1,0:T(8,128)(2,1)S(1)} %get-tuple-element.23), channel_id=1, source_target_pairs={{0,2},{2,0},{4,6},{6,4},{8,10},{10,8},{12,14},{14,12},{1,3},{3,1},... | collective-permute-start | bytes 270344 | tf_op jit(solution)/shard_map/ppermute | solution.py:370
  10.0 11.0 %collective-permute-start.9 = (bf16[448,128]{1,0:T(8,128)(2,1)S(1)}, bf16[448,128]{1,0:T(8,128)(2,1)S(1)}, u32[]{:S(2)}, u32[]{:S(2)}) collective-permute-start(bf16[448,128]{1,0:T(8,128)(2,1)S(1)} %collective-permute-done.2.refs_1_.refs_2_), channel_id=1, source_target_pairs={{0,1},{1,0},{2,3},{3,2},{4,5},{5,4},{6,7},{7,6},{8,9},{9,8},{10,11... | collective-permute-start | bytes 344072 | tf_op jit(solution)/shard_map/ppermute | solution.py:383
  10.0 11.3 %collective-permute-start.3 = (bf16[448,128]{1,0:T(8,128)(2,1)S(1)}, bf16[448,128]{1,0:T(8,128)(2,1)S(1)}, u32[]{:S(2)}, u32[]{:S(2)}) collective-permute-start(bf16[448,128]{1,0:T(8,128)(2,1)S(1)} %collective-permute-done.2.refs_1_.refs_2_), channel_id=1, source_target_pairs={{0,2},{2,0},{4,6},{6,4},{8,10},{10,8},{12,14},{14,12},{1,3},{3,1},... | collective-permute-start | bytes 344072 | tf_op jit(solution)/shard_map/ppermute | solution.py:370
  17.5 4.8 %collective-permute-start.5 = (bf16[448,128]{1,0:T(8,128)(2,1)S(1)}, bf16[448,128]{1,0:T(8,128)(2,1)S(1)}, u32[]{:S(2)}, u32[]{:S(2)}) collective-permute-start(bf16[448,128]{1,0:T(8,128)(2,1)S(1)} %collective-permute-done.4.refs_3_.refs_4_), channel_id=1, source_target_pairs={{0,2},{2,0},{4,6},{6,4},{8,10},{10,8},{12,14},{14,12},{1,3},{3,1},... | collective-permute-start | bytes 344072 | tf_op jit(solution)/shard_map/ppermute | solution.py:370
  19.0 4.8 %collective-permute-start.7 = (bf16[448,128]{1,0:T(8,128)(2,1)S(1)}, bf16[448,128]{1,0:T(8,128)(2,1)S(1)}, u32[]{:S(2)}, u32[]{:S(2)}) collective-permute-start(bf16[448,128]{1,0:T(8,128)(2,1)S(1)} %collective-permute-done.6.refs_5_.refs_6_), channel_id=1, source_target_pairs={{0,2},{2,0},{4,6},{6,4},{8,10},{10,8},{12,14},{14,12},{1,3},{3,1},... | collective-permute-start | bytes 344072 | tf_op jit(solution)/shard_map/ppermute | solution.py:370
  19.5 1.3 %collective-permute-start.8 = (bf16[352,128]{1,0:T(8,128)(2,1)S(1)}, bf16[352,128]{1,0:T(8,128)(2,1)S(1)}, u32[]{:S(2)}, u32[]{:S(2)}) collective-permute-start(bf16[352,128]{1,0:T(8,128)(2,1)S(1)} %collective-permute-done.1.refs_0_.refs_1_), channel_id=1, source_target_pairs={{0,1},{1,0},{2,3},{3,2},{4,5},{5,4},{6,7},{7,6},{8,9},{9,8},{10,11... | collective-permute-start | bytes 270344 | tf_op jit(solution)/shard_map/ppermute | solution.py:383
  20.8 4.5 %collective-permute-start.11 = (bf16[448,128]{1,0:T(8,128)(2,1)S(1)}, bf16[448,128]{1,0:T(8,128)(2,1)S(1)}, u32[]{:S(2)}, u32[]{:S(2)}) collective-permute-start(bf16[448,128]{1,0:T(8,128)(2,1)S(1)} %collective-permute-done.4.refs_3_.refs_4_), channel_id=1, source_target_pairs={{0,1},{1,0},{2,3},{3,2},{4,5},{5,4},{6,7},{7,6},{8,9},{9,8},{10,11... | collective-permute-start | bytes 344072 | tf_op jit(solution)/shard_map/ppermute | solution.py:383
  21.0 4.4 %collective-permute-start.13 = (bf16[448,128]{1,0:T(8,128)(2,1)S(1)}, bf16[448,128]{1,0:T(8,128)(2,1)S(1)}, u32[]{:S(2)}, u32[]{:S(2)}) collective-permute-start(bf16[448,128]{1,0:T(8,128)(2,1)S(1)} %collective-permute-done.6.refs_5_.refs_6_), channel_id=1, source_target_pairs={{0,1},{1,0},{2,3},{3,2},{4,5},{5,4},{6,7},{7,6},{8,9},{9,8},{10,11... | collective-permute-start | bytes 344072 | tf_op jit(solution)/shard_map/ppermute | solution.py:383
  21.3 4.0 %collective-permute-start.10 = (bf16[448,128]{1,0:T(8,128)(2,1)S(1)}, bf16[448,128]{1,0:T(8,128)(2,1)S(1)}, u32[]{:S(2)}, u32[]{:S(2)}) collective-permute-start(bf16[448,128]{1,0:T(8,128)(2,1)S(1)} %collective-permute-done.3.refs_2_.refs_3_), channel_id=1, source_target_pairs={{0,1},{1,0},{2,3},{3,2},{4,5},{5,4},{6,7},{7,6},{8,9},{9,8},{10,11... | collective-permute-start | bytes 344072 | tf_op jit(solution)/shard_map/ppermute | solution.py:383
  22.3 3.1 %collective-permute-start.12 = (bf16[448,128]{1,0:T(8,128)(2,1)S(1)}, bf16[448,128]{1,0:T(8,128)(2,1)S(1)}, u32[]{:S(2)}, u32[]{:S(2)}) collective-permute-start(bf16[448,128]{1,0:T(8,128)(2,1)S(1)} %collective-permute-done.5.refs_4_.refs_5_), channel_id=1, source_target_pairs={{0,1},{1,0},{2,3},{3,2},{4,5},{5,4},{6,7},{7,6},{8,9},{9,8},{10,11... | collective-permute-start | bytes 344072 | tf_op jit(solution)/shard_map/ppermute | solution.py:383
  23.8 1.5 %collective-permute-start.14 = (bf16[448,128]{1,0:T(8,128)(2,1)S(1)}, bf16[448,128]{1,0:T(8,128)(2,1)S(1)}, u32[]{:S(2)}, u32[]{:S(2)}) collective-permute-start(bf16[448,128]{1,0:T(8,128)(2,1)S(1)} %collective-permute-done.7.refs_6_.refs_7_), channel_id=1, source_target_pairs={{0,1},{1,0},{2,3},{3,2},{4,5},{5,4},{6,7},{7,6},{8,9},{9,8},{10,11... | collective-permute-start | bytes 344072 | tf_op jit(solution)/shard_map/ppermute | solution.py:383

commit v6 on v5

--- a/solution.py
+++ b/solution.py
@@ -232,7 +232,7 @@
         lane = lax.broadcasted_iota(jnp.int32, (1, stop - start), 1) + start
         inside = jnp.where((lane >= low) & (lane < high), 1.0, 0.0).astype(jnp.bfloat16)
         cols = pl.ds(pl.multiple_of(base + start, LANES), stop - start)
-        firsts = [(layer * half + h) * rows + (0 if p == 0 else ahead) for p in range(len(blocks))]
+        firsts = [(layer * half + h) * rows + (0 if p == 0 or p % 2 == 1 and p > 1 else ahead) for p in range(len(blocks))]
         bias = jnp.concatenate(
             [block[at : at + rows, :] for at, block in zip(firsts, blocks)], axis=0
         )
@@ -275,7 +275,7 @@
         block_refs, refs = refs[: len(blocks)], refs[len(blocks) :]
         x_ref, q_ref, k_ref, vt_ref, at_ref, n_ref, *work = refs
         for p, block in enumerate((kept_ref, *block_refs)):
-            at = used + total if p % 2 == 1 and p > 1 else 0
+            at = total if p % 2 == 1 and p > 1 else 0
             for k in range(width // LANES):
                 x_ref[block_rows(p, rows), k * LANES : (k + 1) * LANES] = block[
                     at + k * rows : at + (k + 1) * rows, :
@@ -359,6 +359,14 @@
     )(mask, w_qkv, w_out, *state, *near, *far)
 
 
+def apart(joined, parts):
+    pieces, at = [], 0
+    for part in parts:
+        pieces.append(joined[at : at + part.shape[0]])
+        at += part.shape[0]
+    return pieces
+
+
 def spread_body(states, ancestors, noise, pair, token_mask, w_qkv, w_out, w_pair):
     particles, rows, width = states.shape
     heads = w_pair.shape[2]
@@ -370,20 +378,35 @@
         return lax.ppermute(block, "tok", [(t, t ^ k) for t in range(particles)])
 
     other_states = lax.ppermute(states, "dom", swap)
-    near, far, own, local_noise = prepare(
+    near, rest, own, local_noise = prepare(
         pair, mask_row, w_pair.transpose(0, 2, 1), states, noise, w_qkv
     )
     kept, neighbour, *sent = pack(ancestors, own, other_states, local_noise, near)
-    blocks = {}
-    for k in range(particles - 2, 0, -2):
-        blocks[k] = beside(sent[k // 2 - 1], k)
-        blocks[k + 1] = beside(blocks[k])
-    blocks[1] = beside(neighbour)
-    blocks = [blocks[p] for p in range(1, particles)]
-    swapped = [lax.ppermute(block, "dom", swap) for block in blocks]
+    ahead = rows * (width // LANES)
+    passing = range(2, particles, 2)
+    blocks = {k: beside(block, k) for k, block in zip(passing, sent)}
+    blocks[1], blocks[3] = apart(
+        beside(jnp.concatenate([neighbour, blocks[2][ahead:]], axis=0)), [neighbour, blocks[2][ahead:]]
+    )
+    for k in passing[1:-1]:
+        blocks[k + 1] = beside(blocks[k][ahead:])
+    far = {}
+
+    def swap_all(distances):
+        group = [blocks[distance] for distance in distances]
+        swapped = lax.ppermute(jnp.concatenate(group, axis=0), "dom", swap)
+        far.update(zip(distances, apart(swapped, group)))
+
+    blocks[passing[-1] + 1] = beside(blocks[passing[-1]][ahead:])
+    for k in passing:
+        swap_all([k])
+    swap_all(list(range(1, particles - 1, 2)))
+    swap_all([particles - 1])
+    swapped = [far[distance] for distance in range(1, particles)]
+    blocks = [blocks[distance] for distance in range(1, particles)]
     state = first_half(mask_row, kept, near, blocks, w_qkv, rows, heads, scale)
     result = layers(
-        mask_row, state, (near, *blocks), (far, *swapped), w_qkv, w_out, rows, heads, scale
+        mask_row, state, (near, *blocks), (rest, *swapped), w_qkv, w_out, rows, heads, scale
     )
     return lax.all_to_all(result, "tok", 0, 0, tiled=True)
 
@@ -405,7 +428,7 @@
         fits = (
             particles == mesh.shape["tok"]
             and particles & (particles - 1) == 0
-            and particles > 2
+            and particles > 4
             and mesh.shape["dom"] == 2
             and width % (2 * LANES) == 0
             and w_pair.shape[2] % 2 == 0

time: 42.8 us -> 42.1 us (0.984)
  blocking collectives: 13.4 us -> 12.1 us
  waiting for transfers between devices: 7.83 us -> 9.01 us
  starting transfers between devices: 13.4 us -> 12.7 us
    ppermute x7 -> x6, waiting for transfers between devices: 6.52 us -> 8.99 us  [beside(): return lax.ppermute(block, 'tok', [(t, t ^ k) for t in range(particles)])]
    ppermute x7 -> x5, waiting for transfers between devices: 1.3 us -> 0.01 us  [swap_all(): swapped = lax.ppermute(jnp.concatenate(group, axis=0), 'dom', swap)]
    all_to_all x1, blocking collectives: 13.4 us -> 12.1 us  [spread_body(): return lax.all_to_all(result, 'tok', 0, 0, tiled=True)]
    ppermute x7 -> x6, starting transfers between devices: 12.2 us -> 11.1 us  [beside(): return lax.ppermute(block, 'tok', [(t, t ^ k) for t in range(particles)])]
    ppermute x7 -> x5, starting transfers between devices: 0.68 us -> 1.09 us  [swap_all(): swapped = lax.ppermute(jnp.concatenate(group, axis=0), 'dom', swap)]
  transfers between devices with their start and end apart: 15 -> 12, of which waited for: 4 -> 4; matrix products, arithmetic and copies ran while one was open for 0% -> 0% of each run, Pallas kernels for 8% -> 8%
where the time goes in v6:
time: 42.1 us; the launch traced here: 41.9 us
  starting transfers between devices  12.7 us (30%)
  blocking collectives  12.1 us (29%)
  waiting for transfers between devices  9.01 us (21%)
  Pallas kernels  7.2 us (17%)
  local copies, waits for them, and re-layouts  0.75 us (2%)
    all_to_all x1, blocking collectives, spread_body(): return lax.all_to_all(result, 'tok', 0, 0, tiled=True)  12.1 us
    ppermute x6, starting transfers between devices, beside(): return lax.ppermute(block, 'tok', [(t, t ^ k) for t in range(particles)])  11.1 us
    ppermute x6, waiting for transfers between devices, beside(): return lax.ppermute(block, 'tok', [(t, t ^ k) for t in range(particles)])  8.99 us
    pallas_call x1, Pallas kernels, layers(): pl.pallas_call(kernel, out_shape=jax.ShapeDtypeStruct((sources, rows, wid...  3.2 us
    pallas_call x1, Pallas kernels, prepare(): pl.pallas_call(kernel, out_shape=(part, part, jax.ShapeDtypeStruct(own.sh...  1.86 us
    pallas_call x1, Pallas kernels, first_half(): pl.pallas_call(kernel, out_shape=(wide, wide, wide, tall, tall), in_specs...  1.49 us
    ppermute x5, starting transfers between devices, swap_all(): swapped = lax.ppermute(jnp.concatenate(group, axis=0), 'dom', swap)  1.09 us
  transfers between devices with their start and end apart: 12, of which 4 were waited for; matrix products, arithmetic and copies ran while one was open for 0% of the time, Pallas kernels for 8%

profile of v6, /device:TPU:0, one launch (start us, length us, event | category | flops | bytes accessed | tf_op | source)
XLA Modules:
  0.0 41.9 jit_solution(17441901500416012270)
XLA Ops:
  0.0 0.0 copy-start
  0.0 0.0 copy-start.2
  0.0 0.0 copy-start.3
  0.0 0.5 %collective-permute-start = (bf16[8,16,768]{2,1,0:T(8,128)(2,1)}, bf16[8,16,768]{2,1,0:T(8,128)(2,1)S(1)}, u32[]{:S(2)}, u32[]{:S(2)}) collective-permute-start(bf16[8,16,768]{2,1,0:T(8,128)(2,1)} %own_hbm.1), channel_id=1, source_target_pairs={{0,1},{1,0},{2,3},{3,2},{4,5},{5,4},{6,7},{7,6},{8,9},{9,8},{10,11... | collective-permute-start | bytes 589832 | tf_op jit(solution)/shard_map/ppermute | solution.py:380
  0.5 1.9 %prepare.1 = (bf16[256,128]{1,0:T(8,128)(2,1)S(1)}, bf16[256,128]{1,0:T(8,128)(2,1)S(1)}, bf16[8,16,768]{2,1,0:T(8,128)(2,1)S(1)}, bf16[8,16,768]{2,1,0:T(8,128)(2,1)S(1)}) custom-call(bf16[16,128,128]{2,1,0:T(8,128)(2,1)} %pair_hbm.1, s32[1,128]{1,0:T(1,128)} %bitcast.2, bf16[2,16,128]{2,1,0:T(8,128)(2,1)} %bitcast.5, bf16[8,16,768]{2,1,0:T(8,128)(2,1)} %own_hbm.1, ...), custom_call_target="tpu_custom_call" | custom-call | flops 16777216 | bytes 8000000 | tf_op jit(solution)/shard_map/prepare/pallas_call | solution.py:122
  2.4 0.0 copy-start.1
  2.4 0.0 collective-permute-done.other_ref
  2.4 0.0 copy-done.3
  2.4 0.6 %pack.1 = (bf16[96,128]{1,0:T(8,128)(2,1)S(1)}, bf16[352,128]{1,0:T(8,128)(2,1)S(1)}, bf16[448,128]{1,0:T(8,128)(2,1)S(1)}, bf16[448,128]{1,0:T(8,128)(2,1)S(1)}, bf16[448,128]{1,0:T(8,128)(2,1)S(1)}) custom-call(s32[8]{0:T(128)S(1)} %copy-done.3, bf16[8,16,768]{2,1,0:T(8,128)(2,1)S(1)} %get-tuple-element.19.own_ref, ...), custom_call_target="tpu_custom_call" | custom-call | tf_op jit(solution)/shard_map/pack/pallas_call | solution.py:179
  3.1 2.6 %collective-permute-start.1 = (bf16[448,128]{1,0:T(8,128)(2,1)S(1)}, bf16[448,128]{1,0:T(8,128)(2,1)S(1)}, u32[]{:S(2)}, u32[]{:S(2)}) collective-permute-start(bf16[448,128]{1,0:T(8,128)(2,1)S(1)} %get-tuple-element.24), channel_id=1, source_target_pairs={{0,4},{2,6},{4,0},{6,2},{8,12},{10,14},{12,8},{14,10},{1,5},{3,7},... | collective-permute-start | bytes 344072 | tf_op jit(solution)/shard_map/ppermute | solution.py:378
  5.7 2.6 %collective-permute-start.3 = (bf16[448,128]{1,0:T(8,128)(2,1)S(1)}, bf16[448,128]{1,0:T(8,128)(2,1)S(1)}, u32[]{:S(2)}, u32[]{:S(2)}) collective-permute-start(bf16[448,128]{1,0:T(8,128)(2,1)S(1)} %get-tuple-element.25), channel_id=1, source_target_pairs={{0,8},{2,10},{4,12},{6,14},{8,0},{10,2},{12,4},{14,6},{1,9},{3,11}... | collective-permute-start | bytes 344072 | tf_op jit(solution)/shard_map/ppermute | solution.py:378
  8.3 0.0 collective-permute-start.5
  8.3 1.4 %collective-permute-done.1.refs_1_.refs_2_ = bf16[448,128]{1,0:T(8,128)(2,1)S(1)} collective-permute-done((bf16[448,128]{1,0:T(8,128)(2,1)S(1)}, bf16[448,128]{1,0:T(8,128)(2,1)S(1)}, u32[]{:S(2)}, u32[]{:S(2)}) %collective-permute-start.1) | collective-permute-done | bytes 114720 | tf_op jit(solution)/shard_map/ppermute | solution.py:378
  9.7 3.7 %collective-permute-start.2 = (bf16[704,128]{1,0:T(8,128)(2,1)S(1)}, bf16[704,128]{1,0:T(8,128)(2,1)S(1)}, u32[]{:S(2)}, u32[]{:S(2)}) collective-permute-start(bf16[704,128]{1,0:T(8,128)(2,1)S(1)} %pad_maximum_fusion.1), channel_id=1, source_target_pairs={{0,2},{2,0},{4,6},{6,4},{8,10},{10,8},{12,14},{14,12},{1,3},{3,1},... | collective-permute-start | bytes 540680 | tf_op jit(solution)/shard_map/ppermute | solution.py:378
  13.4 4.1 %collective-permute-done.3.refs_3_.refs_4_ = bf16[448,128]{1,0:T(8,128)(2,1)S(1)} collective-permute-done((bf16[448,128]{1,0:T(8,128)(2,1)S(1)}, bf16[448,128]{1,0:T(8,128)(2,1)S(1)}, u32[]{:S(2)}, u32[]{:S(2)}) %collective-permute-start.3) | collective-permute-done | bytes 114720 | tf_op jit(solution)/shard_map/ppermute | solution.py:378
  17.5 1.6 %collective-permute-start.4 = (bf16[352,128]{1,0:T(8,128)(2,1)S(1)}, bf16[352,128]{1,0:T(8,128)(2,1)S(1)}, u32[]{:S(2)}, u32[]{:S(2)}) collective-permute-start(bf16[352,128]{1,0:T(8,128)(2,1)S(1)} %slice.36), channel_id=1, source_target_pairs={{0,2},{2,0},{4,6},{6,4},{8,10},{10,8},{12,14},{14,12},{1,3},{3,1},... | collective-permute-start | bytes 270344 | tf_op jit(solution)/shard_map/ppermute | solution.py:378
  19.1 0.0 collective-permute-done.5.refs_5_.refs_6_
  19.1 0.6 %collective-permute-start.6 = (bf16[352,128]{1,0:T(8,128)(2,1)S(1)}, bf16[352,128]{1,0:T(8,128)(2,1)S(1)}, u32[]{:S(2)}, u32[]{:S(2)}) collective-permute-start(bf16[352,128]{1,0:T(8,128)(2,1)S(1)} %slice.37), channel_id=1, source_target_pairs={{0,2},{2,0},{4,6},{6,4},{8,10},{10,8},{12,14},{14,12},{1,3},{3,1},... | collective-permute-start | bytes 270344 | tf_op jit(solution)/shard_map/ppermute | solution.py:378
  19.7 0.0 collective-permute-start.8
  19.7 0.5 %collective-permute-start.9 = (bf16[448,128]{1,0:T(8,128)(2,1)S(1)}, bf16[448,128]{1,0:T(8,128)(2,1)S(1)}, u32[]{:S(2)}, u32[]{:S(2)}) collective-permute-start(bf16[448,128]{1,0:T(8,128)(2,1)S(1)} %collective-permute-done.3.refs_3_.refs_4_), channel_id=1, source_target_pairs={{0,1},{1,0},{2,3},{3,2},{4,5},{5,4},{6,7},{7,6},{8,9},{9,8},{10,11... | collective-permute-start | bytes 344072 | tf_op jit(solution)/shard_map/ppermute | solution.py:397
  20.2 1.9 %collective-permute-done.4.refs_4_.refs_5_ = bf16[352,128]{1,0:T(8,128)(2,1)S(1)} collective-permute-done((bf16[352,128]{1,0:T(8,128)(2,1)S(1)}, bf16[352,128]{1,0:T(8,128)(2,1)S(1)}, u32[]{:S(2)}, u32[]{:S(2)}) %collective-permute-start.4) | collective-permute-done | bytes 90144 | tf_op jit(solution)/shard_map/ppermute | solution.py:378
  22.1 0.0 collective-permute-start.10
  22.1 1.6 %collective-permute-done.6.refs_6_.refs_7_ = bf16[352,128]{1,0:T(8,128)(2,1)S(1)} collective-permute-done((bf16[352,128]{1,0:T(8,128)(2,1)S(1)}, bf16[352,128]{1,0:T(8,128)(2,1)S(1)}, u32[]{:S(2)}, u32[]{:S(2)}) %collective-permute-start.6) | collective-permute-done | bytes 90144 | tf_op jit(solution)/shard_map/ppermute | solution.py:378
  23.7 0.0 collective-permute-start.11
  23.7 0.0 collective-permute-done.2
  23.7 0.6 %collective-permute-start.7 = (bf16[1056,128]{1,0:T(8,128)(2,1)S(1)}, bf16[1056,128]{1,0:T(8,128)(2,1)S(1)}, u32[]{:S(2)}, u32[]{:S(2)}) collective-permute-start(bf16[1056,128]{1,0:T(8,128)(2,1)S(1)} %pad_maximum_fusion), channel_id=1, source_target_pairs={{0,1},{1,0},{2,3},{3,2},{4,5},{5,4},{6,7},{7,6},{8,9},{9,8},{10,11... | collective-permute-start | bytes 811016 | tf_op jit(solution)/shard_map/ppermute | solution.py:397
  24.3 0.0 copy-done
  24.3 0.0 copy-done.2
  24.3 1.5 %first_half.1 = (bf16[128,768]{1,0:T(8,128)(2,1)S(1)}, bf16[128,768]{1,0:T(8,128)(2,1)S(1)}, bf16[128,768]{1,0:T(8,128)(2,1)S(1)}, bf16[768,128]{1,0:T(8,128)(2,1)S(1)}, bf16[768,128]{1,0:T(8,128)(2,1)S(1)}) custom-call(s32[1,128]{1,0:T(1,128)S(1)} %bitcast.3, bf16[2,768,2304]{2,1,0:T(8,128)(2,1)S(1)} %copy-done, ...), custom_call_target="tpu_custom_call" | custom-call | flops 452984832 | bytes 4718592 | tf_op jit(solution)/shard_map/first_half/pallas_call | solution.py:293
  25.8 0.0 collective-permute-done.7
  25.9 0.0 collective-permute-done.8.refs_10_
  25.9 0.0 collective-permute-done.9.refs_12_
  25.9 0.0 collective-permute-done.10.refs_14_
  25.9 0.0 collective-permute-done.11.refs_15_
  25.9 0.0 copy-done.1
  25.9 3.2 %layers.1 = bf16[8,16,768]{2,1,0:T(8,128)(2,1)S(1)} custom-call(s32[1,128]{1,0:T(1,128)S(1)} %bitcast.4, bf16[2,768,2304]{2,1,0:T(8,128)(2,1)S(1)} %copy-done, bf16[2,768,768]{2,1,0:T(8,128)(2,1)S(1)} %copy-done.1, bf16[128,768]{1,0:T(8,128)(2,1)S(1)} %get-tuple-element.27.x_ref, bf16[128,768]{1,0:T(8,128)(2,1)S(1)} %get-tuple-element.28.q_in, ...), custom_call_target="tpu_custom_call" | custom-call | flops 1056964608 | bytes 5898240 | tf_op jit(solution)/shard_map/layers/pallas_call | solution.py:347
  29.1 12.1 %all_to_all.5 = bf16[8,16,768]{2,1,0:T(8,128)(2,1)S(1)} all-to-all(bf16[8,16,768]{2,1,0:T(8,128)(2,1)S(1)} %layers.1), channel_id=1, replica_groups=mesh['groups'=2,'tok'=8,'dom'=2] {'tok'}, dimensions={0} | all-to-all | bytes 393216 | tf_op jit(solution)/shard_map/all_to_all | solution.py:411
  41.2 0.7 %copy.10 = bf16[8,16,768]{2,1,0:T(8,128)(2,1)} copy(bf16[8,16,768]{2,1,0:T(8,128)(2,1)S(1)} %all_to_all.5) | data formatting | bytes 393216
  (7 shorter events, 0.1 us)
Async XLA Ops:
  0.0 24.3 %copy-start = (bf16[2,768,2304]{2,1,0:T(8,128)(2,1)S(1)}, bf16[2,768,2304]{2,1,0:T(8,128)(2,1)}, u32[]{:S(2)}) copy-start(bf16[2,768,2304]{2,1,0:T(8,128)(2,1)} %wq_ref.1) | copy-start | bytes 21233668
  0.0 24.3 %copy-start.2 = (s32[128]{0:T(128)S(1)}, s32[128]{0:T(128)}, u32[]{:S(2)}) copy-start(s32[128]{0:T(128)} %param.12) | copy-start | bytes 1540
  0.0 2.4 %copy-start.3 = (s32[8]{0:T(128)S(1)}, s32[8]{0:T(128)}, u32[]{:S(2)}) copy-start(s32[8]{0:T(128)} %anc_ref.1) | copy-start | bytes 100
  0.0 2.4 %collective-permute-start = (bf16[8,16,768]{2,1,0:T(8,128)(2,1)}, bf16[8,16,768]{2,1,0:T(8,128)(2,1)S(1)}, u32[]{:S(2)}, u32[]{:S(2)}) collective-permute-start(bf16[8,16,768]{2,1,0:T(8,128)(2,1)} %own_hbm.1), channel_id=1, source_target_pairs={{0,1},{1,0},{2,3},{3,2},{4,5},{5,4},{6,7},{7,6},{8,9},{9,8},{10,11... | collective-permute-start | bytes 589832 | tf_op jit(solution)/shard_map/ppermute | solution.py:380
  2.4 23.5 %copy-start.1 = (bf16[2,768,768]{2,1,0:T(8,128)(2,1)S(1)}, bf16[2,768,768]{2,1,0:T(8,128)(2,1)}, u32[]{:S(2)}) copy-start(bf16[2,768,768]{2,1,0:T(8,128)(2,1)} %wo_ref.1) | copy-start | bytes 7077892
  3.1 6.6 %collective-permute-start.1 = (bf16[448,128]{1,0:T(8,128)(2,1)S(1)}, bf16[448,128]{1,0:T(8,128)(2,1)S(1)}, u32[]{:S(2)}, u32[]{:S(2)}) collective-permute-start(bf16[448,128]{1,0:T(8,128)(2,1)S(1)} %get-tuple-element.24), channel_id=1, source_target_pairs={{0,4},{2,6},{4,0},{6,2},{8,12},{10,14},{12,8},{14,10},{1,5},{3,7},... | collective-permute-start | bytes 344072 | tf_op jit(solution)/shard_map/ppermute | solution.py:378
  5.7 11.8 %collective-permute-start.3 = (bf16[448,128]{1,0:T(8,128)(2,1)S(1)}, bf16[448,128]{1,0:T(8,128)(2,1)S(1)}, u32[]{:S(2)}, u32[]{:S(2)}) collective-permute-start(bf16[448,128]{1,0:T(8,128)(2,1)S(1)} %get-tuple-element.25), channel_id=1, source_target_pairs={{0,8},{2,10},{4,12},{6,14},{8,0},{10,2},{12,4},{14,6},{1,9},{3,11}... | collective-permute-start | bytes 344072 | tf_op jit(solution)/shard_map/ppermute | solution.py:378
  8.3 10.8 %collective-permute-start.5 = (bf16[448,128]{1,0:T(8,128)(2,1)S(1)}, bf16[448,128]{1,0:T(8,128)(2,1)S(1)}, u32[]{:S(2)}, u32[]{:S(2)}) collective-permute-start(bf16[448,128]{1,0:T(8,128)(2,1)S(1)} %get-tuple-element.26), channel_id=1, source_target_pairs={{0,12},{2,14},{4,8},{6,10},{8,4},{10,6},{12,0},{14,2},{1,13},{3,15... | collective-permute-start | bytes 344072 | tf_op jit(solution)/shard_map/ppermute | solution.py:378
  9.7 14.0 %collective-permute-start.2 = (bf16[704,128]{1,0:T(8,128)(2,1)S(1)}, bf16[704,128]{1,0:T(8,128)(2,1)S(1)}, u32[]{:S(2)}, u32[]{:S(2)}) collective-permute-start(bf16[704,128]{1,0:T(8,128)(2,1)S(1)} %pad_maximum_fusion.1), channel_id=1, source_target_pairs={{0,2},{2,0},{4,6},{6,4},{8,10},{10,8},{12,14},{14,12},{1,3},{3,1},... | collective-permute-start | bytes 540680 | tf_op jit(solution)/shard_map/ppermute | solution.py:378
  17.5 4.6 %collective-permute-start.4 = (bf16[352,128]{1,0:T(8,128)(2,1)S(1)}, bf16[352,128]{1,0:T(8,128)(2,1)S(1)}, u32[]{:S(2)}, u32[]{:S(2)}) collective-permute-start(bf16[352,128]{1,0:T(8,128)(2,1)S(1)} %slice.36), channel_id=1, source_target_pairs={{0,2},{2,0},{4,6},{6,4},{8,10},{10,8},{12,14},{14,12},{1,3},{3,1},... | collective-permute-start | bytes 270344 | tf_op jit(solution)/shard_map/ppermute | solution.py:378
  19.1 4.6 %collective-permute-start.6 = (bf16[352,128]{1,0:T(8,128)(2,1)S(1)}, bf16[352,128]{1,0:T(8,128)(2,1)S(1)}, u32[]{:S(2)}, u32[]{:S(2)}) collective-permute-start(bf16[352,128]{1,0:T(8,128)(2,1)S(1)} %slice.37), channel_id=1, source_target_pairs={{0,2},{2,0},{4,6},{6,4},{8,10},{10,8},{12,14},{14,12},{1,3},{3,1},... | collective-permute-start | bytes 270344 | tf_op jit(solution)/shard_map/ppermute | solution.py:378
  19.7 6.2 %collective-permute-start.8 = (bf16[448,128]{1,0:T(8,128)(2,1)S(1)}, bf16[448,128]{1,0:T(8,128)(2,1)S(1)}, u32[]{:S(2)}, u32[]{:S(2)}) collective-permute-start(bf16[448,128]{1,0:T(8,128)(2,1)S(1)} %collective-permute-done.1.refs_1_.refs_2_), channel_id=1, source_target_pairs={{0,1},{1,0},{2,3},{3,2},{4,5},{5,4},{6,7},{7,6},{8,9},{9,8},{10,11... | collective-permute-start | bytes 344072 | tf_op jit(solution)/shard_map/ppermute | solution.py:397
  19.7 6.2 %collective-permute-start.9 = (bf16[448,128]{1,0:T(8,128)(2,1)S(1)}, bf16[448,128]{1,0:T(8,128)(2,1)S(1)}, u32[]{:S(2)}, u32[]{:S(2)}) collective-permute-start(bf16[448,128]{1,0:T(8,128)(2,1)S(1)} %collective-permute-done.3.refs_3_.refs_4_), channel_id=1, source_target_pairs={{0,1},{1,0},{2,3},{3,2},{4,5},{5,4},{6,7},{7,6},{8,9},{9,8},{10,11... | collective-permute-start | bytes 344072 | tf_op jit(solution)/shard_map/ppermute | solution.py:397
  22.1 3.8 %collective-permute-start.10 = (bf16[448,128]{1,0:T(8,128)(2,1)S(1)}, bf16[448,128]{1,0:T(8,128)(2,1)S(1)}, u32[]{:S(2)}, u32[]{:S(2)}) collective-permute-start(bf16[448,128]{1,0:T(8,128)(2,1)S(1)} %collective-permute-done.5.refs_5_.refs_6_), channel_id=1, source_target_pairs={{0,1},{1,0},{2,3},{3,2},{4,5},{5,4},{6,7},{7,6},{8,9},{9,8},{10,11... | collective-permute-start | bytes 344072 | tf_op jit(solution)/shard_map/ppermute | solution.py:397
  23.7 2.2 %collective-permute-start.11 = (bf16[352,128]{1,0:T(8,128)(2,1)S(1)}, bf16[352,128]{1,0:T(8,128)(2,1)S(1)}, u32[]{:S(2)}, u32[]{:S(2)}) collective-permute-start(bf16[352,128]{1,0:T(8,128)(2,1)S(1)} %collective-permute-done.6.refs_6_.refs_7_), channel_id=1, source_target_pairs={{0,1},{1,0},{2,3},{3,2},{4,5},{5,4},{6,7},{7,6},{8,9},{9,8},{10,11... | collective-permute-start | bytes 270344 | tf_op jit(solution)/shard_map/ppermute | solution.py:397
  23.7 2.1 %collective-permute-start.7 = (bf16[1056,128]{1,0:T(8,128)(2,1)S(1)}, bf16[1056,128]{1,0:T(8,128)(2,1)S(1)}, u32[]{:S(2)}, u32[]{:S(2)}) collective-permute-start(bf16[1056,128]{1,0:T(8,128)(2,1)S(1)} %pad_maximum_fusion), channel_id=1, source_target_pairs={{0,1},{1,0},{2,3},{3,2},{4,5},{5,4},{6,7},{7,6},{8,9},{9,8},{10,11... | collective-permute-start | bytes 811016 | tf_op jit(solution)/shard_map/ppermute | solution.py:397

commit v7 on v6

--- a/solution.py
+++ b/solution.py
@@ -104,8 +104,9 @@
         penalty = jnp.where(mask_ref[...] > 0, 0.0, MASKED).astype(jnp.float32)
         w_all = w_ref[...].reshape(blocks, channels)
         copies[2].wait()
+        terms = across(w_all, pair_ref[...].reshape(rows * keys, channels))
         for i in range(rows):
-            piece = across(w_all, pair_ref[i]) + penalty
+            piece = terms[:, i * keys : (i + 1) * keys] + penalty
             rows_ref[:, i, :] = piece - jnp.max(piece, axis=-1, keepdims=True)
         dom = lax.axis_index("dom")
         for l in range(layer_count):
@@ -398,8 +399,8 @@
         far.update(zip(distances, apart(swapped, group)))
 
     blocks[passing[-1] + 1] = beside(blocks[passing[-1]][ahead:])
-    for k in passing:
-        swap_all([k])
+    swap_all(list(passing[:-1]))
+    swap_all([passing[-1]])
     swap_all(list(range(1, particles - 1, 2)))
     swap_all([particles - 1])
     swapped = [far[distance] for distance in range(1, particles)]

time: 42.1 us -> 42 us (level)
    ppermute x5 -> x4, starting transfers between devices: 1.09 us -> 1.14 us  [swap_all(): swapped = lax.ppermute(jnp.concatenate(group, axis=0), 'dom', swap)]
  transfers between devices with their start and end apart: 12 -> 11, of which waited for: 4 -> 3; matrix products, arithmetic and copies ran while one was open for 0% -> 0% of each run, Pallas kernels for 8% -> 8%
where the time goes in v7:
time: 42 us; the launch traced here: 41.8 us
  starting transfers between devices  12.7 us (30%)
  blocking collectives  12.1 us (29%)
  waiting for transfers between devices  8.93 us (21%)
  Pallas kernels  7.12 us (17%)
  local copies, waits for them, and re-layouts  0.76 us (2%)
    all_to_all x1, blocking collectives, spread_body(): return lax.all_to_all(result, 'tok', 0, 0, tiled=True)  12.1 us
    ppermute x6, starting transfers between devices, beside(): return lax.ppermute(block, 'tok', [(t, t ^ k) for t in range(particles)])  11.1 us
    ppermute x6, waiting for transfers between devices, beside(): return lax.ppermute(block, 'tok', [(t, t ^ k) for t in range(particles)])  8.92 us
    pallas_call x1, Pallas kernels, layers(): pl.pallas_call(kernel, out_shape=jax.ShapeDtypeStruct((sources, rows, wid...  3.2 us
    pallas_call x1, Pallas kernels, prepare(): pl.pallas_call(kernel, out_shape=(part, part, jax.ShapeDtypeStruct(own.sh...  1.79 us
    pallas_call x1, Pallas kernels, first_half(): pl.pallas_call(kernel, out_shape=(wide, wide, wide, tall, tall), in_specs...  1.49 us
    ppermute x4, starting transfers between devices, swap_all(): swapped = lax.ppermute(jnp.concatenate(group, axis=0), 'dom', swap)  1.14 us
  transfers between devices with their start and end apart: 11, of which 3 were waited for; matrix products, arithmetic and copies ran while one was open for 0% of the time, Pallas kernels for 8%

profile of v7, /device:TPU:0, one launch (start us, length us, event | category | flops | bytes accessed | tf_op | source)
XLA Modules:
  0.0 41.8 jit_solution(12853953700312634778)
XLA Ops:
  0.0 0.0 copy-start
  0.0 0.0 copy-start.2
  0.0 0.0 copy-start.3
  0.0 0.5 %collective-permute-start = (bf16[8,16,768]{2,1,0:T(8,128)(2,1)}, bf16[8,16,768]{2,1,0:T(8,128)(2,1)S(1)}, u32[]{:S(2)}, u32[]{:S(2)}) collective-permute-start(bf16[8,16,768]{2,1,0:T(8,128)(2,1)} %own_hbm.1), channel_id=1, source_target_pairs={{0,1},{1,0},{2,3},{3,2},{4,5},{5,4},{6,7},{7,6},{8,9},{9,8},{10,11... | collective-permute-start | bytes 589832 | tf_op jit(solution)/shard_map/ppermute | solution.py:381
  0.5 1.8 %prepare.1 = (bf16[256,128]{1,0:T(8,128)(2,1)S(1)}, bf16[256,128]{1,0:T(8,128)(2,1)S(1)}, bf16[8,16,768]{2,1,0:T(8,128)(2,1)S(1)}, bf16[8,16,768]{2,1,0:T(8,128)(2,1)S(1)}) custom-call(bf16[16,128,128]{2,1,0:T(8,128)(2,1)} %pair_hbm.1, s32[1,128]{1,0:T(1,128)} %bitcast.2, bf16[2,16,128]{2,1,0:T(8,128)(2,1)} %bitcast.5, bf16[8,16,768]{2,1,0:T(8,128)(2,1)} %own_hbm.1, ...), custom_call_target="tpu_custom_call" | custom-call | flops 16777216 | bytes 8000000 | tf_op jit(solution)/shard_map/prepare/pallas_call | solution.py:123
  2.3 0.0 copy-start.1
  2.3 0.0 collective-permute-done.other_ref
  2.3 0.0 copy-done.3
  2.4 0.6 %pack.1 = (bf16[96,128]{1,0:T(8,128)(2,1)S(1)}, bf16[352,128]{1,0:T(8,128)(2,1)S(1)}, bf16[448,128]{1,0:T(8,128)(2,1)S(1)}, bf16[448,128]{1,0:T(8,128)(2,1)S(1)}, bf16[448,128]{1,0:T(8,128)(2,1)S(1)}) custom-call(s32[8]{0:T(128)S(1)} %copy-done.3, bf16[8,16,768]{2,1,0:T(8,128)(2,1)S(1)} %get-tuple-element.19.own_ref, ...), custom_call_target="tpu_custom_call" | custom-call | tf_op jit(solution)/shard_map/pack/pallas_call | solution.py:180
  3.0 2.6 %collective-permute-start.1 = (bf16[448,128]{1,0:T(8,128)(2,1)S(1)}, bf16[448,128]{1,0:T(8,128)(2,1)S(1)}, u32[]{:S(2)}, u32[]{:S(2)}) collective-permute-start(bf16[448,128]{1,0:T(8,128)(2,1)S(1)} %get-tuple-element.24), channel_id=1, source_target_pairs={{0,4},{2,6},{4,0},{6,2},{8,12},{10,14},{12,8},{14,10},{1,5},{3,7},... | collective-permute-start | bytes 344072 | tf_op jit(solution)/shard_map/ppermute | solution.py:379
  5.6 2.6 %collective-permute-start.3 = (bf16[448,128]{1,0:T(8,128)(2,1)S(1)}, bf16[448,128]{1,0:T(8,128)(2,1)S(1)}, u32[]{:S(2)}, u32[]{:S(2)}) collective-permute-start(bf16[448,128]{1,0:T(8,128)(2,1)S(1)} %get-tuple-element.25), channel_id=1, source_target_pairs={{0,8},{2,10},{4,12},{6,14},{8,0},{10,2},{12,4},{14,6},{1,9},{3,11}... | collective-permute-start | bytes 344072 | tf_op jit(solution)/shard_map/ppermute | solution.py:379
  8.2 0.0 collective-permute-start.5
  8.2 1.4 %collective-permute-done.1.refs_1_.refs_2_ = bf16[448,128]{1,0:T(8,128)(2,1)S(1)} collective-permute-done((bf16[448,128]{1,0:T(8,128)(2,1)S(1)}, bf16[448,128]{1,0:T(8,128)(2,1)S(1)}, u32[]{:S(2)}, u32[]{:S(2)}) %collective-permute-start.1) | collective-permute-done | bytes 114720 | tf_op jit(solution)/shard_map/ppermute | solution.py:379
  9.6 3.7 %collective-permute-start.2 = (bf16[704,128]{1,0:T(8,128)(2,1)S(1)}, bf16[704,128]{1,0:T(8,128)(2,1)S(1)}, u32[]{:S(2)}, u32[]{:S(2)}) collective-permute-start(bf16[704,128]{1,0:T(8,128)(2,1)S(1)} %pad_maximum_fusion.2), channel_id=1, source_target_pairs={{0,2},{2,0},{4,6},{6,4},{8,10},{10,8},{12,14},{14,12},{1,3},{3,1},... | collective-permute-start | bytes 540680 | tf_op jit(solution)/shard_map/ppermute | solution.py:379
  13.3 4.1 %collective-permute-done.3.refs_3_.refs_4_ = bf16[448,128]{1,0:T(8,128)(2,1)S(1)} collective-permute-done((bf16[448,128]{1,0:T(8,128)(2,1)S(1)}, bf16[448,128]{1,0:T(8,128)(2,1)S(1)}, u32[]{:S(2)}, u32[]{:S(2)}) %collective-permute-start.3) | collective-permute-done | bytes 114720 | tf_op jit(solution)/shard_map/ppermute | solution.py:379
  17.4 1.6 %collective-permute-start.4 = (bf16[352,128]{1,0:T(8,128)(2,1)S(1)}, bf16[352,128]{1,0:T(8,128)(2,1)S(1)}, u32[]{:S(2)}, u32[]{:S(2)}) collective-permute-start(bf16[352,128]{1,0:T(8,128)(2,1)S(1)} %slice.44), channel_id=1, source_target_pairs={{0,2},{2,0},{4,6},{6,4},{8,10},{10,8},{12,14},{14,12},{1,3},{3,1},... | collective-permute-start | bytes 270344 | tf_op jit(solution)/shard_map/ppermute | solution.py:379
  19.0 0.0 collective-permute-done.5.refs_5_.refs_6_
  19.0 0.6 %collective-permute-start.6 = (bf16[352,128]{1,0:T(8,128)(2,1)S(1)}, bf16[352,128]{1,0:T(8,128)(2,1)S(1)}, u32[]{:S(2)}, u32[]{:S(2)}) collective-permute-start(bf16[352,128]{1,0:T(8,128)(2,1)S(1)} %slice.45), channel_id=1, source_target_pairs={{0,2},{2,0},{4,6},{6,4},{8,10},{10,8},{12,14},{14,12},{1,3},{3,1},... | collective-permute-start | bytes 270344 | tf_op jit(solution)/shard_map/ppermute | solution.py:379
  19.6 0.1 collective-permute-start.8
  19.7 0.5 %collective-permute-start.9 = (bf16[448,128]{1,0:T(8,128)(2,1)S(1)}, bf16[448,128]{1,0:T(8,128)(2,1)S(1)}, u32[]{:S(2)}, u32[]{:S(2)}) collective-permute-start(bf16[448,128]{1,0:T(8,128)(2,1)S(1)} %collective-permute-done.5.refs_5_.refs_6_), channel_id=1, source_target_pairs={{0,1},{1,0},{2,3},{3,2},{4,5},{5,4},{6,7},{7,6},{8,9},{9,8},{10,11... | collective-permute-start | bytes 344072 | tf_op jit(solution)/shard_map/ppermute | solution.py:398
  20.2 3.4 %collective-permute-done.6.refs_6_.refs_7_ = bf16[352,128]{1,0:T(8,128)(2,1)S(1)} collective-permute-done((bf16[352,128]{1,0:T(8,128)(2,1)S(1)}, bf16[352,128]{1,0:T(8,128)(2,1)S(1)}, u32[]{:S(2)}, u32[]{:S(2)}) %collective-permute-start.6) | collective-permute-done | bytes 90144 | tf_op jit(solution)/shard_map/ppermute | solution.py:379
  23.6 0.0 collective-permute-start.10
  23.6 0.0 collective-permute-done.4.refs_4_.refs_5_
  23.6 0.0 collective-permute-done.2
  23.7 0.6 %collective-permute-start.7 = (bf16[1056,128]{1,0:T(8,128)(2,1)S(1)}, bf16[1056,128]{1,0:T(8,128)(2,1)S(1)}, u32[]{:S(2)}, u32[]{:S(2)}) collective-permute-start(bf16[1056,128]{1,0:T(8,128)(2,1)S(1)} %pad_maximum_fusion), channel_id=1, source_target_pairs={{0,1},{1,0},{2,3},{3,2},{4,5},{5,4},{6,7},{7,6},{8,9},{9,8},{10,11... | collective-permute-start | bytes 811016 | tf_op jit(solution)/shard_map/ppermute | solution.py:398
  24.2 0.0 copy-done
  24.2 0.0 copy-done.2
  24.3 1.5 %first_half.1 = (bf16[128,768]{1,0:T(8,128)(2,1)S(1)}, bf16[128,768]{1,0:T(8,128)(2,1)S(1)}, bf16[128,768]{1,0:T(8,128)(2,1)S(1)}, bf16[768,128]{1,0:T(8,128)(2,1)S(1)}, bf16[768,128]{1,0:T(8,128)(2,1)S(1)}) custom-call(s32[1,128]{1,0:T(1,128)S(1)} %bitcast.3, bf16[2,768,2304]{2,1,0:T(8,128)(2,1)S(1)} %copy-done, ...), custom_call_target="tpu_custom_call" | custom-call | flops 452984832 | bytes 4718592 | tf_op jit(solution)/shard_map/first_half/pallas_call | solution.py:294
  25.7 0.0 collective-permute-done.8
  25.8 0.0 collective-permute-done.7
  25.8 0.0 collective-permute-done.9.refs_14_
  25.8 0.0 collective-permute-done.10.refs_15_
  25.8 0.0 copy-done.1
  25.9 3.2 %layers.1 = bf16[8,16,768]{2,1,0:T(8,128)(2,1)S(1)} custom-call(s32[1,128]{1,0:T(1,128)S(1)} %bitcast.4, bf16[2,768,2304]{2,1,0:T(8,128)(2,1)S(1)} %copy-done, bf16[2,768,768]{2,1,0:T(8,128)(2,1)S(1)} %copy-done.1, bf16[128,768]{1,0:T(8,128)(2,1)S(1)} %get-tuple-element.27.x_ref, bf16[128,768]{1,0:T(8,128)(2,1)S(1)} %get-tuple-element.28.q_in, ...), custom_call_target="tpu_custom_call" | custom-call | flops 1056964608 | bytes 5898240 | tf_op jit(solution)/shard_map/layers/pallas_call | solution.py:348
  29.1 12.1 %all_to_all.5 = bf16[8,16,768]{2,1,0:T(8,128)(2,1)S(1)} all-to-all(bf16[8,16,768]{2,1,0:T(8,128)(2,1)S(1)} %layers.1), channel_id=1, replica_groups=mesh['groups'=2,'tok'=8,'dom'=2] {'tok'}, dimensions={0} | all-to-all | bytes 393216 | tf_op jit(solution)/shard_map/all_to_all | solution.py:412
  41.1 0.7 %copy.10 = bf16[8,16,768]{2,1,0:T(8,128)(2,1)} copy(bf16[8,16,768]{2,1,0:T(8,128)(2,1)S(1)} %all_to_all.5) | data formatting | bytes 393216
  (9 shorter events, 0.1 us)
Async XLA Ops:
  0.0 24.2 %copy-start = (bf16[2,768,2304]{2,1,0:T(8,128)(2,1)S(1)}, bf16[2,768,2304]{2,1,0:T(8,128)(2,1)}, u32[]{:S(2)}) copy-start(bf16[2,768,2304]{2,1,0:T(8,128)(2,1)} %wq_ref.1) | copy-start | bytes 21233668
  0.0 24.2 %copy-start.2 = (s32[128]{0:T(128)S(1)}, s32[128]{0:T(128)}, u32[]{:S(2)}) copy-start(s32[128]{0:T(128)} %param.12) | copy-start | bytes 1540
  0.0 2.3 %copy-start.3 = (s32[8]{0:T(128)S(1)}, s32[8]{0:T(128)}, u32[]{:S(2)}) copy-start(s32[8]{0:T(128)} %anc_ref.1) | copy-start | bytes 100
  0.0 2.3 %collective-permute-start = (bf16[8,16,768]{2,1,0:T(8,128)(2,1)}, bf16[8,16,768]{2,1,0:T(8,128)(2,1)S(1)}, u32[]{:S(2)}, u32[]{:S(2)}) collective-permute-start(bf16[8,16,768]{2,1,0:T(8,128)(2,1)} %own_hbm.1), channel_id=1, source_target_pairs={{0,1},{1,0},{2,3},{3,2},{4,5},{5,4},{6,7},{7,6},{8,9},{9,8},{10,11... | collective-permute-start | bytes 589832 | tf_op jit(solution)/shard_map/ppermute | solution.py:381
  2.3 23.5 %copy-start.1 = (bf16[2,768,768]{2,1,0:T(8,128)(2,1)S(1)}, bf16[2,768,768]{2,1,0:T(8,128)(2,1)}, u32[]{:S(2)}) copy-start(bf16[2,768,768]{2,1,0:T(8,128)(2,1)} %wo_ref.1) | copy-start | bytes 7077892
  3.0 6.6 %collective-permute-start.1 = (bf16[448,128]{1,0:T(8,128)(2,1)S(1)}, bf16[448,128]{1,0:T(8,128)(2,1)S(1)}, u32[]{:S(2)}, u32[]{:S(2)}) collective-permute-start(bf16[448,128]{1,0:T(8,128)(2,1)S(1)} %get-tuple-element.24), channel_id=1, source_target_pairs={{0,4},{2,6},{4,0},{6,2},{8,12},{10,14},{12,8},{14,10},{1,5},{3,7},... | collective-permute-start | bytes 344072 | tf_op jit(solution)/shard_map/ppermute | solution.py:379
  5.6 11.8 %collective-permute-start.3 = (bf16[448,128]{1,0:T(8,128)(2,1)S(1)}, bf16[448,128]{1,0:T(8,128)(2,1)S(1)}, u32[]{:S(2)}, u32[]{:S(2)}) collective-permute-start(bf16[448,128]{1,0:T(8,128)(2,1)S(1)} %get-tuple-element.25), channel_id=1, source_target_pairs={{0,8},{2,10},{4,12},{6,14},{8,0},{10,2},{12,4},{14,6},{1,9},{3,11}... | collective-permute-start | bytes 344072 | tf_op jit(solution)/shard_map/ppermute | solution.py:379
  8.2 10.8 %collective-permute-start.5 = (bf16[448,128]{1,0:T(8,128)(2,1)S(1)}, bf16[448,128]{1,0:T(8,128)(2,1)S(1)}, u32[]{:S(2)}, u32[]{:S(2)}) collective-permute-start(bf16[448,128]{1,0:T(8,128)(2,1)S(1)} %get-tuple-element.26), channel_id=1, source_target_pairs={{0,12},{2,14},{4,8},{6,10},{8,4},{10,6},{12,0},{14,2},{1,13},{3,15... | collective-permute-start | bytes 344072 | tf_op jit(solution)/shard_map/ppermute | solution.py:379
  9.6 14.0 %collective-permute-start.2 = (bf16[704,128]{1,0:T(8,128)(2,1)S(1)}, bf16[704,128]{1,0:T(8,128)(2,1)S(1)}, u32[]{:S(2)}, u32[]{:S(2)}) collective-permute-start(bf16[704,128]{1,0:T(8,128)(2,1)S(1)} %pad_maximum_fusion.2), channel_id=1, source_target_pairs={{0,2},{2,0},{4,6},{6,4},{8,10},{10,8},{12,14},{14,12},{1,3},{3,1},... | collective-permute-start | bytes 540680 | tf_op jit(solution)/shard_map/ppermute | solution.py:379
  17.4 6.2 %collective-permute-start.4 = (bf16[352,128]{1,0:T(8,128)(2,1)S(1)}, bf16[352,128]{1,0:T(8,128)(2,1)S(1)}, u32[]{:S(2)}, u32[]{:S(2)}) collective-permute-start(bf16[352,128]{1,0:T(8,128)(2,1)S(1)} %slice.44), channel_id=1, source_target_pairs={{0,2},{2,0},{4,6},{6,4},{8,10},{10,8},{12,14},{14,12},{1,3},{3,1},... | collective-permute-start | bytes 270344 | tf_op jit(solution)/shard_map/ppermute | solution.py:379
  19.0 4.6 %collective-permute-start.6 = (bf16[352,128]{1,0:T(8,128)(2,1)S(1)}, bf16[352,128]{1,0:T(8,128)(2,1)S(1)}, u32[]{:S(2)}, u32[]{:S(2)}) collective-permute-start(bf16[352,128]{1,0:T(8,128)(2,1)S(1)} %slice.45), channel_id=1, source_target_pairs={{0,2},{2,0},{4,6},{6,4},{8,10},{10,8},{12,14},{14,12},{1,3},{3,1},... | collective-permute-start | bytes 270344 | tf_op jit(solution)/shard_map/ppermute | solution.py:379
  19.6 6.1 %collective-permute-start.8 = (bf16[896,128]{1,0:T(8,128)(2,1)S(1)}, bf16[896,128]{1,0:T(8,128)(2,1)S(1)}, u32[]{:S(2)}, u32[]{:S(2)}) collective-permute-start(bf16[896,128]{1,0:T(8,128)(2,1)S(1)} %pad_maximum_fusion.1), channel_id=1, source_target_pairs={{0,1},{1,0},{2,3},{3,2},{4,5},{5,4},{6,7},{7,6},{8,9},{9,8},{10,11... | collective-permute-start | bytes 688136 | tf_op jit(solution)/shard_map/ppermute | solution.py:398
  19.7 6.1 %collective-permute-start.9 = (bf16[448,128]{1,0:T(8,128)(2,1)S(1)}, bf16[448,128]{1,0:T(8,128)(2,1)S(1)}, u32[]{:S(2)}, u32[]{:S(2)}) collective-permute-start(bf16[448,128]{1,0:T(8,128)(2,1)S(1)} %collective-permute-done.5.refs_5_.refs_6_), channel_id=1, source_target_pairs={{0,1},{1,0},{2,3},{3,2},{4,5},{5,4},{6,7},{7,6},{8,9},{9,8},{10,11... | collective-permute-start | bytes 344072 | tf_op jit(solution)/shard_map/ppermute | solution.py:398
  23.6 2.2 %collective-permute-start.10 = (bf16[352,128]{1,0:T(8,128)(2,1)S(1)}, bf16[352,128]{1,0:T(8,128)(2,1)S(1)}, u32[]{:S(2)}, u32[]{:S(2)}) collective-permute-start(bf16[352,128]{1,0:T(8,128)(2,1)S(1)} %collective-permute-done.6.refs_6_.refs_7_), channel_id=1, source_target_pairs={{0,1},{1,0},{2,3},{3,2},{4,5},{5,4},{6,7},{7,6},{8,9},{9,8},{10,11... | collective-permute-start | bytes 270344 | tf_op jit(solution)/shard_map/ppermute | solution.py:398
  23.7 2.1 %collective-permute-start.7 = (bf16[1056,128]{1,0:T(8,128)(2,1)S(1)}, bf16[1056,128]{1,0:T(8,128)(2,1)S(1)}, u32[]{:S(2)}, u32[]{:S(2)}) collective-permute-start(bf16[1056,128]{1,0:T(8,128)(2,1)S(1)} %pad_maximum_fusion), channel_id=1, source_target_pairs={{0,1},{1,0},{2,3},{3,2},{4,5},{5,4},{6,7},{7,6},{8,9},{9,8},{10,11... | collective-permute-start | bytes 811016 | tf_op jit(solution)/shard_map/ppermute | solution.py:398

commit v8 on v7

--- a/solution.py
+++ b/solution.py
@@ -80,68 +80,56 @@
     return pl.BlockSpec(memory_space=pltpu.SMEM)
 
 
-def prepare(pair, mask_row, w_rows, own, noise, w_qkv):
+def make_bias(pair, mask_row, w_rows, w_qkv, side):
     rows, keys, channels = pair.shape
     layer_count, heads, _ = w_rows.shape
     half = heads // 2
-    blocks = layer_count * heads
-
-    def kernel(
-        pair_hbm, mask_hbm, w_hbm, own_hbm, noise_hbm, wq_hbm,
-        near_ref, far_ref, own_ref, noise_ref, pair_ref, mask_ref, w_ref, rows_ref, sem,
-    ):
+    blocks = layer_count * half
+
+    def kernel(pair_hbm, mask_hbm, w_hbm, wq_hbm, out_ref, pair_ref, mask_ref, w_ref, rows_ref, sem):
         copies = [
             pltpu.make_async_copy(mask_hbm, mask_ref, sem.at[0]),
             pltpu.make_async_copy(w_hbm, w_ref, sem.at[1]),
             pltpu.make_async_copy(pair_hbm, pair_ref, sem.at[2]),
-            pltpu.make_async_copy(own_hbm, own_ref, sem.at[3]),
-            pltpu.make_async_copy(noise_hbm, noise_ref, sem.at[4]),
         ]
         for copy in copies:
             copy.start()
-        copies[0].wait()
-        copies[1].wait()
+        for copy in copies:
+            copy.wait()
         penalty = jnp.where(mask_ref[...] > 0, 0.0, MASKED).astype(jnp.float32)
-        w_all = w_ref[...].reshape(blocks, channels)
-        copies[2].wait()
-        terms = across(w_all, pair_ref[...].reshape(rows * keys, channels))
+        low = lax.axis_index("dom") == side
+        part = jnp.concatenate(
+            [
+                jnp.where(low, w[:half], w[half:])
+                for w in (w_ref[l].astype(jnp.float32) for l in range(layer_count))
+            ],
+            axis=0,
+        ).astype(jnp.bfloat16)
+        terms = across(part, pair_ref[...].reshape(rows * keys, channels))
         for i in range(rows):
             piece = terms[:, i * keys : (i + 1) * keys] + penalty
             rows_ref[:, i, :] = piece - jnp.max(piece, axis=-1, keepdims=True)
-        dom = lax.axis_index("dom")
-        for l in range(layer_count):
-            for h in range(half):
-                at = (l * half + h) * rows
-                near = l * heads + dom * half + h
-                far = l * heads + (1 - dom) * half + h
-                near_ref[at : at + rows, :] = rows_ref[near].astype(jnp.bfloat16)
-                far_ref[at : at + rows, :] = rows_ref[far].astype(jnp.bfloat16)
-        for copy in copies[3:]:
-            copy.wait()
-
-    part = jax.ShapeDtypeStruct((blocks // 2 * rows, keys), jnp.bfloat16)
+        for h in range(blocks):
+            out_ref[h * rows : (h + 1) * rows, :] = rows_ref[h].astype(jnp.bfloat16)
+
     return pl.pallas_call(
         kernel,
-        out_shape=(
-            part, part,
-            jax.ShapeDtypeStruct(own.shape, own.dtype),
-            jax.ShapeDtypeStruct(noise.shape, noise.dtype),
-        ),
-        in_specs=[in_hbm()] * 6,
-        out_specs=(whole_vmem(),) * 4,
+        out_shape=jax.ShapeDtypeStruct((blocks * rows, keys), jnp.bfloat16),
+        in_specs=[in_hbm()] * 4,
+        out_specs=whole_vmem(),
         scratch_shapes=[
             pltpu.VMEM(pair.shape, pair.dtype),
             pltpu.VMEM(mask_row.shape, mask_row.dtype),
             pltpu.VMEM(w_rows.shape, w_rows.dtype),
             pltpu.VMEM((blocks, rows, keys), jnp.float32),
-            pltpu.SemaphoreType.DMA((5,)),
+            pltpu.SemaphoreType.DMA((3,)),
         ],
         cost_estimate=pl.CostEstimate(
             flops=2 * blocks * rows * keys * channels, transcendentals=0, bytes_accessed=8000000
         ),
         compiler_params=pltpu.CompilerParams(vmem_limit_bytes=6 * 2**20),
-        name="prepare",
-    )(*(stay(a) for a in (pair, mask_row, w_rows, own, noise, w_qkv)))
+        name="make_bias",
+    )(*(stay(a) for a in (pair, mask_row, w_rows, w_qkv)))
 
 
 def block_source(position):
@@ -379,12 +367,13 @@
         return lax.ppermute(block, "tok", [(t, t ^ k) for t in range(particles)])
 
     other_states = lax.ppermute(states, "dom", swap)
-    near, rest, own, local_noise = prepare(
-        pair, mask_row, w_pair.transpose(0, 2, 1), states, noise, w_qkv
-    )
-    kept, neighbour, *sent = pack(ancestors, own, other_states, local_noise, near)
+    w_rows = w_pair.transpose(0, 2, 1)
+    near = make_bias(pair, mask_row, w_rows, w_qkv, 0)
+    kept, neighbour, *sent = pack(ancestors, states, other_states, noise, near)
     ahead = rows * (width // LANES)
     passing = range(2, particles, 2)
+    late_pair, _ = lax.optimization_barrier((pair, kept))
+    rest = make_bias(late_pair, mask_row, w_rows, w_qkv, 1)
     blocks = {k: beside(block, k) for k, block in zip(passing, sent)}
     blocks[1], blocks[3] = apart(
         beside(jnp.concatenate([neighbour, blocks[2][ahead:]], axis=0)), [neighbour, blocks[2][ahead:]]

time: 42 us -> 41.9 us (level)
  waiting for transfers between devices: 8.93 us -> 7.48 us
  Pallas kernels: 7.12 us -> 8.54 us
    ppermute x6, waiting for transfers between devices: 8.92 us -> 7.46 us  [beside(): return lax.ppermute(block, 'tok', [(t, t ^ k) for t in range(particles)])]
    pallas_call x1 -> x2, Pallas kernels: 1.79 us -> 3.21 us  [make_bias(): pl.pallas_call(kernel, out_shape=jax.ShapeDtypeStruct((blocks * rows, key...]
  transfers between devices with their start and end apart: 11 -> 11, of which waited for: 3 -> 3; matrix products, arithmetic and copies ran while one was open for 0% -> 0% of each run, Pallas kernels for 8% -> 11%
where the time goes in v8:
time: 41.9 us; the launch traced here: 41.7 us
  starting transfers between devices  12.6 us (30%)
  blocking collectives  12 us (29%)
  Pallas kernels  8.54 us (20%)
  waiting for transfers between devices  7.48 us (18%)
  local copies, waits for them, and re-layouts  0.78 us (2%)
    all_to_all x1, blocking collectives, spread_body(): return lax.all_to_all(result, 'tok', 0, 0, tiled=True)  12 us
    ppermute x6, starting transfers between devices, beside(): return lax.ppermute(block, 'tok', [(t, t ^ k) for t in range(particles)])  11 us
    ppermute x6, waiting for transfers between devices, beside(): return lax.ppermute(block, 'tok', [(t, t ^ k) for t in range(particles)])  7.46 us
    pallas_call x2, Pallas kernels, make_bias(): pl.pallas_call(kernel, out_shape=jax.ShapeDtypeStruct((blocks * rows, key...  3.21 us
    pallas_call x1, Pallas kernels, layers(): pl.pallas_call(kernel, out_shape=jax.ShapeDtypeStruct((sources, rows, wid...  3.2 us
    pallas_call x1, Pallas kernels, first_half(): pl.pallas_call(kernel, out_shape=(wide, wide, wide, tall, tall), in_specs...  1.5 us
    ppermute x4, starting transfers between devices, swap_all(): swapped = lax.ppermute(jnp.concatenate(group, axis=0), 'dom', swap)  1.14 us
  transfers between devices with their start and end apart: 11, of which 3 were waited for; matrix products, arithmetic and copies ran while one was open for 0% of the time, Pallas kernels for 11%

profile of v8, /device:TPU:0, one launch (start us, length us, event | category | flops | bytes accessed | tf_op | source)
XLA Modules:
  0.0 41.7 jit_solution(10897122459592413655)
XLA Ops:
  0.0 0.0 copy-start.1
  0.0 0.0 copy-start.2
  0.0 0.0 copy-start.4
  0.0 0.5 %collective-permute-start = (bf16[8,16,768]{2,1,0:T(8,128)(2,1)}, bf16[8,16,768]{2,1,0:T(8,128)(2,1)S(1)}, u32[]{:S(2)}, u32[]{:S(2)}) collective-permute-start(bf16[8,16,768]{2,1,0:T(8,128)(2,1)} %own_ref.1), channel_id=1, source_target_pairs={{0,1},{1,0},{2,3},{3,2},{4,5},{5,4},{6,7},{7,6},{8,9},{9,8},{10,11... | collective-permute-start | bytes 589832 | tf_op jit(solution)/shard_map/ppermute | solution.py:369
  0.5 0.0 slice-start
  0.5 1.6 %make_bias.2.bias_ref.near_ref.refs_0_ = bf16[256,128]{1,0:T(8,128)(2,1)S(1)} custom-call(bf16[16,128,128]{2,1,0:T(8,128)(2,1)} %pair_hbm.2, s32[1,128]{1,0:T(1,128)} %bitcast.4, bf16[2,16,128]{2,1,0:T(8,128)(2,1)} %bitcast.8, bf16[2,768,2304]{2,1,0:T(8,128)(2,1)} %wq_ref.1), custom_call_target="tpu_custom_call" | custom-call | flops 8388608 | bytes 8000000 | tf_op jit(solution)/shard_map/make_bias/pallas_call | solution.py:115
  2.1 0.0 copy-start.3
  2.2 0.0 collective-permute-done.other_ref
  2.2 0.0 copy-done.1
  2.2 0.0 copy-done.2
  2.2 0.0 copy-done.4
  2.2 0.6 %pack.1 = (bf16[96,128]{1,0:T(8,128)(2,1)S(1)}, bf16[352,128]{1,0:T(8,128)(2,1)S(1)}, bf16[448,128]{1,0:T(8,128)(2,1)S(1)}, bf16[448,128]{1,0:T(8,128)(2,1)S(1)}, bf16[448,128]{1,0:T(8,128)(2,1)S(1)}) custom-call(s32[8]{0:T(128)S(1)} %copy-done.4, bf16[8,16,768]{2,1,0:T(8,128)(2,1)S(1)} %copy-done.1, bf16[8,16,768]{2,1,0:T(8,128)(2,1)S(1)} %collective-permute-done.other_ref, ...), custom_call_target="tpu_custom_call" | custom-call | tf_op jit(solution)/shard_map/pack/pallas_call | solution.py:168
  2.8 2.7 %collective-permute-start.1 = (bf16[448,128]{1,0:T(8,128)(2,1)S(1)}, bf16[448,128]{1,0:T(8,128)(2,1)S(1)}, u32[]{:S(2)}, u32[]{:S(2)}) collective-permute-start(bf16[448,128]{1,0:T(8,128)(2,1)S(1)} %get-tuple-element.18), channel_id=1, source_target_pairs={{0,4},{2,6},{4,0},{6,2},{8,12},{10,14},{12,8},{14,10},{1,5},{3,7},... | collective-permute-start | bytes 344072 | tf_op jit(solution)/shard_map/ppermute | solution.py:367
  5.5 2.6 %collective-permute-start.3 = (bf16[448,128]{1,0:T(8,128)(2,1)S(1)}, bf16[448,128]{1,0:T(8,128)(2,1)S(1)}, u32[]{:S(2)}, u32[]{:S(2)}) collective-permute-start(bf16[448,128]{1,0:T(8,128)(2,1)S(1)} %get-tuple-element.19), channel_id=1, source_target_pairs={{0,8},{2,10},{4,12},{6,14},{8,0},{10,2},{12,4},{14,6},{1,9},{3,11}... | collective-permute-start | bytes 344072 | tf_op jit(solution)/shard_map/ppermute | solution.py:367
  8.1 0.0 collective-permute-start.5
  8.1 1.2 %collective-permute-done.1.refs_1_.refs_2_ = bf16[448,128]{1,0:T(8,128)(2,1)S(1)} collective-permute-done((bf16[448,128]{1,0:T(8,128)(2,1)S(1)}, bf16[448,128]{1,0:T(8,128)(2,1)S(1)}, u32[]{:S(2)}, u32[]{:S(2)}) %collective-permute-start.1) | collective-permute-done | bytes 114720 | tf_op jit(solution)/shard_map/ppermute | solution.py:367
  9.3 3.6 %collective-permute-start.2 = (bf16[704,128]{1,0:T(8,128)(2,1)S(1)}, bf16[704,128]{1,0:T(8,128)(2,1)S(1)}, u32[]{:S(2)}, u32[]{:S(2)}) collective-permute-start(bf16[704,128]{1,0:T(8,128)(2,1)S(1)} %pad_maximum_fusion.2), channel_id=1, source_target_pairs={{0,2},{2,0},{4,6},{6,4},{8,10},{10,8},{12,14},{14,12},{1,3},{3,1},... | collective-permute-start | bytes 540680 | tf_op jit(solution)/shard_map/ppermute | solution.py:367
  12.9 0.0 slice-start.1
  12.9 1.6 %make_bias.3.refs_8_ = bf16[256,128]{1,0:T(8,128)(2,1)S(1)} custom-call(bf16[16,128,128]{2,1,0:T(8,128)(2,1)} %pair_hbm.2, s32[1,128]{1,0:T(1,128)} %bitcast.5, bf16[2,16,128]{2,1,0:T(8,128)(2,1)} %bitcast.9, bf16[2,768,2304]{2,1,0:T(8,128)(2,1)} %wq_ref.1), custom_call_target="tpu_custom_call" | custom-call | flops 8388608 | bytes 8000000 | tf_op jit(solution)/shard_map/make_bias/pallas_call | solution.py:115
  14.5 0.0 copy-start
  14.5 2.8 %collective-permute-done.3.refs_3_.refs_4_ = bf16[448,128]{1,0:T(8,128)(2,1)S(1)} collective-permute-done((bf16[448,128]{1,0:T(8,128)(2,1)S(1)}, bf16[448,128]{1,0:T(8,128)(2,1)S(1)}, u32[]{:S(2)}, u32[]{:S(2)}) %collective-permute-start.3) | collective-permute-done | bytes 114720 | tf_op jit(solution)/shard_map/ppermute | solution.py:367
  17.4 1.6 %collective-permute-start.4 = (bf16[352,128]{1,0:T(8,128)(2,1)S(1)}, bf16[352,128]{1,0:T(8,128)(2,1)S(1)}, u32[]{:S(2)}, u32[]{:S(2)}) collective-permute-start(bf16[352,128]{1,0:T(8,128)(2,1)S(1)} %slice.44), channel_id=1, source_target_pairs={{0,2},{2,0},{4,6},{6,4},{8,10},{10,8},{12,14},{14,12},{1,3},{3,1},... | collective-permute-start | bytes 270344 | tf_op jit(solution)/shard_map/ppermute | solution.py:367
  18.9 0.0 collective-permute-done.5.refs_5_.refs_6_
  19.0 0.6 %collective-permute-start.6 = (bf16[352,128]{1,0:T(8,128)(2,1)S(1)}, bf16[352,128]{1,0:T(8,128)(2,1)S(1)}, u32[]{:S(2)}, u32[]{:S(2)}) collective-permute-start(bf16[352,128]{1,0:T(8,128)(2,1)S(1)} %slice.45), channel_id=1, source_target_pairs={{0,2},{2,0},{4,6},{6,4},{8,10},{10,8},{12,14},{14,12},{1,3},{3,1},... | collective-permute-start | bytes 270344 | tf_op jit(solution)/shard_map/ppermute | solution.py:367
  19.5 0.1 collective-permute-start.8
  19.6 0.5 %collective-permute-start.9 = (bf16[448,128]{1,0:T(8,128)(2,1)S(1)}, bf16[448,128]{1,0:T(8,128)(2,1)S(1)}, u32[]{:S(2)}, u32[]{:S(2)}) collective-permute-start(bf16[448,128]{1,0:T(8,128)(2,1)S(1)} %collective-permute-done.5.refs_5_.refs_6_), channel_id=1, source_target_pairs={{0,1},{1,0},{2,3},{3,2},{4,5},{5,4},{6,7},{7,6},{8,9},{9,8},{10,11... | collective-permute-start | bytes 344072 | tf_op jit(solution)/shard_map/ppermute | solution.py:387
  20.1 3.4 %collective-permute-done.6.refs_6_.refs_7_ = bf16[352,128]{1,0:T(8,128)(2,1)S(1)} collective-permute-done((bf16[352,128]{1,0:T(8,128)(2,1)S(1)}, bf16[352,128]{1,0:T(8,128)(2,1)S(1)}, u32[]{:S(2)}, u32[]{:S(2)}) %collective-permute-start.6) | collective-permute-done | bytes 90144 | tf_op jit(solution)/shard_map/ppermute | solution.py:367
  23.5 0.0 collective-permute-start.10
  23.5 0.0 collective-permute-done.4.refs_4_.refs_5_
  23.6 0.0 collective-permute-done.2
  23.6 0.6 %collective-permute-start.7 = (bf16[1056,128]{1,0:T(8,128)(2,1)S(1)}, bf16[1056,128]{1,0:T(8,128)(2,1)S(1)}, u32[]{:S(2)}, u32[]{:S(2)}) collective-permute-start(bf16[1056,128]{1,0:T(8,128)(2,1)S(1)} %pad_maximum_fusion), channel_id=1, source_target_pairs={{0,1},{1,0},{2,3},{3,2},{4,5},{5,4},{6,7},{7,6},{8,9},{9,8},{10,11... | collective-permute-start | bytes 811016 | tf_op jit(solution)/shard_map/ppermute | solution.py:387
  24.2 0.0 slice-done
  24.2 0.0 copy-done.3
  24.2 0.0 slice-done.1
  24.2 1.5 %first_half.1 = (bf16[128,768]{1,0:T(8,128)(2,1)S(1)}, bf16[128,768]{1,0:T(8,128)(2,1)S(1)}, bf16[128,768]{1,0:T(8,128)(2,1)S(1)}, bf16[768,128]{1,0:T(8,128)(2,1)S(1)}, bf16[768,128]{1,0:T(8,128)(2,1)S(1)}) custom-call(s32[1,128]{1,0:T(1,128)S(1)} %bitcast.6, bf16[2,768,2304]{2,1,0:T(8,128)(2,1)S(1)} %bitcast.3, ...), custom_call_target="tpu_custom_call" | custom-call | flops 452984832 | bytes 4718592 | tf_op jit(solution)/shard_map/first_half/pallas_call | solution.py:282
  25.7 0.0 collective-permute-done.8
  25.7 0.0 collective-permute-done.7
  25.8 0.0 collective-permute-done.9.refs_14_
  25.8 0.0 collective-permute-done.10.refs_15_
  25.8 0.0 copy-done
  25.8 3.2 %layers.1 = bf16[8,16,768]{2,1,0:T(8,128)(2,1)S(1)} custom-call(s32[1,128]{1,0:T(1,128)S(1)} %bitcast.7, bf16[2,768,2304]{2,1,0:T(8,128)(2,1)S(1)} %bitcast.3, bf16[2,768,768]{2,1,0:T(8,128)(2,1)S(1)} %copy-done, bf16[128,768]{1,0:T(8,128)(2,1)S(1)} %get-tuple-element.21.x_ref, bf16[128,768]{1,0:T(8,128)(2,1)S(1)} %get-tuple-element.22.q_in, ...), custom_call_target="tpu_custom_call" | custom-call | flops 1056964608 | bytes 5898240 | tf_op jit(solution)/shard_map/layers/pallas_call | solution.py:336
  29.0 12.0 %all_to_all.5 = bf16[8,16,768]{2,1,0:T(8,128)(2,1)S(1)} all-to-all(bf16[8,16,768]{2,1,0:T(8,128)(2,1)S(1)} %layers.1), channel_id=1, replica_groups=mesh['groups'=2,'tok'=8,'dom'=2] {'tok'}, dimensions={0} | all-to-all | bytes 393216 | tf_op jit(solution)/shard_map/all_to_all | solution.py:401
  41.0 0.7 %copy.10 = bf16[8,16,768]{2,1,0:T(8,128)(2,1)} copy(bf16[8,16,768]{2,1,0:T(8,128)(2,1)S(1)} %all_to_all.5) | data formatting | bytes 393216
  (10 shorter events, 0.1 us)
Async XLA Ops:
  0.0 2.2 %copy-start.1 = (bf16[8,16,768]{2,1,0:T(8,128)(2,1)S(1)}, bf16[8,16,768]{2,1,0:T(8,128)(2,1)}, u32[]{:S(2)}) copy-start(bf16[8,16,768]{2,1,0:T(8,128)(2,1)} %own_ref.1) | copy-start | bytes 589828
  0.0 2.2 %copy-start.2 = (bf16[8,16,768]{2,1,0:T(8,128)(2,1)S(1)}, bf16[8,16,768]{2,1,0:T(8,128)(2,1)}, u32[]{:S(2)}) copy-start(bf16[8,16,768]{2,1,0:T(8,128)(2,1)} %noise_ref.1) | copy-start | bytes 589828
  0.0 2.2 %copy-start.4 = (s32[8]{0:T(128)S(1)}, s32[8]{0:T(128)}, u32[]{:S(2)}) copy-start(s32[8]{0:T(128)} %anc_ref.1) | copy-start | bytes 100
  0.0 2.1 %collective-permute-start = (bf16[8,16,768]{2,1,0:T(8,128)(2,1)}, bf16[8,16,768]{2,1,0:T(8,128)(2,1)S(1)}, u32[]{:S(2)}, u32[]{:S(2)}) collective-permute-start(bf16[8,16,768]{2,1,0:T(8,128)(2,1)} %own_ref.1), channel_id=1, source_target_pairs={{0,1},{1,0},{2,3},{3,2},{4,5},{5,4},{6,7},{7,6},{8,9},{9,8},{10,11... | collective-permute-start | bytes 589832 | tf_op jit(solution)/shard_map/ppermute | solution.py:369
  0.5 23.6 %slice-start = ((s8[7077888]{0:T(1024)(128)(4,1)}), s8[4194304]{0:T(1024)(128)(4,1)S(1)}, s32[]{:S(2)}) async-start(s8[7077888]{0:T(1024)(128)(4,1)} %bitcast.2), calls=%async_computation.1 | async-start | bytes 8388608
  2.1 22.0 %copy-start.3 = (s32[128]{0:T(128)S(1)}, s32[128]{0:T(128)}, u32[]{:S(2)}) copy-start(s32[128]{0:T(128)} %param.12) | copy-start | bytes 1540
  2.8 6.5 %collective-permute-start.1 = (bf16[448,128]{1,0:T(8,128)(2,1)S(1)}, bf16[448,128]{1,0:T(8,128)(2,1)S(1)}, u32[]{:S(2)}, u32[]{:S(2)}) collective-permute-start(bf16[448,128]{1,0:T(8,128)(2,1)S(1)} %get-tuple-element.18), channel_id=1, source_target_pairs={{0,4},{2,6},{4,0},{6,2},{8,12},{10,14},{12,8},{14,10},{1,5},{3,7},... | collective-permute-start | bytes 344072 | tf_op jit(solution)/shard_map/ppermute | solution.py:367
  5.5 11.8 %collective-permute-start.3 = (bf16[448,128]{1,0:T(8,128)(2,1)S(1)}, bf16[448,128]{1,0:T(8,128)(2,1)S(1)}, u32[]{:S(2)}, u32[]{:S(2)}) collective-permute-start(bf16[448,128]{1,0:T(8,128)(2,1)S(1)} %get-tuple-element.19), channel_id=1, source_target_pairs={{0,8},{2,10},{4,12},{6,14},{8,0},{10,2},{12,4},{14,6},{1,9},{3,11}... | collective-permute-start | bytes 344072 | tf_op jit(solution)/shard_map/ppermute | solution.py:367
  8.1 10.8 %collective-permute-start.5 = (bf16[448,128]{1,0:T(8,128)(2,1)S(1)}, bf16[448,128]{1,0:T(8,128)(2,1)S(1)}, u32[]{:S(2)}, u32[]{:S(2)}) collective-permute-start(bf16[448,128]{1,0:T(8,128)(2,1)S(1)} %get-tuple-element.20), channel_id=1, source_target_pairs={{0,12},{2,14},{4,8},{6,10},{8,4},{10,6},{12,0},{14,2},{1,13},{3,15... | collective-permute-start | bytes 344072 | tf_op jit(solution)/shard_map/ppermute | solution.py:367
  9.3 14.2 %collective-permute-start.2 = (bf16[704,128]{1,0:T(8,128)(2,1)S(1)}, bf16[704,128]{1,0:T(8,128)(2,1)S(1)}, u32[]{:S(2)}, u32[]{:S(2)}) collective-permute-start(bf16[704,128]{1,0:T(8,128)(2,1)S(1)} %pad_maximum_fusion.2), channel_id=1, source_target_pairs={{0,2},{2,0},{4,6},{6,4},{8,10},{10,8},{12,14},{14,12},{1,3},{3,1},... | collective-permute-start | bytes 540680 | tf_op jit(solution)/shard_map/ppermute | solution.py:367
  12.9 11.3 %slice-start.1 = ((s8[7077888]{0:T(1024)(128)(4,1)}), s8[2883584]{0:T(1024)(128)(4,1)S(1)}, s32[]{:S(2)}) async-start(s8[7077888]{0:T(1024)(128)(4,1)} %bitcast.2), calls=%async_computation.2 | async-start | bytes 5767168
  14.5 11.3 %copy-start = (bf16[2,768,768]{2,1,0:T(8,128)(2,1)S(1)}, bf16[2,768,768]{2,1,0:T(8,128)(2,1)}, u32[]{:S(2)}) copy-start(bf16[2,768,768]{2,1,0:T(8,128)(2,1)} %wo_ref.1) | copy-start | bytes 7077892
  17.4 6.2 %collective-permute-start.4 = (bf16[352,128]{1,0:T(8,128)(2,1)S(1)}, bf16[352,128]{1,0:T(8,128)(2,1)S(1)}, u32[]{:S(2)}, u32[]{:S(2)}) collective-permute-start(bf16[352,128]{1,0:T(8,128)(2,1)S(1)} %slice.44), channel_id=1, source_target_pairs={{0,2},{2,0},{4,6},{6,4},{8,10},{10,8},{12,14},{14,12},{1,3},{3,1},... | collective-permute-start | bytes 270344 | tf_op jit(solution)/shard_map/ppermute | solution.py:367
  19.0 4.6 %collective-permute-start.6 = (bf16[352,128]{1,0:T(8,128)(2,1)S(1)}, bf16[352,128]{1,0:T(8,128)(2,1)S(1)}, u32[]{:S(2)}, u32[]{:S(2)}) collective-permute-start(bf16[352,128]{1,0:T(8,128)(2,1)S(1)} %slice.45), channel_id=1, source_target_pairs={{0,2},{2,0},{4,6},{6,4},{8,10},{10,8},{12,14},{14,12},{1,3},{3,1},... | collective-permute-start | bytes 270344 | tf_op jit(solution)/shard_map/ppermute | solution.py:367
  19.5 6.2 %collective-permute-start.8 = (bf16[896,128]{1,0:T(8,128)(2,1)S(1)}, bf16[896,128]{1,0:T(8,128)(2,1)S(1)}, u32[]{:S(2)}, u32[]{:S(2)}) collective-permute-start(bf16[896,128]{1,0:T(8,128)(2,1)S(1)} %pad_maximum_fusion.1), channel_id=1, source_target_pairs={{0,1},{1,0},{2,3},{3,2},{4,5},{5,4},{6,7},{7,6},{8,9},{9,8},{10,11... | collective-permute-start | bytes 688136 | tf_op jit(solution)/shard_map/ppermute | solution.py:387
  19.6 6.2 %collective-permute-start.9 = (bf16[448,128]{1,0:T(8,128)(2,1)S(1)}, bf16[448,128]{1,0:T(8,128)(2,1)S(1)}, u32[]{:S(2)}, u32[]{:S(2)}) collective-permute-start(bf16[448,128]{1,0:T(8,128)(2,1)S(1)} %collective-permute-done.5.refs_5_.refs_6_), channel_id=1, source_target_pairs={{0,1},{1,0},{2,3},{3,2},{4,5},{5,4},{6,7},{7,6},{8,9},{9,8},{10,11... | collective-permute-start | bytes 344072 | tf_op jit(solution)/shard_map/ppermute | solution.py:387
  23.5 2.2 %collective-permute-start.10 = (bf16[352,128]{1,0:T(8,128)(2,1)S(1)}, bf16[352,128]{1,0:T(8,128)(2,1)S(1)}, u32[]{:S(2)}, u32[]{:S(2)}) collective-permute-start(bf16[352,128]{1,0:T(8,128)(2,1)S(1)} %collective-permute-done.6.refs_6_.refs_7_), channel_id=1, source_target_pairs={{0,1},{1,0},{2,3},{3,2},{4,5},{5,4},{6,7},{7,6},{8,9},{9,8},{10,11... | collective-permute-start | bytes 270344 | tf_op jit(solution)/shard_map/ppermute | solution.py:387
  23.6 2.2 %collective-permute-start.7 = (bf16[1056,128]{1,0:T(8,128)(2,1)S(1)}, bf16[1056,128]{1,0:T(8,128)(2,1)S(1)}, u32[]{:S(2)}, u32[]{:S(2)}) collective-permute-start(bf16[1056,128]{1,0:T(8,128)(2,1)S(1)} %pad_maximum_fusion), channel_id=1, source_target_pairs={{0,1},{1,0},{2,3},{3,2},{4,5},{5,4},{6,7},{7,6},{8,9},{9,8},{10,11... | collective-permute-start | bytes 811016 | tf_op jit(solution)/shard_map/ppermute | solution.py:387

commit v9 on v8

--- a/solution.py
+++ b/solution.py
@@ -389,8 +389,8 @@
 
     blocks[passing[-1] + 1] = beside(blocks[passing[-1]][ahead:])
     swap_all(list(passing[:-1]))
-    swap_all([passing[-1]])
-    swap_all(list(range(1, particles - 1, 2)))
+    swap_all([passing[-1]] + list(range(1, particles - 3, 2)))
+    swap_all([particles - 3])
     swap_all([particles - 1])
     swapped = [far[distance] for distance in range(1, particles)]
     blocks = [blocks[distance] for distance in range(1, particles)]

time: 41.9 us -> 41.9 us (level)
  starting transfers between devices: 12.6 us -> 12.1 us
  waiting for transfers between devices: 7.48 us -> 7.97 us
    ppermute x6, waiting for transfers between devices: 7.46 us -> 7.96 us  [beside(): return lax.ppermute(block, 'tok', [(t, t ^ k) for t in range(particles)])]
    ppermute x4, starting transfers between devices: 1.14 us -> 0.65 us  [swap_all(): swapped = lax.ppermute(jnp.concatenate(group, axis=0), 'dom', swap)]
  transfers between devices with their start and end apart: 11 -> 11, of which waited for: 3 -> 4; matrix products, arithmetic and copies ran while one was open for 0% -> 0% of each run, Pallas kernels for 11% -> 11%
where the time goes in v9:
time: 41.9 us; the launch traced here: 41.7 us
  starting transfers between devices  12.1 us (29%)
  blocking collectives  12 us (29%)
  Pallas kernels  8.56 us (20%)
  waiting for transfers between devices  7.97 us (19%)
  local copies, waits for them, and re-layouts  0.78 us (2%)
    all_to_all x1, blocking collectives, spread_body(): return lax.all_to_all(result, 'tok', 0, 0, tiled=True)  12 us
    ppermute x6, starting transfers between devices, beside(): return lax.ppermute(block, 'tok', [(t, t ^ k) for t in range(particles)])  11 us
    ppermute x6, waiting for transfers between devices, beside(): return lax.ppermute(block, 'tok', [(t, t ^ k) for t in range(particles)])  7.96 us
    pallas_call x1, Pallas kernels, layers(): pl.pallas_call(kernel, out_shape=jax.ShapeDtypeStruct((sources, rows, wid...  3.21 us
    pallas_call x2, Pallas kernels, make_bias(): pl.pallas_call(kernel, out_shape=jax.ShapeDtypeStruct((blocks * rows, key...  3.21 us
    pallas_call x1, Pallas kernels, first_half(): pl.pallas_call(kernel, out_shape=(wide, wide, wide, tall, tall), in_specs...  1.49 us
  transfers between devices with their start and end apart: 11, of which 4 were waited for; matrix products, arithmetic and copies ran while one was open for 0% of the time, Pallas kernels for 11%

profile of v9, /device:TPU:0, one launch (start us, length us, event | category | flops | bytes accessed | tf_op | source)
XLA Modules:
  0.0 41.7 jit_solution(14666966482547523850)
XLA Ops:
  0.0 0.0 copy-start.1
  0.0 0.0 copy-start.2
  0.0 0.0 copy-start.4
  0.0 0.5 %collective-permute-start = (bf16[8,16,768]{2,1,0:T(8,128)(2,1)}, bf16[8,16,768]{2,1,0:T(8,128)(2,1)S(1)}, u32[]{:S(2)}, u32[]{:S(2)}) collective-permute-start(bf16[8,16,768]{2,1,0:T(8,128)(2,1)} %own_ref.1), channel_id=1, source_target_pairs={{0,1},{1,0},{2,3},{3,2},{4,5},{5,4},{6,7},{7,6},{8,9},{9,8},{10,11... | collective-permute-start | bytes 589832 | tf_op jit(solution)/shard_map/ppermute | solution.py:369
  0.5 0.0 slice-start
  0.5 1.6 %make_bias.2.bias_ref.near_ref.refs_0_ = bf16[256,128]{1,0:T(8,128)(2,1)S(1)} custom-call(bf16[16,128,128]{2,1,0:T(8,128)(2,1)} %pair_hbm.2, s32[1,128]{1,0:T(1,128)} %bitcast.4, bf16[2,16,128]{2,1,0:T(8,128)(2,1)} %bitcast.8, bf16[2,768,2304]{2,1,0:T(8,128)(2,1)} %wq_ref.1), custom_call_target="tpu_custom_call" | custom-call | flops 8388608 | bytes 8000000 | tf_op jit(solution)/shard_map/make_bias/pallas_call | solution.py:115
  2.1 0.0 copy-start.3
  2.2 0.0 collective-permute-done.other_ref
  2.2 0.0 copy-done.1
  2.2 0.0 copy-done.2
  2.2 0.0 copy-done.4
  2.2 0.6 %pack.1 = (bf16[96,128]{1,0:T(8,128)(2,1)S(1)}, bf16[352,128]{1,0:T(8,128)(2,1)S(1)}, bf16[448,128]{1,0:T(8,128)(2,1)S(1)}, bf16[448,128]{1,0:T(8,128)(2,1)S(1)}, bf16[448,128]{1,0:T(8,128)(2,1)S(1)}) custom-call(s32[8]{0:T(128)S(1)} %copy-done.4, bf16[8,16,768]{2,1,0:T(8,128)(2,1)S(1)} %copy-done.1, bf16[8,16,768]{2,1,0:T(8,128)(2,1)S(1)} %collective-permute-done.other_ref, ...), custom_call_target="tpu_custom_call" | custom-call | tf_op jit(solution)/shard_map/pack/pallas_call | solution.py:168
  2.8 2.7 %collective-permute-start.1 = (bf16[448,128]{1,0:T(8,128)(2,1)S(1)}, bf16[448,128]{1,0:T(8,128)(2,1)S(1)}, u32[]{:S(2)}, u32[]{:S(2)}) collective-permute-start(bf16[448,128]{1,0:T(8,128)(2,1)S(1)} %get-tuple-element.18), channel_id=1, source_target_pairs={{0,4},{2,6},{4,0},{6,2},{8,12},{10,14},{12,8},{14,10},{1,5},{3,7},... | collective-permute-start | bytes 344072 | tf_op jit(solution)/shard_map/ppermute | solution.py:367
  5.5 2.6 %collective-permute-start.3 = (bf16[448,128]{1,0:T(8,128)(2,1)S(1)}, bf16[448,128]{1,0:T(8,128)(2,1)S(1)}, u32[]{:S(2)}, u32[]{:S(2)}) collective-permute-start(bf16[448,128]{1,0:T(8,128)(2,1)S(1)} %get-tuple-element.19), channel_id=1, source_target_pairs={{0,8},{2,10},{4,12},{6,14},{8,0},{10,2},{12,4},{14,6},{1,9},{3,11}... | collective-permute-start | bytes 344072 | tf_op jit(solution)/shard_map/ppermute | solution.py:367
  8.1 0.0 collective-permute-start.5
  8.1 1.2 %collective-permute-done.1.refs_1_.refs_2_ = bf16[448,128]{1,0:T(8,128)(2,1)S(1)} collective-permute-done((bf16[448,128]{1,0:T(8,128)(2,1)S(1)}, bf16[448,128]{1,0:T(8,128)(2,1)S(1)}, u32[]{:S(2)}, u32[]{:S(2)}) %collective-permute-start.1) | collective-permute-done | bytes 114720 | tf_op jit(solution)/shard_map/ppermute | solution.py:367
  9.3 3.6 %collective-permute-start.2 = (bf16[704,128]{1,0:T(8,128)(2,1)S(1)}, bf16[704,128]{1,0:T(8,128)(2,1)S(1)}, u32[]{:S(2)}, u32[]{:S(2)}) collective-permute-start(bf16[704,128]{1,0:T(8,128)(2,1)S(1)} %pad_maximum_fusion.2), channel_id=1, source_target_pairs={{0,2},{2,0},{4,6},{6,4},{8,10},{10,8},{12,14},{14,12},{1,3},{3,1},... | collective-permute-start | bytes 540680 | tf_op jit(solution)/shard_map/ppermute | solution.py:367
  12.9 0.0 slice-start.1
  12.9 1.6 %make_bias.3.refs_8_ = bf16[256,128]{1,0:T(8,128)(2,1)S(1)} custom-call(bf16[16,128,128]{2,1,0:T(8,128)(2,1)} %pair_hbm.2, s32[1,128]{1,0:T(1,128)} %bitcast.5, bf16[2,16,128]{2,1,0:T(8,128)(2,1)} %bitcast.9, bf16[2,768,2304]{2,1,0:T(8,128)(2,1)} %wq_ref.1), custom_call_target="tpu_custom_call" | custom-call | flops 8388608 | bytes 8000000 | tf_op jit(solution)/shard_map/make_bias/pallas_call | solution.py:115
  14.5 0.0 copy-start
  14.5 2.8 %collective-permute-done.3.refs_3_.refs_4_ = bf16[448,128]{1,0:T(8,128)(2,1)S(1)} collective-permute-done((bf16[448,128]{1,0:T(8,128)(2,1)S(1)}, bf16[448,128]{1,0:T(8,128)(2,1)S(1)}, u32[]{:S(2)}, u32[]{:S(2)}) %collective-permute-start.3) | collective-permute-done | bytes 114720 | tf_op jit(solution)/shard_map/ppermute | solution.py:367
  17.4 1.6 %collective-permute-start.4 = (bf16[352,128]{1,0:T(8,128)(2,1)S(1)}, bf16[352,128]{1,0:T(8,128)(2,1)S(1)}, u32[]{:S(2)}, u32[]{:S(2)}) collective-permute-start(bf16[352,128]{1,0:T(8,128)(2,1)S(1)} %slice.44), channel_id=1, source_target_pairs={{0,2},{2,0},{4,6},{6,4},{8,10},{10,8},{12,14},{14,12},{1,3},{3,1},... | collective-permute-start | bytes 270344 | tf_op jit(solution)/shard_map/ppermute | solution.py:367
  18.9 0.0 collective-permute-done.5.refs_5_.refs_6_
  19.0 0.6 %collective-permute-start.6 = (bf16[352,128]{1,0:T(8,128)(2,1)S(1)}, bf16[352,128]{1,0:T(8,128)(2,1)S(1)}, u32[]{:S(2)}, u32[]{:S(2)}) collective-permute-start(bf16[352,128]{1,0:T(8,128)(2,1)S(1)} %slice.45), channel_id=1, source_target_pairs={{0,2},{2,0},{4,6},{6,4},{8,10},{10,8},{12,14},{14,12},{1,3},{3,1},... | collective-permute-start | bytes 270344 | tf_op jit(solution)/shard_map/ppermute | solution.py:367
  19.5 0.1 collective-permute-start.8
  19.6 2.3 %collective-permute-done.4.refs_4_.refs_5_ = bf16[352,128]{1,0:T(8,128)(2,1)S(1)} collective-permute-done((bf16[352,128]{1,0:T(8,128)(2,1)S(1)}, bf16[352,128]{1,0:T(8,128)(2,1)S(1)}, u32[]{:S(2)}, u32[]{:S(2)}) %collective-permute-start.4) | collective-permute-done | bytes 90144 | tf_op jit(solution)/shard_map/ppermute | solution.py:367
  21.9 0.0 collective-permute-start.9
  21.9 1.6 %collective-permute-done.6.refs_6_.refs_7_ = bf16[352,128]{1,0:T(8,128)(2,1)S(1)} collective-permute-done((bf16[352,128]{1,0:T(8,128)(2,1)S(1)}, bf16[352,128]{1,0:T(8,128)(2,1)S(1)}, u32[]{:S(2)}, u32[]{:S(2)}) %collective-permute-start.6) | collective-permute-done | bytes 90144 | tf_op jit(solution)/shard_map/ppermute | solution.py:367
  23.5 0.0 collective-permute-start.10
  23.5 0.0 collective-permute-done.2
  23.6 0.6 %collective-permute-start.7 = (bf16[1152,128]{1,0:T(8,128)(2,1)S(1)}, bf16[1152,128]{1,0:T(8,128)(2,1)S(1)}, u32[]{:S(2)}, u32[]{:S(2)}) collective-permute-start(bf16[1152,128]{1,0:T(8,128)(2,1)S(1)} %pad_maximum_fusion), channel_id=1, source_target_pairs={{0,1},{1,0},{2,3},{3,2},{4,5},{5,4},{6,7},{7,6},{8,9},{9,8},{10,11... | collective-permute-start | bytes 884744 | tf_op jit(solution)/shard_map/ppermute | solution.py:387
  24.2 0.0 slice-done
  24.2 0.0 copy-done.3
  24.2 0.0 slice-done.1
  24.2 1.5 %first_half.1 = (bf16[128,768]{1,0:T(8,128)(2,1)S(1)}, bf16[128,768]{1,0:T(8,128)(2,1)S(1)}, bf16[128,768]{1,0:T(8,128)(2,1)S(1)}, bf16[768,128]{1,0:T(8,128)(2,1)S(1)}, bf16[768,128]{1,0:T(8,128)(2,1)S(1)}) custom-call(s32[1,128]{1,0:T(1,128)S(1)} %bitcast.6, bf16[2,768,2304]{2,1,0:T(8,128)(2,1)S(1)} %bitcast.3, ...), custom_call_target="tpu_custom_call" | custom-call | flops 452984832 | bytes 4718592 | tf_op jit(solution)/shard_map/first_half/pallas_call | solution.py:282
  25.7 0.0 collective-permute-done.8
  25.7 0.0 collective-permute-done.7
  25.8 0.0 collective-permute-done.9.refs_13_
  25.8 0.0 collective-permute-done.10.refs_15_
  25.8 0.0 copy-done
  25.8 3.2 %layers.1 = bf16[8,16,768]{2,1,0:T(8,128)(2,1)S(1)} custom-call(s32[1,128]{1,0:T(1,128)S(1)} %bitcast.7, bf16[2,768,2304]{2,1,0:T(8,128)(2,1)S(1)} %bitcast.3, bf16[2,768,768]{2,1,0:T(8,128)(2,1)S(1)} %copy-done, bf16[128,768]{1,0:T(8,128)(2,1)S(1)} %get-tuple-element.21.x_ref, bf16[128,768]{1,0:T(8,128)(2,1)S(1)} %get-tuple-element.22.q_in, ...), custom_call_target="tpu_custom_call" | custom-call | flops 1056964608 | bytes 5898240 | tf_op jit(solution)/shard_map/layers/pallas_call | solution.py:336
  29.0 12.0 %all_to_all.5 = bf16[8,16,768]{2,1,0:T(8,128)(2,1)S(1)} all-to-all(bf16[8,16,768]{2,1,0:T(8,128)(2,1)S(1)} %layers.1), channel_id=1, replica_groups=mesh['groups'=2,'tok'=8,'dom'=2] {'tok'}, dimensions={0} | all-to-all | bytes 393216 | tf_op jit(solution)/shard_map/all_to_all | solution.py:401
  41.1 0.7 %copy.10 = bf16[8,16,768]{2,1,0:T(8,128)(2,1)} copy(bf16[8,16,768]{2,1,0:T(8,128)(2,1)S(1)} %all_to_all.5) | data formatting | bytes 393216
  (11 shorter events, 0.1 us)
Async XLA Ops:
  0.0 2.2 %copy-start.1 = (bf16[8,16,768]{2,1,0:T(8,128)(2,1)S(1)}, bf16[8,16,768]{2,1,0:T(8,128)(2,1)}, u32[]{:S(2)}) copy-start(bf16[8,16,768]{2,1,0:T(8,128)(2,1)} %own_ref.1) | copy-start | bytes 589828
  0.0 2.2 %copy-start.2 = (bf16[8,16,768]{2,1,0:T(8,128)(2,1)S(1)}, bf16[8,16,768]{2,1,0:T(8,128)(2,1)}, u32[]{:S(2)}) copy-start(bf16[8,16,768]{2,1,0:T(8,128)(2,1)} %noise_ref.1) | copy-start | bytes 589828
  0.0 2.2 %copy-start.4 = (s32[8]{0:T(128)S(1)}, s32[8]{0:T(128)}, u32[]{:S(2)}) copy-start(s32[8]{0:T(128)} %anc_ref.1) | copy-start | bytes 100
  0.0 2.1 %collective-permute-start = (bf16[8,16,768]{2,1,0:T(8,128)(2,1)}, bf16[8,16,768]{2,1,0:T(8,128)(2,1)S(1)}, u32[]{:S(2)}, u32[]{:S(2)}) collective-permute-start(bf16[8,16,768]{2,1,0:T(8,128)(2,1)} %own_ref.1), channel_id=1, source_target_pairs={{0,1},{1,0},{2,3},{3,2},{4,5},{5,4},{6,7},{7,6},{8,9},{9,8},{10,11... | collective-permute-start | bytes 589832 | tf_op jit(solution)/shard_map/ppermute | solution.py:369
  0.5 23.6 %slice-start = ((s8[7077888]{0:T(1024)(128)(4,1)}), s8[4194304]{0:T(1024)(128)(4,1)S(1)}, s32[]{:S(2)}) async-start(s8[7077888]{0:T(1024)(128)(4,1)} %bitcast.2), calls=%async_computation.1 | async-start | bytes 8388608
  2.1 22.0 %copy-start.3 = (s32[128]{0:T(128)S(1)}, s32[128]{0:T(128)}, u32[]{:S(2)}) copy-start(s32[128]{0:T(128)} %param.12) | copy-start | bytes 1540
  2.8 6.5 %collective-permute-start.1 = (bf16[448,128]{1,0:T(8,128)(2,1)S(1)}, bf16[448,128]{1,0:T(8,128)(2,1)S(1)}, u32[]{:S(2)}, u32[]{:S(2)}) collective-permute-start(bf16[448,128]{1,0:T(8,128)(2,1)S(1)} %get-tuple-element.18), channel_id=1, source_target_pairs={{0,4},{2,6},{4,0},{6,2},{8,12},{10,14},{12,8},{14,10},{1,5},{3,7},... | collective-permute-start | bytes 344072 | tf_op jit(solution)/shard_map/ppermute | solution.py:367
  5.5 11.8 %collective-permute-start.3 = (bf16[448,128]{1,0:T(8,128)(2,1)S(1)}, bf16[448,128]{1,0:T(8,128)(2,1)S(1)}, u32[]{:S(2)}, u32[]{:S(2)}) collective-permute-start(bf16[448,128]{1,0:T(8,128)(2,1)S(1)} %get-tuple-element.19), channel_id=1, source_target_pairs={{0,8},{2,10},{4,12},{6,14},{8,0},{10,2},{12,4},{14,6},{1,9},{3,11}... | collective-permute-start | bytes 344072 | tf_op jit(solution)/shard_map/ppermute | solution.py:367
  8.1 10.8 %collective-permute-start.5 = (bf16[448,128]{1,0:T(8,128)(2,1)S(1)}, bf16[448,128]{1,0:T(8,128)(2,1)S(1)}, u32[]{:S(2)}, u32[]{:S(2)}) collective-permute-start(bf16[448,128]{1,0:T(8,128)(2,1)S(1)} %get-tuple-element.20), channel_id=1, source_target_pairs={{0,12},{2,14},{4,8},{6,10},{8,4},{10,6},{12,0},{14,2},{1,13},{3,15... | collective-permute-start | bytes 344072 | tf_op jit(solution)/shard_map/ppermute | solution.py:367
  9.3 14.2 %collective-permute-start.2 = (bf16[704,128]{1,0:T(8,128)(2,1)S(1)}, bf16[704,128]{1,0:T(8,128)(2,1)S(1)}, u32[]{:S(2)}, u32[]{:S(2)}) collective-permute-start(bf16[704,128]{1,0:T(8,128)(2,1)S(1)} %pad_maximum_fusion.2), channel_id=1, source_target_pairs={{0,2},{2,0},{4,6},{6,4},{8,10},{10,8},{12,14},{14,12},{1,3},{3,1},... | collective-permute-start | bytes 540680 | tf_op jit(solution)/shard_map/ppermute | solution.py:367
  12.9 11.3 %slice-start.1 = ((s8[7077888]{0:T(1024)(128)(4,1)}), s8[2883584]{0:T(1024)(128)(4,1)S(1)}, s32[]{:S(2)}) async-start(s8[7077888]{0:T(1024)(128)(4,1)} %bitcast.2), calls=%async_computation.2 | async-start | bytes 5767168
  14.5 11.3 %copy-start = (bf16[2,768,768]{2,1,0:T(8,128)(2,1)S(1)}, bf16[2,768,768]{2,1,0:T(8,128)(2,1)}, u32[]{:S(2)}) copy-start(bf16[2,768,768]{2,1,0:T(8,128)(2,1)} %wo_ref.1) | copy-start | bytes 7077892
  17.4 4.6 %collective-permute-start.4 = (bf16[352,128]{1,0:T(8,128)(2,1)S(1)}, bf16[352,128]{1,0:T(8,128)(2,1)S(1)}, u32[]{:S(2)}, u32[]{:S(2)}) collective-permute-start(bf16[352,128]{1,0:T(8,128)(2,1)S(1)} %slice.44), channel_id=1, source_target_pairs={{0,2},{2,0},{4,6},{6,4},{8,10},{10,8},{12,14},{14,12},{1,3},{3,1},... | collective-permute-start | bytes 270344 | tf_op jit(solution)/shard_map/ppermute | solution.py:367
  19.0 4.6 %collective-permute-start.6 = (bf16[352,128]{1,0:T(8,128)(2,1)S(1)}, bf16[352,128]{1,0:T(8,128)(2,1)S(1)}, u32[]{:S(2)}, u32[]{:S(2)}) collective-permute-start(bf16[352,128]{1,0:T(8,128)(2,1)S(1)} %slice.45), channel_id=1, source_target_pairs={{0,2},{2,0},{4,6},{6,4},{8,10},{10,8},{12,14},{14,12},{1,3},{3,1},... | collective-permute-start | bytes 270344 | tf_op jit(solution)/shard_map/ppermute | solution.py:367
  19.5 6.2 %collective-permute-start.8 = (bf16[896,128]{1,0:T(8,128)(2,1)S(1)}, bf16[896,128]{1,0:T(8,128)(2,1)S(1)}, u32[]{:S(2)}, u32[]{:S(2)}) collective-permute-start(bf16[896,128]{1,0:T(8,128)(2,1)S(1)} %pad_maximum_fusion.1), channel_id=1, source_target_pairs={{0,1},{1,0},{2,3},{3,2},{4,5},{5,4},{6,7},{7,6},{8,9},{9,8},{10,11... | collective-permute-start | bytes 688136 | tf_op jit(solution)/shard_map/ppermute | solution.py:387
  21.9 3.8 %collective-permute-start.9 = (bf16[352,128]{1,0:T(8,128)(2,1)S(1)}, bf16[352,128]{1,0:T(8,128)(2,1)S(1)}, u32[]{:S(2)}, u32[]{:S(2)}) collective-permute-start(bf16[352,128]{1,0:T(8,128)(2,1)S(1)} %collective-permute-done.4.refs_4_.refs_5_), channel_id=1, source_target_pairs={{0,1},{1,0},{2,3},{3,2},{4,5},{5,4},{6,7},{7,6},{8,9},{9,8},{10,11... | collective-permute-start | bytes 270344 | tf_op jit(solution)/shard_map/ppermute | solution.py:387
  23.5 2.3 %collective-permute-start.10 = (bf16[352,128]{1,0:T(8,128)(2,1)S(1)}, bf16[352,128]{1,0:T(8,128)(2,1)S(1)}, u32[]{:S(2)}, u32[]{:S(2)}) collective-permute-start(bf16[352,128]{1,0:T(8,128)(2,1)S(1)} %collective-permute-done.6.refs_6_.refs_7_), channel_id=1, source_target_pairs={{0,1},{1,0},{2,3},{3,2},{4,5},{5,4},{6,7},{7,6},{8,9},{9,8},{10,11... | collective-permute-start | bytes 270344 | tf_op jit(solution)/shard_map/ppermute | solution.py:387
  23.6 2.2 %collective-permute-start.7 = (bf16[1152,128]{1,0:T(8,128)(2,1)S(1)}, bf16[1152,128]{1,0:T(8,128)(2,1)S(1)}, u32[]{:S(2)}, u32[]{:S(2)}) collective-permute-start(bf16[1152,128]{1,0:T(8,128)(2,1)S(1)} %pad_maximum_fusion), channel_id=1, source_target_pairs={{0,1},{1,0},{2,3},{3,2},{4,5},{5,4},{6,7},{7,6},{8,9},{9,8},{10,11... | collective-permute-start | bytes 884744 | tf_op jit(solution)/shard_map/ppermute | solution.py:387
